TPU v7x, 32 devices: a whole 2x2x4 slice. The times are simulated.
32 devices in a mesh: dp: 2 (over x), seq: 16 (over z, y, core).
Axes of the slice: x: 2, y: 2, z: 4, core: 2. Of those that a mesh axis runs over, the one named last changes fastest.
Arguments:
- frames: bfloat16 [4, 1024, 1024], P('dp', 'seq'), may hold values from -6 to 6
- out_grad: bfloat16 [4, 1024, 1024], P('dp', 'seq'), may hold values from -6 to 6
- order: int32 [4], P('dp'), may hold values from 0 to 3, each once
- lengths: int32 [4], replicated, may hold values from 1 to 1024, 2560 in all
- first_gain: bfloat16 [1024], P(('dp', 'seq')), may hold values from 0.25 to 1.75
- first_shift: bfloat16 [1024], P(('dp', 'seq')), may hold values from -3 to 3
- query_weight: bfloat16 [1024, 1024], P(('dp', 'seq')), may hold values from -0.1875 to 0.1875
- query_bias: bfloat16 [1024], P(('dp', 'seq')), may hold values from -3 to 3
- key_weight: bfloat16 [1024, 1024], P(('dp', 'seq')), may hold values from -0.1875 to 0.1875
- value_weight: bfloat16 [1024, 1024], P(('dp', 'seq')), may hold values from -0.1875 to 0.1875
- value_bias: bfloat16 [1024], P(('dp', 'seq')), may hold values from -3 to 3
- output_weight: bfloat16 [1024, 1024], P(('dp', 'seq')), may hold values from -3 to 3
- output_bias: bfloat16 [1024], P(('dp', 'seq')), may hold values from -3 to 3
- second_gain: bfloat16 [1024], P(('dp', 'seq')), may hold values from 0.25 to 1.75
- second_shift: bfloat16 [1024], P(('dp', 'seq')), may hold values from -3 to 3
- up_weight: bfloat16 [1024, 4096], P(('dp', 'seq')), may hold values from -0.1875 to 0.1875
- up_bias: bfloat16 [4096], P(('dp', 'seq')), may hold values from -3 to 3
- down_weight: bfloat16 [4096, 1024], P(('dp', 'seq')), may hold values from -0.09375 to 0.09375
- down_bias: bfloat16 [1024], P(('dp', 'seq')), may hold values from -3 to 3
Outputs:
- output: bfloat16 [4, 1024, 1024], P('dp', 'seq')
- frames_grad: bfloat16 [4, 1024, 1024], P('dp', 'seq')
- first_gain_grad: float32 [1024], P(('dp', 'seq'))
- first_shift_grad: float32 [1024], P(('dp', 'seq'))
- query_weight_grad: float32 [1024, 1024], P(('dp', 'seq'))
- query_bias_grad: float32 [1024], P(('dp', 'seq'))
- key_weight_grad: float32 [1024, 1024], P(('dp', 'seq'))
- value_weight_grad: float32 [1024, 1024], P(('dp', 'seq'))
- value_bias_grad: float32 [1024], P(('dp', 'seq'))
- output_weight_grad: float32 [1024, 1024], P(('dp', 'seq'))
- output_bias_grad: float32 [1024], P(('dp', 'seq'))
- second_gain_grad: float32 [1024], P(('dp', 'seq'))
- second_shift_grad: float32 [1024], P(('dp', 'seq'))
- up_weight_grad: float32 [1024, 4096], P(('dp', 'seq'))
- up_bias_grad: float32 [4096], P(('dp', 'seq'))
- down_weight_grad: float32 [4096, 1024], P(('dp', 'seq'))
- down_bias_grad: float32 [1024], P(('dp', 'seq'))
Inputs may be any that keep to these rules, and one draw needn't show every extreme that they name: order[s] is the utterance held in slot s; each utterance is held by exactly one slot. lengths[u] counts the true frames of utterance u; frames from lengths[u] on are padding and are masked as keys; the longest utterance fills all 1024 frames.
All inputs are finite; a program needn't handle non-finite values.
Results may differ from a plain program's by a relative error of at most 0.012.
Values may be sent and summed in bfloat16 or wider, within the bound.
No kernel may reach another device: no remote copies, remote signals or barrier semaphores. Data moves between devices by JAX's collectives and lax.ppermute only.
A program may use at most 256 MiB of HBM per device.

v0:
```python
import functools

import jax
import jax.numpy as jnp
from jax import lax
from jax.experimental import pallas as pl
from jax.experimental.pallas import tpu as pltpu
from jax.sharding import PartitionSpec as P

HEAD = 64
f32 = jnp.float32
bf16 = jnp.bfloat16
norm_eps = 1e-05
inv_root_two = 0.7071067811865476
inv_root_tau = 0.3989422804014327
NN = (((1,), (0,)), ((), ()))
NT = (((1,), (1,)), ((), ()))
TN = (((0,), (0,)), ((), ()))
MIB = 1024 * 1024


def dot(a, b, dims=NN):
    return lax.dot_general(a, b, dims, preferred_element_type=f32)


def normalize(rows):
    average = jnp.mean(rows, axis=-1, keepdims=True)
    centered = rows - average
    inv_std = lax.rsqrt(jnp.mean(centered * centered, axis=-1, keepdims=True) + norm_eps)
    return centered * inv_std, inv_std


def norm_back(grad_rows, scaled, inv_std, gain):
    grad_hat = grad_rows * gain
    return inv_std * (
        grad_hat
        - jnp.mean(grad_hat, axis=-1, keepdims=True)
        - scaled * jnp.mean(grad_hat * scaled, axis=-1, keepdims=True)
    )


def sds(shape, dtype):
    return jax.ShapeDtypeStruct(shape, dtype)


def vmem(like):
    return pltpu.VMEM(like.shape, like.dtype)


class Near:
    def __init__(self, array):
        self.array = array
        self.shape, self.dtype = array.shape, array.dtype


def near(arrays):
    return [Near(a) for a in arrays]


class Place:
    def __init__(self, slots, n):
        seq_at = lax.axis_index("seq")
        self.h, self.j = seq_at // n, seq_at % n
        self.dp = lax.axis_index("dp")
        self.group = self.dp * slots + self.h
        self.length = None


def call(grid, kernel, args, outs, name, flops=0, scratch=(), sems=1, limit=None, lengths=()):
    here = pl.BlockSpec(memory_space=pltpu.HBM)
    anywhere = pl.BlockSpec(memory_space=pl.ANY)
    scalars = pl.BlockSpec(memory_space=pltpu.SMEM)
    nbytes = sum(a.shape[0] * a.shape[1] * a.dtype.itemsize for a in list(args) + list(outs))

    def body(*refs):
        place = Place(*grid[:2])
        if lengths:
            order_ref, lengths_ref = refs[:2]
            place.length = lengths_ref[order_ref[place.h]]
        kernel(place, *refs[len(lengths) :])

    return pl.pallas_call(
        body,
        out_shape=tuple(o.array if isinstance(o, Near) else pltpu.HBM(o.shape, o.dtype) for o in outs),
        in_specs=[scalars] * len(lengths) + [anywhere if isinstance(a, Near) else here for a in args],
        out_specs=tuple(anywhere if isinstance(o, Near) else here for o in outs),
        scratch_shapes=list(scratch) + [pltpu.SemaphoreType.DMA((sems,))],
        compiler_params=pltpu.CompilerParams(vmem_limit_bytes=(limit or 8 * grid[2]) * MIB),
        cost_estimate=pl.CostEstimate(flops=int(flops), bytes_accessed=int(nbytes), transcendentals=0),
        name=name,
    )(
        *lengths,
        *[a.array if isinstance(a, Near) else pltpu.with_memory_space_constraint(a, pltpu.HBM) for a in args],
    )


class Mover:
    def __init__(self, sems):
        self.sems, self.used, self.open = sems, 0, []

    def start(self, source, target):
        copy = pltpu.make_async_copy(source, target, self.sems.at[self.used])
        self.used += 1
        copy.start()
        return copy

    def put(self, source, target):
        self.open.append(self.start(source, target))

    def drain(self):
        for copy in self.open:
            copy.wait()
        self.open = []


def cost(microseconds):
    return microseconds * 1150 * 10**6


def after(value, *others):
    return lax.optimization_barrier((value,) + others)[0]


def rows_at(index, rows):
    return pl.ds(pl.multiple_of(index * rows, rows), rows)


def send_rows(move, place, n, rows, source, send_s, keep, send):
    for r in range(1, n, 2):
        here = slice((r // 2) * rows, (r // 2 + 1) * rows)
        send_s[here, :] = source[rows_at(place.j ^ r, rows), :].astype(bf16)
        move.put(send_s.at[here, :], send.at[here, :])
    for r in range(0, n, 2):
        here = slice((r // 2) * rows, (r // 2 + 1) * rows)
        move.put(source.at[rows_at(place.j ^ r, rows), :], keep.at[here, :])


def rows_kernel(place, frames, out_grad, x_own, x_send, dy_own, dy_send, sems):
    move = Mover(sems)
    for rows, own, sent in ((frames, x_own, x_send), (out_grad, dy_own, dy_send)):
        move.put(rows.at[1 - place.h], sent)
        move.put(rows.at[place.h], own)
    move.drain()


def pack_kernel(n, slots, groups, first_row, place, *refs):
    wq, wk, wv = refs[:3]
    small = refs[3:12]
    packed, q_s, k_s, v_s, *rest = refs[12:]
    small_s, (packed_s, sems) = rest[:9], rest[9:]
    move = Mover(sems)
    loads = [move.start(a, b) for a, b in ((wq, q_s), (wk, k_s), (wv, v_s))]
    loads += [move.start(a, b) for a, b in zip(small, small_s)]
    for copy in loads:
        copy.wait()
    rs = wq.shape[0]
    hd = wq.shape[1] // n
    chunk = small[8].shape[1]
    zeros = jnp.zeros((packed_s.shape[1] - rs, packed_s.shape[2]), bf16)
    for m in range(n):
        cols = slice(m * hd, (m + 1) * hd)
        packed_s[m, rs:, :] = zeros
        packed_s[m, :rs, :hd] = q_s[:, cols]
        packed_s[m, :rs, hd : 2 * hd] = k_s[:, cols]
        packed_s[m, :rs, 2 * hd : 3 * hd] = v_s[:, cols]
        for i in range(8):
            packed_s[m, first_row + i : first_row + i + 1, :rs] = small_s[i][...]
        packed_s[m, first_row : first_row + 1, hd : hd + chunk] = small_s[8][...]
    for i in range(slots):
        move.put(packed_s, packed.at[i * n : (i + 1) * n])
    move.drain()


def pack_up_kernel(n, groups, place, up, packed, up_s, packed_s, sems):
    move = Mover(sems)
    move.start(up, up_s).wait()
    chunk = up.shape[1] // (n * groups)
    for m in range(n):
        for g in range(groups):
            at = (g * n + m) * chunk
            packed_s[m, :, g * chunk : (g + 1) * chunk] = up_s[:, at : at + chunk]
    move.put(packed_s, packed)
    move.drain()


def join_kernel(n, place, up, down, ffn, sems):
    move = Mover(sems)
    width, mine = down.shape[1], ffn.shape[1]
    chunk = down.shape[0]
    feats = ffn.shape[0] - width // mine * chunk
    move.put(up, ffn.at[:feats, :])
    for c in range(width // mine):
        move.put(down.at[:, c * mine : (c + 1) * mine], ffn.at[feats + c * chunk : feats + (c + 1) * chunk, :])
    move.drain()


def key_mask(place, rows, n, half, width):
    row = lax.broadcasted_iota(jnp.int32, (rows, width), 0)
    member = row // (2 * half)
    inside = row % (2 * half)
    own = (inside < half).astype(jnp.int32)
    h = place.h
    block_half = own * h + (1 - own) * (1 - h)
    frame = (block_half * n + member) * half + inside % half
    return frame < place.length


def first_kernel(n, dp_size, groups, half, qb, first_row, place, *refs):
    xs, gots, wos = refs[:n], refs[n : n + dp_size], refs[n + dp_size : n + dp_size + groups // dp_size]
    at = n + dp_size + groups // dp_size
    outs = refs[at : at + 11]
    hat_out, h_out, qkv_out, o_out, lse_out, w_out, vec_out, bias_up_out, wo_out, keep, send = outs
    x_s, hat_s, h_s, qkv_s, o_s, lse_s, got_s, w_s, vec_s, bias_up_s, wo3, wo_s, y_s, send_s, bias, sems = refs[at + 11 :]
    move = Mover(sems)
    j = place.j
    rows = 2 * half
    total = n * rows
    ndev = got_s.shape[0]
    hd = got_s.shape[2] // 3
    seq_size = ndev // dp_size
    rs = x_s.shape[1] // ndev
    chunk = bias_up_s.shape[1] // groups
    load = [move.start(gots[i], got_s.at[pl.ds((place.dp ^ i) * seq_size, seq_size)]) for i in range(dp_size)]
    copies = [move.start(xs[r], x_s.at[rows_at(j ^ r, rows), :]) for r in range(n)]
    slots = groups // dp_size
    outw = [
        move.start(wos[i].at[k], wo3.at[(place.dp ^ k) * slots + (place.h ^ i)])
        for k in range(dp_size)
        for i in range(slots)
    ]
    bias[...] = jnp.where(key_mask(place, total, n, half, 128), 0.0, -1.0).astype(f32)
    for copy in load:
        copy.wait()
    for d in range(ndev):
        w_s[d * rs : (d + 1) * rs, :] = got_s[d, :rs, :]
        vec_s[:, d * rs : (d + 1) * rs] = got_s[d, first_row : first_row + 8, :rs].astype(f32)
    bq, bv = [], []
    for t in range(groups):
        bias_up_s[:, t * chunk : (t + 1) * chunk] = got_s[
            t * n + j, first_row : first_row + 1, hd : hd + chunk
        ].astype(f32)
        bq.append(got_s[j * groups + t, first_row + 2 : first_row + 3, :rs].astype(f32))
        bv.append(got_s[j * groups + t, first_row + 3 : first_row + 4, :rs].astype(f32))
    bq = jnp.concatenate(bq, axis=1)
    bv = jnp.concatenate(bv, axis=1)
    move.put(w_s, w_out)
    move.put(vec_s, vec_out)
    move.put(bias_up_s, bias_up_out)
    for r in range(n):
        copies[r].wait()
        base = pl.multiple_of((j ^ r) * rows, rows)
        for part in range(2):
            at = pl.ds(base + part * half, half)
            scaled, _ = normalize(x_s[at, :].astype(f32))
            hat_s[at, :] = scaled.astype(bf16)
            h_s[at, :] = (scaled * vec_s[0:1, :] + vec_s[1:2, :]).astype(bf16)
    block = min(512, total)
    for i in range(total // block):
        at = slice(i * block, (i + 1) * block)
        qkv = dot(h_s[at, :], w_s[...])
        qkv_s[at, :hd] = ((qkv[:, :hd] + bq) * 0.125).astype(bf16)
        qkv_s[at, hd : 2 * hd] = qkv[:, hd : 2 * hd].astype(bf16)
        qkv_s[at, 2 * hd :] = (qkv[:, 2 * hd :] + bv).astype(bf16)
    move.put(hat_s, hat_out)
    move.put(h_s, h_out)
    move.put(qkv_s, qkv_out)
    heads = hd // HEAD
    for head in range(heads):
        cols = slice(head * HEAD, (head + 1) * HEAD)
        kh = qkv_s[:, hd + head * HEAD : hd + (head + 1) * HEAD]
        vt = qkv_s[:, 2 * hd + head * HEAD : 2 * hd + (head + 1) * HEAD].astype(f32).T.astype(bf16)

        def step(i, _, cols=cols, kh=kh, vt=vt, head=head):
            at = rows_at(i, qb)
            scores = dot(kh, qkv_s[at, cols], NT)
            scores = jnp.where(bias[:, 0:1] >= 0.0, scores, -1e30)
            row_max = jnp.max(scores, axis=0, keepdims=True)
            e = jnp.exp(scores - row_max)
            row_sum = jnp.sum(e, axis=0, keepdims=True)
            ot = dot(vt, e.astype(bf16)) / row_sum
            o_s[at, cols] = ot.T.astype(bf16)
            lse_s[head : head + 1, at] = row_max + jnp.log(row_sum)
            return 0

        lax.fori_loop(0, total // qb, step, 0)
    move.put(o_s, o_out)
    move.put(lse_s, lse_out)
    for copy in outw:
        copy.wait()
    for t in range(groups):
        wo_s[t * rs : (t + 1) * rs, :] = wo3[t]
    move.put(wo_s, wo_out)
    for i in range(total // block):
        at = slice(i * block, (i + 1) * block)
        y_s[at, :] = dot(o_s[at, :], wo_s[...])
    send_rows(move, place, n, rows, y_s, send_s, keep, send)
    move.drain()


def mid_kernel(count, place, *refs):
    ins, x, vec = refs[:count], refs[count], refs[count + 1]
    y_out, h_out = refs[count + 2 : count + 4]
    held = refs[count + 4 : 2 * count + 4]
    x_s, vec_s, y_s, h_s, sems = refs[2 * count + 4 :]
    move = Mover(sems)
    loads = [move.start(a, b) for a, b in zip(ins, held)]
    loads += [move.start(x, x_s), move.start(vec, vec_s)]
    for copy in loads:
        copy.wait()
    y = held[0][...]
    for i in range(1, count):
        y = y + held[i][...].astype(f32)
    y = x_s[...].astype(f32) + y + vec_s[4:5, :]
    y_s[...] = y
    scaled, _ = normalize(y)
    h_s[...] = (scaled * vec_s[5:6, :] + vec_s[6:7, :]).astype(bf16)
    move.put(h_s, h_out)
    move.put(y_s, y_out)
    move.drain()


def down_back_kernel(n, groups, place, *refs):
    dys, ws = refs[:n], refs[n : n + groups]
    dy_out, dg_out, w_up_out, w_down_out, dy_s, dg_s, w_up, w_down, sems = refs[n + groups :]
    move = Mover(sems)
    j, g = place.j, place.group
    rows = dys[0].shape[0]
    chunk = w_down.shape[0] // groups
    mine = w_up.shape[1]
    feats = w_up.shape[0] // groups
    first, last = [], []
    for i in range(groups):
        for c in range(w_down.shape[1] // mine):
            source = ws[i].at[feats + c * chunk : feats + (c + 1) * chunk, :]
            first.append(move.start(source, w_down.at[rows_at(g ^ i, chunk), c * mine : (c + 1) * mine]))
    copies = [move.start(dys[r], dy_s.at[rows_at(j ^ r, rows), :]) for r in range(n)]
    for i in range(groups):
        last.append(move.start(ws[i].at[:feats, :], w_up.at[rows_at(g ^ i, feats), :]))
    for copy in first:
        copy.wait()
    move.put(w_down, w_down_out)
    for copy in copies:
        copy.wait()
    block = min(512, dy_s.shape[0])
    for i in range(dy_s.shape[0] // block):
        at = slice(i * block, (i + 1) * block)
        dg_s[at, :] = dot(dy_s[at, :], w_down[...], NT)
        move.put(dg_s.at[at, :], dg_out.at[at, :])
    for copy in last:
        copy.wait()
    move.put(w_up, w_up_out)
    move.put(dy_s, dy_out)
    move.drain()


def ffn_kernel(n, place, *refs):
    hs = refs[:n]
    w_up_in, b_up_in, dg_in = refs[n : n + 3]
    h_out, g_out, du_out, keep, send, db_out = refs[n + 3 : n + 9]
    w_up, b_up, dg, h_s, g_s, du_s, dh_s, send_s, db, sems = refs[n + 9 :]
    move = Mover(sems)
    rows = hs[0].shape[0]
    total = n * rows
    copies = [move.start(hs[r], h_s.at[rows_at(place.j ^ r, rows), :]) for r in range(n)]
    copies += [move.start(w_up_in, w_up), move.start(b_up_in, b_up)]
    late = move.start(dg_in, dg)
    for copy in copies:
        copy.wait()
    block = min(512, total)
    sums = jnp.zeros(db.shape, f32)
    for i in range(total // block):
        at = slice(i * block, (i + 1) * block)
        u = dot(h_s[at, :], w_up[...]) + b_up[...]
        cdf = 0.5 * (1.0 + lax.erf(u * inv_root_two))
        g_s[at, :] = (u * cdf).astype(bf16)
        slope = cdf + u * jnp.exp(-0.5 * u * u) * inv_root_tau
        if i == 0:
            late.wait()
        du = (dg[at, :] * slope).astype(bf16)
        du_s[at, :] = du
        sums = sums + jnp.sum(du.astype(f32), axis=0, keepdims=True)
        dh_s[at, :] = dot(du, w_up[...], NT)
    db[...] = sums
    send_rows(move, place, n, rows, dh_s, send_s, keep, send)
    move.put(h_s, h_out)
    move.put(g_s, g_out)
    move.put(du_s, du_out)
    move.put(db, db_out)
    move.drain()


def down_kernel(n, place, g_in, w_in, keep, send, g, w, out_s, send_s, sems):
    move = Mover(sems)
    for copy in [move.start(w_in, w), move.start(g_in, g)]:
        copy.wait()
    total = g.shape[0]
    block = min(512, total)
    for i in range(total // block):
        at = slice(i * block, (i + 1) * block)
        out_s[at, :] = dot(g[at, :], w[...])
    send_rows(move, place, n, total // n, out_s, send_s, keep, send)
    move.drain()


def ffn_grads_kernel(groups, place, h_in, du_in, dy_in, g_in, *refs):
    outs = refs[:groups]
    h, du, dy, g, grads, stage, sems = refs[groups:]
    move = Mover(sems)
    loads = [move.start(a, b) for a, b in ((h_in, h), (du_in, du), (dy_in, dy), (g_in, g))]
    feats = h.shape[1] // groups
    mine = du.shape[1]
    chunk = mine // groups
    loads[0].wait()
    loads[1].wait()
    for i in range(groups):
        grads[i, :feats, :] = dot(h[:, i * feats : (i + 1) * feats], du[...], TN)
    loads[2].wait()
    loads[3].wait()
    for c in range(dy.shape[1] // mine):
        part = dot(g[...], dy[:, c * mine : (c + 1) * mine], TN)
        for i in range(groups):
            grads[i, feats + c * chunk : feats + (c + 1) * chunk, :] = part[i * chunk : (i + 1) * chunk, :]
    for i in range(1, groups):
        stage[i - 1] = grads[place.group ^ i].astype(bf16)
        move.put(stage.at[i - 1], outs[i])
    move.put(grads.at[place.group], outs[0])
    move.drain()


def pair_kernel(place, keep, recv, *refs):
    count = (len(refs) - 3) // 2
    outs = refs[:count]
    keep_s, recv_s = refs[count : count + 2]
    stage, sems = refs[count + 2 : 2 * count + 2], refs[2 * count + 2]
    move = Mover(sems)
    rows = outs[0].shape[0]
    order = list(range(1, count)) + [0]
    loads = {}
    for i in order:
        here = slice(i * rows, (i + 1) * rows)
        loads[i] = (
            move.start(keep.at[here, :], keep_s.at[here, :]),
            move.start(recv.at[here, :], recv_s.at[here, :]),
        )
    for i in order:
        here = slice(i * rows, (i + 1) * rows)
        for copy in loads[i]:
            copy.wait()
        stage[i][...] = (keep_s[here, :] + recv_s[here, :].astype(f32)).astype(outs[i].dtype)
        move.put(stage[i], outs[i])
    move.drain()


def fold_kernel(count, place, *refs):
    ins, outs = refs[: 2 * count], refs[2 * count : 3 * count]
    held, stage, sems = refs[3 * count : 5 * count], refs[5 * count : 6 * count], refs[6 * count]
    move = Mover(sems)
    loads = [move.start(a, b) for a, b in zip(ins, held)]
    for i in range(count):
        loads[i].wait()
        loads[count + i].wait()
        stage[i][...] = (held[i][...].astype(f32) + held[count + i][...].astype(f32)).astype(bf16)
        move.put(stage[i], outs[i])
    move.drain()


def out_kernel(count, place, *refs):
    ins = refs[: count + 2]
    kept, sent = refs[count + 2 : count + 4]
    held = refs[count + 4 : 2 * count + 6]
    out_s, sems = refs[2 * count + 6 :]
    move = Mover(sems)
    for copy in [move.start(a, b) for a, b in zip(ins, held)]:
        copy.wait()
    total = held[0][...] + held[count][...]
    for i in range(1, count):
        total = total + held[i][...].astype(f32)
    out_s[...] = (total + held[count + 1][7:8, :]).astype(bf16)
    half = kept.shape[0]
    move.put(out_s.at[half:, :], sent)
    move.put(out_s.at[:half, :], kept)
    move.drain()


def mid_back_kernel(count, place, *refs):
    ins = refs[: count + 3]
    dy1_out, da_out, small_out = refs[count + 3 : count + 6]
    held = refs[count + 6 : 2 * count + 9]
    dy1_s, da_s, small, sems = refs[2 * count + 9 :]
    move = Mover(sems)
    for copy in [move.start(a, b) for a, b in zip(ins, held)]:
        copy.wait()
    dh = held[0][...]
    for i in range(1, count):
        dh = dh + held[i][...].astype(f32)
    y, vec, dy = held[count : count + 3]
    scaled, inv_std = normalize(y[...])
    dyf = dy[...].astype(f32)
    dy1 = dyf + norm_back(dh, scaled, inv_std, vec[5:6, :])
    da = dy1.astype(bf16)
    da_s[...] = da
    move.put(da_s, da_out)
    dy1_s[...] = dy1
    move.put(dy1_s, dy1_out)
    small[0:1, :] = jnp.sum(dh * scaled, axis=0, keepdims=True)
    small[1:2, :] = jnp.sum(dh, axis=0, keepdims=True)
    small[2:3, :] = jnp.sum(da.astype(f32), axis=0, keepdims=True)
    small[3:4, :] = jnp.sum(dyf, axis=0, keepdims=True)
    move.put(small, small_out)
    move.drain()


def attend_back_kernel(n, half, qb, place, *refs):
    das, ins = refs[:n], refs[n : n + 4]
    dqkv_out, keep, send, db_out, da_out = refs[n + 4 : n + 9]
    da, qkv, lse, wo, w, dqkv, dh_s, send_s, db, do, bias, acc_k, acc_v, sems = refs[n + 9 :]
    rows = 2 * half
    move = Mover(sems)
    copies = [move.start(das[r], da.at[rows_at(place.j ^ r, rows), :]) for r in range(n)]
    loads = [move.start(a, b) for a, b in zip(ins, (wo, qkv, lse, w))]
    total = qkv.shape[0]
    hd = do.shape[1]
    heads = hd // HEAD
    bias[...] = jnp.where(key_mask(place, total, n, half, 128), 0.0, -1.0).astype(f32)
    loads[0].wait()
    for copy in copies:
        copy.wait()
    move.put(da, da_out)
    block = min(512, total)
    for i in range(total // block):
        at = slice(i * block, (i + 1) * block)
        do[at, :] = dot(da[at, :], wo[...], NT).astype(bf16)
    for copy in loads[1:]:
        copy.wait()
    for head in range(heads):
        cols = slice(head * HEAD, (head + 1) * HEAD)
        kh = qkv[:, hd + head * HEAD : hd + (head + 1) * HEAD]
        vh = qkv[:, 2 * hd + head * HEAD : 2 * hd + (head + 1) * HEAD]
        kt = kh.astype(f32).T.astype(bf16)
        acc_k[...] = jnp.zeros_like(acc_k)
        acc_v[...] = jnp.zeros_like(acc_v)

        def step(i, _, cols=cols, kh=kh, vh=vh, kt=kt, head=head):
            at = rows_at(i, qb)
            qh = qkv[at, cols]
            doh = do[at, cols]
            scores = dot(kh, qh, NT)
            probs = jnp.where(bias[:, 0:1] >= 0.0, jnp.exp(scores - lse[head : head + 1, at]), 0.0)
            dp = dot(vh, doh, NT)
            centre = jnp.sum(probs * dp, axis=0, keepdims=True)
            ds = (probs * (dp - centre)).astype(bf16)
            acc_v[...] += dot(probs.astype(bf16), doh)
            acc_k[...] += dot(ds, qh)
            dq = dot(kt, ds)
            dqkv[at, cols] = (dq.T.astype(bf16).astype(f32) * 0.125).astype(bf16)
            return 0

        lax.fori_loop(0, total // qb, step, 0)
        dqkv[:, hd + head * HEAD : hd + (head + 1) * HEAD] = acc_k[...].astype(bf16)
        dqkv[:, 2 * hd + head * HEAD : 2 * hd + (head + 1) * HEAD] = acc_v[...].astype(bf16)
    move.put(dqkv, dqkv_out)
    sums = jnp.zeros(db.shape, f32)
    for i in range(total // block):
        at = slice(i * block, (i + 1) * block)
        grads = dqkv[at, :]
        sums = sums + jnp.sum(grads.astype(f32), axis=0, keepdims=True)
        dh_s[at, :] = dot(grads, w[...], NT)
    db[...] = sums
    send_rows(move, place, n, rows, dh_s, send_s, keep, send)
    move.put(db, db_out)
    move.drain()


def attn_grads_kernel(n, dp_size, groups, first_row, place, *refs):
    ins, outs = refs[:7], refs[7 : 7 + dp_size]
    dqkv, h, w, hat, two, db, up, small, grads, packed_s, sems = refs[7 + dp_size :]
    move = Mover(sems)
    j = place.j
    loads = [move.start(a, b) for a, b in zip(ins, (dqkv, h, w, hat, two, db, up))]
    ndev = packed_s.shape[0]
    hd = dqkv.shape[1] // 3
    rs = h.shape[1] // ndev
    chunk = up.shape[1] // groups
    loads[0].wait()
    loads[1].wait()
    grads[...] = dot(h[...], dqkv[...], TN).astype(bf16)
    for copy in loads[2:]:
        copy.wait()
    small[...] = jnp.zeros_like(small)
    step_rows = min(512, hat.shape[0])

    def step(i, _):
        at = rows_at(i, step_rows)
        dh = dot(dqkv[at, :], w[...], NT)
        small[0:1, :] += jnp.sum(dh * hat[at, :].astype(f32), axis=0, keepdims=True)
        small[1:2, :] += jnp.sum(dh, axis=0, keepdims=True)
        return 0

    lax.fori_loop(0, hat.shape[0] // step_rows, step, 0)
    small[4:8, :] = two[...]
    zeros = jnp.zeros((packed_s.shape[1] - rs, packed_s.shape[2]), bf16)
    for d in range(ndev):
        packed_s[d, rs:, :] = zeros
        packed_s[d, :rs, :] = grads[d * rs : (d + 1) * rs, :]
        packed_s[d, first_row : first_row + 8, :rs] = small[:, d * rs : (d + 1) * rs].astype(bf16)
    for t in range(groups):
        cols = slice(t * rs, (t + 1) * rs)
        at = j * groups + t
        packed_s[at, first_row + 2 : first_row + 3, :rs] = db[:, :hd][:, cols].astype(bf16)
        packed_s[at, first_row + 3 : first_row + 4, :rs] = db[:, 2 * hd :][:, cols].astype(bf16)
        packed_s[t * n + j, first_row : first_row + 1, hd : hd + chunk] = up[
            :, t * chunk : (t + 1) * chunk
        ].astype(bf16)
    seq_size = ndev // dp_size
    for i in list(range(1, dp_size)) + [0]:
        move.put(packed_s.at[pl.ds((place.dp ^ i) * seq_size, seq_size)], outs[i])
    move.drain()


def out_grads_kernel(dp_size, groups, place, da_in, o_in, *refs):
    outs = refs[:dp_size]
    da, o, grads, stage, sems = refs[dp_size:]
    move = Mover(sems)
    for copy in [move.start(o_in, o), move.start(da_in, da)]:
        copy.wait()
    all_rows = dot(o[...], da[...], TN)
    rs = grads.shape[1]
    for t in range(groups):
        grads[t] = all_rows[t * rs : (t + 1) * rs, :]
    slots = groups // dp_size
    for k in range(dp_size):
        for i in range(slots):
            stage[k, i] = grads[(place.dp ^ k) * slots + (place.h ^ i)].astype(bf16)
        move.put(stage.at[k], outs[k])
    move.drain()


def last_kernel(count, place, *refs):
    ins, rider = refs[: count + 3], refs[count + 3]
    kept, sent = refs[count + 4 : count + 6]
    held = refs[count + 6 : 2 * count + 9]
    out_s, sems = refs[2 * count + 9 :]
    move = Mover(sems)
    half = kept.shape[0]
    move.put(rider.at[1], sent.at[half:, :])
    for copy in [move.start(a, b) for a, b in zip(ins, held)]:
        copy.wait()
    x, dy1, vec = held[count:]
    dh = held[0][...]
    for i in range(1, count):
        dh = dh + held[i][...].astype(f32)
    scaled, inv_std = normalize(x[...].astype(f32))
    out_s[...] = (dy1[...] + norm_back(dh, scaled, inv_std, vec[0:1, :])).astype(bf16)
    move.put(out_s.at[half:, :], sent.at[:half, :])
    move.put(out_s.at[:half, :], kept)
    move.drain()


def ffn_sum_kernel(count, place, *refs):
    ins, (up_out, down_out) = refs[:count], refs[count : count + 2]
    held, (total, up_s, down_s, sems) = refs[count + 2 : 2 * count + 2], refs[2 * count + 2 :]
    move = Mover(sems)
    for copy in [move.start(a, b) for a, b in zip(ins, held)]:
        copy.wait()
    ffn = held[0][...].astype(f32)
    for piece in held[1:]:
        ffn = ffn + piece[...].astype(f32)
    total[...] = ffn
    n, rs, mine = up_s.shape
    chunk, width = down_s.shape
    for m in range(n):
        up_s[m] = total[m * rs : (m + 1) * rs, :].astype(bf16)
    move.put(up_s, up_out)
    feats = n * rs
    for c in range(width // mine):
        down_s[:, c * mine : (c + 1) * mine] = total[feats + c * chunk : feats + (c + 1) * chunk, :]
    move.put(down_s, down_out)
    move.drain()


def unpack_kernel(n, groups, first_row, place, *refs):
    back, up_back, out_w = refs[:3]
    halves = refs[3:7]
    output, frames_grad, out_w_grad, up, wq, wk, wv = refs[7:14]
    vectors = refs[14:23]
    back_s, up_back_s, in_s, out_s, up_s, q_s, k_s, v_s = refs[23:31]
    vectors_s, sems = refs[31:40], refs[40]
    move = Mover(sems)
    load, more, third = move.start(back, back_s), move.start(up_back, up_back_s), move.start(out_w, in_s)
    half = output.shape[1]
    for i, target in enumerate((output, frames_grad)):
        move.put(halves[2 * i], target.at[place.h])
        move.put(halves[2 * i + 1].at[:half, :], target.at[1 - place.h])
    third.wait()
    out_s[...] = in_s[...].astype(f32)
    move.put(out_s, out_w_grad)
    rs = wq.shape[0]
    hd = wq.shape[1] // n
    chunk = up.shape[1] // (n * groups)
    more.wait()
    for m in range(n):
        for g in range(groups):
            at = (g * n + m) * chunk
            up_s[:, at : at + chunk] = up_back_s[m, :, g * chunk : (g + 1) * chunk].astype(f32)
    move.put(up_s, up)
    load.wait()
    sums = jnp.zeros((8, 3 * hd), f32)
    for m in range(n):
        cols = slice(m * hd, (m + 1) * hd)
        total = back_s[m].astype(f32)
        for i in range(m + n, back_s.shape[0], n):
            total = total + back_s[i].astype(f32)
        for i, target in enumerate((q_s, k_s, v_s)):
            target[:, cols] = total[:rs, i * hd : (i + 1) * hd]
        sums = sums + total[first_row:, :]
    for a, b in ((q_s, wq), (k_s, wk), (v_s, wv)):
        move.put(a, b)
    for i in range(8):
        vectors_s[i][...] = sums[i : i + 1, :rs]
    vectors_s[8][...] = sums[0:1, hd : hd + chunk]
    for a, b in zip(vectors_s, vectors):
        move.put(a, b)
    move.drain()


def on_device(
    dp_size,
    seq_size,
    frames,
    out_grad,
    order,
    lengths,
    first_gain,
    first_shift,
    query_weight,
    query_bias,
    key_weight,
    value_weight,
    value_bias,
    output_weight,
    output_bias,
    second_gain,
    second_shift,
    up_weight,
    up_bias,
    down_weight,
    down_bias,
):
    slots, half, width = frames.shape
    n = seq_size // slots
    groups = dp_size * slots
    ndev = dp_size * seq_size
    hd = width // n
    heads = hd // HEAD
    rs = query_weight.shape[0]
    hidden = up_weight.shape[1]
    chunk = hidden // ndev
    mine = hidden // n
    parts = width // mine
    feats = n * rs
    rows = 2 * half
    total = n * rows
    qb = 512
    count = n // 2
    both = ("dp", "seq")
    first_row = -(-rs // 8) * 8
    block_rows = first_row + 8

    scale = -(-total // 1024)
    grid = (slots, n, scale)

    def xor(value, bit):
        return lax.ppermute(value, "seq", [(i, i ^ bit) for i in range(seq_size)])

    def gather_direct(value):
        got = [xor(value, r) for r in range(n - 2, 0, -2)]
        return [value] + got[::-1]

    def gather_pair(even):
        out = []
        for piece in even:
            out += [piece, xor(piece, 1)]
        return out

    def pair(keep, recv):
        outs = [sds((rows, width), f32)] + [sds((rows, width), bf16)] * (count - 1)
        return call(
        grid,
            pair_kernel,
            [keep, Near(recv)],
            near(outs),
            "pair",
            cost(1),
            scratch=[vmem(keep), vmem(recv)] + [vmem(o) for o in outs],
            sems=3 * count,
        )

    def scatter(pieces):
        return [pieces[0]] + [xor(pieces[i], 2 * i) for i in range(count - 1, 0, -1)][::-1]

    def to_group(value, i):
        pairs = []
        for d in range(ndev):
            dp_of, seq_of = d // seq_size, d % seq_size
            g_of = (dp_of * slots + seq_of // n) ^ i
            pairs.append((d, g_of // slots * seq_size + g_of % slots * n + seq_of % n))
        return lax.ppermute(value, both, pairs)

    def members(value):
        index = [[s * n + i for i in range(n)] for s in range(slots)]
        return lax.all_to_all(value, "seq", 0, 0, tiled=True, axis_index_groups=index)

    def fold(kept, got):
        outs = [sds(a.shape, bf16) for a in kept]
        return call(
            grid,
            functools.partial(fold_kernel, len(kept)),
            near(list(kept) + list(got)),
            near(outs),
            "fold",
            cost(2),
            scratch=[vmem(a) for a in list(kept) + list(got) + outs],
            sems=3 * len(kept),
        )

    def spread(pieces):
        bit = len(pieces)
        while bit < groups:
            pieces = pieces + [to_group(piece, bit) for piece in pieces]
            bit *= 2
        return pieces

    def to_dp(value, i):
        return lax.ppermute(value, "dp", [(d, d ^ i) for d in range(dp_size)])

    def owner_pairs(k):
        pairs = []
        for d in range(ndev):
            g_of = (d % groups) ^ (k * slots)
            pairs.append((d, g_of // slots * seq_size + g_of % slots * n + d // groups))
        return pairs

    owners = owner_pairs(0)
    out_w = jnp.stack([lax.ppermute(output_weight, both, owner_pairs(k)) for k in range(dp_size)])

    small_in = [first_gain, first_shift, query_bias, value_bias, output_bias, second_gain, second_shift, down_bias]
    small_in = [v.reshape(1, -1) for v in small_in + [up_bias]]
    weights_in = [query_weight, key_weight, value_weight]
    half_sds, row_sds = sds((half, width), bf16), sds((rows, width), bf16)
    packed_sds, up_sds = sds((seq_size, block_rows, 3 * hd), bf16), sds((n, rs, mine), bf16)
    x_own, x_send, dy_own, dy_send = call(
        grid, rows_kernel, [frames, out_grad], near([half_sds] * 4), "rows", cost(1), sems=4
    )
    x_recv = xor(x_send, n)
    (packed,) = call(
        grid,
        functools.partial(pack_kernel, n, slots, groups, first_row),
        [after(weights_in[0], x_send)] + weights_in[1:] + small_in,
        near([packed_sds]),
        "pack",
        cost(2),
        scratch=[vmem(w) for w in weights_in] + [vmem(v) for v in small_in] + [pltpu.VMEM((n, block_rows, 3 * hd), bf16)],
        sems=12 + slots,
    )
    (up_packed,) = call(
        grid,
        functools.partial(pack_up_kernel, n, groups),
        [up_weight],
        near([up_sds]),
        "pack_up",
        cost(1),
        scratch=[vmem(up_weight), vmem(up_sds)],
        sems=2,
    )
    attn_w = lax.all_to_all(packed, "seq", 0, 0, tiled=True)
    up_mine = members(after(up_packed, attn_w))
    x = jnp.concatenate([x_own, x_recv])
    x_even = gather_direct(x)
    wos = [out_w, xor(out_w, n)]
    dy_recv = xor(after(dy_send, attn_w), n)
    attn_ws = [attn_w]
    while len(attn_ws) < dp_size:
        attn_ws += [to_dp(piece, len(attn_ws)) for piece in attn_ws]
    ffn_sds = sds((feats + parts * chunk, mine), bf16)
    (ffn_w,) = call(
        grid,
        functools.partial(join_kernel, n),
        near([up_mine.reshape(feats, mine), down_weight]),
        near([ffn_sds]),
        "join",
        cost(1),
        sems=1 + parts,
    )
    ffn_half = to_group(after(ffn_w, attn_w), 1)
    xs = gather_pair([after(piece, attn_ws[-1], wos[-1]) for piece in x_even])
    dy = jnp.concatenate([dy_own, dy_recv])

    ffn_go, dy_go, xs, attn_ws, wos = lax.optimization_barrier((ffn_w, dy, tuple(xs), tuple(attn_ws), tuple(wos)))
    xs, attn_ws, wos = list(xs), list(attn_ws), list(wos)
    ffn_ws = [ffn_w, ffn_half, to_group(ffn_go, 2)]
    dy_even = gather_direct(dy_go)
    x_sds = sds((total, width), bf16)
    keep_sds, send_sds = sds((total // 2, width), f32), sds((total // 2, width), bf16)
    outs = [
        x_sds,
        x_sds,
        sds((total, 3 * hd), bf16),
        sds((total, hd), bf16),
        sds((heads, total), f32),
        sds((width, 3 * hd), bf16),
        sds((8, width), f32),
        sds((1, mine), f32),
        sds((hd, width), bf16),
        keep_sds,
        send_sds,
    ]
    s_hat, s_h, s_qkv, s_o, s_lse, s_w, s_vec, s_bias, s_wo, _, s_send = [vmem(o) for o in outs]
    s_rows = pltpu.VMEM((total, width), f32)
    s_got = pltpu.VMEM((ndev, block_rows, 3 * hd), bf16)
    s_wo3 = pltpu.VMEM((groups, rs, width), bf16)
    hat, h_first, qkv, o_heads, lse, w_qkv, vec, bias_up, wo, keep, send = call(
        grid,
        functools.partial(first_kernel, n, dp_size, groups, half, qb, first_row),
        near(xs + attn_ws + wos),
        outs[:-1] + near(outs[-1:]),
        "first",
        cost(17),
        scratch=[vmem(x_sds), s_hat, s_h, s_qkv, s_o, s_lse, s_got, s_w, s_vec, s_bias, s_wo3, s_wo, s_rows, s_send]
        + [pltpu.VMEM((total, 128), f32)],
        sems=3 * n + groups + dp_size + 10,
        lengths=(order, lengths),
        limit=48,
    )
    send = after(send, *ffn_ws[1:], *dy_even[1:])

    y_sds = sds((rows, width), f32)
    y_pieces = pair(keep, xor(send, 1))
    ys = scatter(y_pieces)
    dys = gather_pair([dy_even[0]] + [after(piece, y_pieces[0]) for piece in dy_even[1:]])
    ffn_ws = spread(ffn_ws + [to_group(after(ffn_ws[1], y_pieces[0]), 2)])
    y1, h2 = call(
        grid,
        functools.partial(mid_kernel, count),
        near(ys + [x]) + [vec],
        [y_sds, Near(row_sds)],
        "mid",
        cost(2),
        scratch=[vmem(a) for a in ys + [row_sds, vec, y_sds, row_sds]],
        sems=count + 4,
    )
    h2_even = gather_direct(h2)

    outs = [x_sds, sds((total, mine), f32), sds((width, mine), bf16), sds((mine, width), bf16)]
    dy_all, dg, w_up, w_down = call(
        grid,
        functools.partial(down_back_kernel, n, groups),
        near(dys + ffn_ws),
        outs,
        "down_back",
        cost(5),
        scratch=[vmem(o) for o in outs],
        sems=2 * n + groups * (parts + 1) + 3,
        limit=14 * scale,
    )
    h2s = gather_pair(h2_even[:1] + [after(piece, dg) for piece in h2_even[1:]])

    act_sds = sds((total, mine), bf16)
    outs = [x_sds, act_sds, act_sds, keep_sds, send_sds, sds((1, mine), f32)]
    h2_all, g, du, keep, send, d_bias_up = call(
        grid,
        functools.partial(ffn_kernel, n),
        near(h2s) + [w_up, bias_up, dg],
        outs[:4] + near(outs[4:5]) + outs[5:],
        "ffn",
        cost(9),
        scratch=[vmem(a) for a in [w_up, bias_up, dg] + outs[:3]] + [s_rows, vmem(outs[4]), vmem(outs[5])],
        sems=3 * n + 7,
        limit=28 * scale,
    )
    dh2 = scatter(pair(keep, xor(send, 1)))

    g_then = after(g, dh2[0])
    out_keep, out_send = call(
        grid,
        functools.partial(down_kernel, n),
        [g_then, w_down],
        [keep_sds, Near(send_sds)],
        "down",
        cost(4),
        scratch=[vmem(g), vmem(w_down), s_rows, vmem(send_sds)],
        sems=n + 2,
        limit=16 * scale,
    )
    ffn_parts = call(
        grid,
        functools.partial(ffn_grads_kernel, groups),
        [h2_all, du, dy_all, g_then],
        [sds(ffn_sds.shape, f32)] + near([ffn_sds] * (groups - 1)),
        "ffn_grads",
        cost(5),
        scratch=[vmem(a) for a in (x_sds, act_sds, x_sds, act_sds)]
        + [pltpu.VMEM((groups,) + ffn_sds.shape, f32), pltpu.VMEM((groups - 1,) + ffn_sds.shape, bf16)],
        sems=4 + groups,
        limit=20 * scale,
    )

    small_sds = sds((4, width), f32)
    outs = [y_sds, row_sds, small_sds]
    dy1, da, small_two = call(
        grid,
        functools.partial(mid_back_kernel, count),
        near(dh2) + [after(y1, ffn_parts[0], out_keep), vec, Near(dy)],
        outs[:1] + near(outs[1:2]) + outs[2:],
        "mid_back",
        cost(3),
        scratch=[vmem(a) for a in dh2 + [y1, vec, row_sds] + outs],
        sems=count + 6,
    )
    da_even = gather_direct(da)
    bit = groups // 2
    while bit > 2:
        ffn_parts = fold(ffn_parts[:bit], [to_group(piece, bit) for piece in ffn_parts[bit:]])
        bit //= 2
    ffn_got = [to_group(piece, 2) for piece in ffn_parts[2:4]]
    out_kept = pair(out_keep, xor(after(out_send, da), 1))
    (ffn_next,) = fold([after(ffn_parts[1], out_kept[0])], ffn_got[1:])
    das = gather_pair([da_even[0]] + [after(piece, ffn_next) for piece in da_even[1:]])

    out_kept, das, ffn_next = lax.optimization_barrier((tuple(out_kept), tuple(das), ffn_next))
    out_kept, das = list(out_kept), list(das)
    ffn_got = [ffn_got[0], to_group(ffn_next, 1)]
    out_pieces = scatter(out_kept)
    ins = [wo, qkv, lse, w_qkv]
    outs = [sds((total, 3 * hd), bf16), keep_sds, send_sds, sds((1, 3 * hd), f32), x_sds]
    d_qkv, keep, send, d_bias_qkv, da_all = call(
        grid,
        functools.partial(attend_back_kernel, n, half, qb),
        near(das) + ins,
        outs[:2] + near(outs[2:3]) + outs[3:],
        "attend_back",
        cost(15),
        scratch=[vmem(x_sds)]
        + [vmem(a) for a in (qkv, lse, wo, w_qkv, outs[0])]
        + [s_rows, vmem(outs[2]), vmem(outs[3]), pltpu.VMEM((total, hd), bf16), pltpu.VMEM((total, 128), f32)]
        + [pltpu.VMEM((total, HEAD), f32)] * 2,
        sems=2 * n + 9,
        lengths=(order, lengths),
        limit=48,
    )
    recv = xor(after(send, *out_pieces[1:], *ffn_got), 1)

    ins = [d_qkv, h_first, w_qkv, hat, small_two, d_bias_qkv, d_bias_up]
    attn_parts = call(
        grid,
        functools.partial(attn_grads_kernel, n, dp_size, groups, first_row),
        ins,
        near([packed_sds] * dp_size),
        "attn_grads",
        cost(6),
        scratch=[vmem(a) for a in ins]
        + [
            pltpu.VMEM((8, width), f32),
            pltpu.VMEM((width, 3 * hd), bf16),
            pltpu.VMEM((ndev, block_rows, 3 * hd), bf16),
        ],
        sems=7 + dp_size,
        limit=20 * scale,
    )
    dh1_pieces = pair(after(keep, attn_parts[0]), recv)
    dh1 = scatter(dh1_pieces)
    bit = dp_size // 2
    while bit > 1:
        attn_parts = fold(attn_parts[:bit], [to_dp(piece, bit) for piece in attn_parts[bit:]])
        bit //= 2
    attn_got = to_dp(attn_parts[1], 1)

    ffn_sums = [after(ffn_parts[0], dh1_pieces[0])] + ffn_got
    down_sds = sds((chunk, width), f32)
    up_back, down_weight_grad = call(
        grid,
        functools.partial(ffn_sum_kernel, 3),
        ffn_sums[:1] + near(ffn_sums[1:]),
        [Near(up_sds), down_sds],
        "ffn_sum",
        cost(2),
        scratch=[vmem(a) for a in ffn_sums] + [pltpu.VMEM(ffn_sds.shape, f32), vmem(up_sds), vmem(down_sds)],
        sems=5,
    )
    up_back = members(up_back)
    out_parts = call(
        grid,
        functools.partial(out_grads_kernel, dp_size, groups),
        [da_all, after(o_heads, dh1_pieces[0])],
        near([sds((slots, rs, width), bf16)] * dp_size),
        "out_grads",
        cost(2),
        scratch=[
            vmem(x_sds),
            vmem(o_heads),
            pltpu.VMEM((groups, rs, width), f32),
            pltpu.VMEM((dp_size, slots, rs, width), bf16),
        ],
        sems=2 + dp_size,
        limit=10 * scale,
    )
    bit = dp_size // 2
    while bit > 1:
        out_parts = fold(out_parts[:bit], [to_dp(piece, bit) for piece in out_parts[bit:]])
        bit //= 2

    (attn_sum,) = fold([after(attn_parts[0], up_back)], [attn_got])
    back = lax.all_to_all(attn_sum, "seq", 0, 0, tiled=True)
    (out_w_sum,) = fold([after(out_parts[0], attn_sum)], [to_dp(out_parts[1], 1)])

    ins = out_pieces + [y1, vec]
    out_own, out_sent = call(
        grid,
        functools.partial(out_kernel, count),
        near([after(ins[0], attn_sum)] + ins[1:count]) + ins[count:],
        near([half_sds] * 2),
        "out",
        cost(2),
        scratch=[vmem(a) for a in ins + [row_sds]],
        sems=len(ins) + 2,
    )
    out_other = xor(out_sent, n)

    ins = dh1 + [x, after(dy1, attn_sum), vec]
    kept, sent = call(
        grid,
        functools.partial(last_kernel, count),
        near(ins[: count + 1]) + ins[count + 1 :] + near([out_w_sum]),
        near([half_sds, sds((half + rs, width), bf16)]),
        "last",
        cost(2),
        scratch=[vmem(a) for a in ins + [row_sds]],
        sems=len(ins) + 3,
    )
    other = xor(sent, n)
    out_w = (out_w_sum[0].astype(f32) + other[half:].astype(f32)).astype(bf16)
    out_w = lax.ppermute(out_w, both, [(b, a) for a, b in owners])
    frames_sds = sds(frames.shape, bf16)
    weight_sds = sds((rs, width), f32)
    outs = [weight_sds, sds((rs, hidden), f32)] + [weight_sds] * 3
    vectors = [sds((1, rs), f32)] * 8 + [sds((1, chunk), f32)]
    output, frames_grad, output_weight_grad, up_weight_grad, d_query, d_key, d_value, *vectors = call(
        grid,
        functools.partial(unpack_kernel, n, groups, first_row),
        near([back, up_back, out_w, out_own, out_other, kept, other]),
        [frames_sds] * 2 + outs + vectors,
        "unpack",
        cost(2),
        scratch=[vmem(a) for a in [back, up_back, out_w] + outs + vectors],
        sems=24,
    )
    vectors = [v.reshape(-1) for v in vectors]
    return (
        output,
        frames_grad,
        vectors[0],
        vectors[1],
        d_query,
        vectors[2],
        d_key,
        d_value,
        vectors[3],
        output_weight_grad,
        vectors[6],
        vectors[4],
        vectors[5],
        up_weight_grad,
        vectors[8],
        down_weight_grad,
        vectors[7],
    )


def solution(mesh):
    vector = P(("dp", "seq"))
    matrix = P(("dp", "seq"), None)
    rows = P("dp", "seq", None)
    return jax.shard_map(
        functools.partial(on_device, mesh.shape["dp"], mesh.shape["seq"]),
        mesh=mesh,
        in_specs=(
            rows,
            rows,
            P("dp"),
            P(),
            vector,
            vector,
            matrix,
            vector,
            matrix,
            matrix,
            vector,
            matrix,
            vector,
            vector,
            vector,
            matrix,
            vector,
            matrix,
            vector,
        ),
        out_specs=(
            rows,
            rows,
            vector,
            vector,
            matrix,
            vector,
            matrix,
            matrix,
            vector,
            matrix,
            vector,
            vector,
            vector,
            matrix,
            vector,
            matrix,
            vector,
        ),
        check_vma=False,
    )
```

profile of v0, /device:TPU:0, one launch (start us, length us, event | category | flops | bytes accessed | tf_op | source)
XLA Modules:
  0.0 260.1 jit_solution(4641636468737287110)
XLA Ops:
  1.8 1.9 pack.1
  3.8 7.4 %all-to-all-start = ((bf16[16,40,384]{2,1,0:T(8,128)(2,1)}), bf16[16,40,384]{2,1,0:T(8,128)(2,1)S(1)}, u32[]{:S(2)}, u32[]{:S(2)}) async-start(bf16[16,40,384]{2,1,0:T(8,128)(2,1)} %pack.1), calls=%async_computation | async-start | bytes 983040 | tf_op jit(solution)/shard_map/all_to_all | solution.py:875
  11.2 2.8 %collective-permute-start.1 = (bf16[64,1024]{1,0:T(8,128)(2,1)S(1)}, bf16[64,1024]{1,0:T(8,128)(2,1)S(1)}, u32[]{:S(2)}, u32[]{:S(2)}) collective-permute-start(bf16[64,1024]{1,0:T(8,128)(2,1)S(1)} %get-tuple-element.158), channel_id=1, source_target_pairs={{0,8},{1,9},{2,10},{3,11},{4,12},{5,13},{6,14},{7,15},{8,0},{9,1},... | collective-permute-start | bytes 393224 | tf_op jit(solution)/shard_map/ppermute | solution.py:773
  14.0 1.5 collective-permute-start.4
  16.1 9.3 %all-to-all-done.refs_10_ = bf16[16,40,384]{2,1,0:T(8,128)(2,1)S(1)} async-done(((bf16[16,40,384]{2,1,0:T(8,128)(2,1)}), bf16[16,40,384]{2,1,0:T(8,128)(2,1)S(1)}, u32[]{:S(2)}, u32[]{:S(2)}) %all-to-all-start) | async-done | bytes 491552 | tf_op jit(solution)/shard_map/all_to_all | solution.py:875
  25.4 1.5 collective-permute-start.2
  26.9 5.8 %collective-permute-done.1 = bf16[64,1024]{1,0:T(8,128)(2,1)S(1)} collective-permute-done((bf16[64,1024]{1,0:T(8,128)(2,1)S(1)}, bf16[64,1024]{1,0:T(8,128)(2,1)S(1)}, u32[]{:S(2)}, u32[]{:S(2)}) %collective-permute-start.1) | collective-permute-done | bytes 131104 | tf_op jit(solution)/shard_map/ppermute | solution.py:773
  32.9 2.9 %collective-permute-start.9 = (bf16[128,1024]{1,0:T(8,128)(2,1)S(1)}, bf16[128,1024]{1,0:T(8,128)(2,1)S(1)}, u32[]{:S(2)}, u32[]{:S(2)}) collective-permute-start(bf16[128,1024]{1,0:T(8,128)(2,1)S(1)} %constant_dynamic-update-slice_fusion.2.refs_2_.refs_4_), channel_id=1, source_target_pairs={{0,4},{1,5},{2,6},{3,7},{4,0},{5,1},{6,2},{7,3},{8,12},{9,13},{10,... | collective-permute-start | bytes 786440 | tf_op jit(solution)/shard_map/ppermute | solution.py:773
  36.3 1.7 pack_up.1
  38.1 3.4 %all-to-all-start.1 = ((bf16[8,32,512]{2,1,0:T(8,128)(2,1)}), bf16[8,32,512]{2,1,0:T(8,128)(2,1)S(1)}, u32[]{:S(2)}, u32[]{:S(2)}) async-start(bf16[8,32,512]{2,1,0:T(8,128)(2,1)} %pack_up.1), calls=%async_computation.1 | async-start | bytes 524288 | tf_op jit(solution)/shard_map/all_to_all | solution.py:811
  42.7 7.4 %collective-permute-done.5.refs_13_ = bf16[2,32,1024]{2,1,0:T(8,128)(2,1)S(1)} collective-permute-done((bf16[2,32,1024]{2,1,0:T(8,128)(2,1)S(1)}, bf16[2,32,1024]{2,1,0:T(8,128)(2,1)S(1)}, u32[]{:S(2)}, u32[]{:S(2)}) %collective-permute-start.5) | collective-permute-done | bytes 131104 | tf_op jit(solution)/shard_map/ppermute | solution.py:773
  50.8 3.4 %collective-permute-start = (bf16[64,1024]{1,0:T(8,128)(2,1)S(1)}, bf16[64,1024]{1,0:T(8,128)(2,1)S(1)}, u32[]{:S(2)}, u32[]{:S(2)}) collective-permute-start(bf16[64,1024]{1,0:T(8,128)(2,1)S(1)} %get-tuple-element.163), channel_id=1, source_target_pairs={{0,8},{1,9},{2,10},{3,11},{4,12},{5,13},{6,14},{7,15},{8,0},{9,1},... | collective-permute-start | bytes 393224 | tf_op jit(solution)/shard_map/ppermute | solution.py:773
  55.3 4.7 %collective-permute-done = bf16[64,1024]{1,0:T(8,128)(2,1)S(1)} collective-permute-done((bf16[64,1024]{1,0:T(8,128)(2,1)S(1)}, bf16[64,1024]{1,0:T(8,128)(2,1)S(1)}, u32[]{:S(2)}, u32[]{:S(2)}) %collective-permute-start) | collective-permute-done | bytes 131104 | tf_op jit(solution)/shard_map/ppermute | solution.py:773
  60.3 3.1 %collective-permute-start.17 = (bf16[128,1024]{1,0:T(8,128)(2,1)S(1)}, bf16[128,1024]{1,0:T(8,128)(2,1)S(1)}, u32[]{:S(2)}, u32[]{:S(2)}) collective-permute-start(bf16[128,1024]{1,0:T(8,128)(2,1)S(1)} %constant_dynamic-update-slice_fusion.refs_0_.refs_6_), channel_id=1, source_target_pairs={{0,6},{1,7},{2,4},{3,5},{4,2},{5,3},{6,0},{7,1},{8,14},{9,15},{10,... | collective-permute-start | bytes 786440 | tf_op jit(solution)/shard_map/ppermute | solution.py:773
  64.1 1.5 collective-permute-start.14
  65.6 13.1 %first.1 = (bf16[1024,1024]{1,0:T(8,128)(2,1)}, bf16[1024,1024]{1,0:T(8,128)(2,1)}, bf16[1024,384]{1,0:T(8,128)(2,1)}, bf16[1024,128]{1,0:T(8,128)(2,1)}, f32[2,...) custom-call(s32[2]{0:T(128)S(1)} %copy-done.3, ...), custom_call_target="tpu_custom_call" | custom-call | flops 19549999104 | bytes 11580160 | tf_op jit(solution)/shard_map/first/pallas_call | solution.py:82
  78.7 4.2 %collective-permute-done.13.refs_9_ = bf16[512,512]{1,0:T(8,128)(2,1)S(1)} collective-permute-done((bf16[512,512]{1,0:T(8,128)(2,1)S(1)}, bf16[512,512]{1,0:T(8,128)(2,1)S(1)}, u32[]{:S(2)}, u32[]{:S(2)}) %collective-permute-start.13) | collective-permute-done | bytes 524320 | tf_op jit(solution)/shard_map/ppermute | solution.py:807
  83.7 2.7 %collective-permute-done.18.refs_1_ = bf16[512,1024]{1,0:T(8,128)(2,1)S(1)} collective-permute-done((bf16[512,1024]{1,0:T(8,128)(2,1)S(1)}, bf16[512,1024]{1,0:T(8,128)(2,1)S(1)}, u32[]{:S(2)}, u32[]{:S(2)}) %collective-permute-start.18) | collective-permute-done | bytes 1048608 | tf_op jit(solution)/shard_map/ppermute | solution.py:773
  86.4 1.7 pair.4
  88.1 1.5 collective-permute-start.19
  89.6 2.0 collective-permute-start.21
  92.2 4.3 %collective-permute-done.19.refs_1_ = bf16[128,1024]{1,0:T(8,128)(2,1)S(1)} collective-permute-done((bf16[128,1024]{1,0:T(8,128)(2,1)S(1)}, bf16[128,1024]{1,0:T(8,128)(2,1)S(1)}, u32[]{:S(2)}, u32[]{:S(2)}) %collective-permute-start.19) | collective-permute-done | bytes 262176 | tf_op jit(solution)/shard_map/ppermute | solution.py:773
  96.5 2.3 collective-permute-done.20.refs_2_
  98.8 4.5 %collective-permute-done.21.refs_3_ = bf16[128,1024]{1,0:T(8,128)(2,1)S(1)} collective-permute-done((bf16[128,1024]{1,0:T(8,128)(2,1)S(1)}, bf16[128,1024]{1,0:T(8,128)(2,1)S(1)}, u32[]{:S(2)}, u32[]{:S(2)}) %collective-permute-start.21) | collective-permute-done | bytes 262176 | tf_op jit(solution)/shard_map/ppermute | solution.py:773
  103.3 2.1 mid.1
  105.4 1.3 collective-permute-start.32
  106.7 1.7 collective-permute-start.30
  109.0 4.0 %down_back.1 = (bf16[1024,1024]{1,0:T(8,128)(2,1)}, f32[1024,512]{1,0:T(8,128)}, bf16[1024,512]{1,0:T(8,128)(2,1)}, bf16[512,1024]{1,0:T(8,128)(2,1)}) custom-call(bf16[128,1024]{1,0:T(8,128)(2,1)S(1)} %constant_dynamic-update-slice_fusion.refs_0_.refs_6_, bf16[128,1024]{1,0:T(8,128)(2,1)S(1)} %collective-permute-done.24.refs_1_, ...), custom_call_target="tpu_custom_call" | custom-call | flops 5750000128 | bytes 10485760 | tf_op jit(solution)/shard_map/down_back/pallas_call | solution.py:82
  113.0 2.5 collective-permute-done.32.refs_6_
  115.5 5.2 %collective-permute-done.30.refs_4_ = bf16[128,1024]{1,0:T(8,128)(2,1)S(1)} collective-permute-done((bf16[128,1024]{1,0:T(8,128)(2,1)S(1)}, bf16[128,1024]{1,0:T(8,128)(2,1)S(1)}, u32[]{:S(2)}, u32[]{:S(2)}) %collective-permute-start.30) | collective-permute-done | bytes 262176 | tf_op jit(solution)/shard_map/ppermute | solution.py:773
  123.1 8.0 %ffn.1 = (bf16[1024,1024]{1,0:T(8,128)(2,1)}, bf16[1024,512]{1,0:T(8,128)(2,1)}, bf16[1024,512]{1,0:T(8,128)(2,1)}, f32[512,1024]{1,0:T(8,128)}, bf16[512,1024]{1,0:T(8,128)(2,1)S(1)}, /*index=5*/f32[1,512]{1,0:T(1,128)}) custom-call(bf16[128,1024]{1,0:T(8,128)(2,1)S(1)} %get-tuple-element.192.refs_0_, ...), custom_call_target="tpu_custom_call" | custom-call | flops 10350000128 | bytes 12587008 | tf_op jit(solution)/shard_map/ffn/pallas_call | solution.py:82
  131.3 2.5 collective-permute-done.34.refs_1_
  133.8 1.7 pair.5
  135.6 1.5 collective-permute-start.35
  137.3 1.8 collective-permute-start.37
  139.1 5.8 %ffn_grads.1 = (f32[512,512]{1,0:T(8,128)}, bf16[512,512]{1,0:T(8,128)(2,1)S(1)}, bf16[512,512]{1,0:T(8,128)(2,1)S(1)}, bf16[512,512]{1,0:T(8,128)(2,1)S(1)}) custom-call(bf16[1024,1024]{1,0:T(8,128)(2,1)} %get-tuple-element.215.refs_0_, bf16[1024,512]{1,0:T(8,128)(2,1)} %get-tuple-element.216.refs_1_, bf16[1024,1024]{1,0:T(8,128)(2,1)} %get-tuple-element.217.refs_2_, ...), custom_call_target="tpu_custom_call" | custom-call | flops 5750000128 | bytes 8912896 | tf_op jit(solution)/shard_map/ffn_grads/pallas_call | solution.py:82
  144.9 4.4 %down.1 = (f32[512,1024]{1,0:T(8,128)}, bf16[512,1024]{1,0:T(8,128)(2,1)S(1)}) custom-call(bf16[1024,512]{1,0:T(8,128)(2,1)} %get-tuple-element.207.refs_0_.refs_3_, bf16[512,1024]{1,0:T(8,128)(2,1)} %get-tuple-element.208.refs_1_), custom_call_target="tpu_custom_call" | custom-call | flops 4600000000 | bytes 5242880 | tf_op jit(solution)/shard_map/down/pallas_call | solution.py:82
  149.3 1.4 collective-permute-done.37.refs_3_
  150.8 2.6 mid_back.1
  155.2 1.3 collective-permute-start.43
  157.5 1.7 pair.6
  159.3 8.5 %collective-permute-done.41.refs_1_ = bf16[512,512]{1,0:T(8,128)(2,1)S(1)} collective-permute-done((bf16[512,512]{1,0:T(8,128)(2,1)S(1)}, bf16[512,512]{1,0:T(8,128)(2,1)S(1)}, u32[]{:S(2)}, u32[]{:S(2)}) %collective-permute-start.41) | collective-permute-done | bytes 524320 | tf_op jit(solution)/shard_map/ppermute | solution.py:807
  169.5 1.5 collective-permute-start.50
  172.9 1.8 collective-permute-start.49
  175.3 14.0 %attend_back.1 = (bf16[1024,384]{1,0:T(8,128)(2,1)}, f32[512,1024]{1,0:T(8,128)}, bf16[512,1024]{1,0:T(8,128)(2,1)S(1)}, f32[1,384]{1,0:T(1,128)}, bf16[1024,1024]{1,0:T(8,128)(2,1)}) custom-call(s32[2]{0:T(128)S(1)} %copy-done.3, s32[4]{0:T(128)S(1)} %copy-done.4, bf16[128,1024]{1,0:T(8,128)(2,1)S(1)} %get-tuple-element.232.refs_2_, ...), custom_call_target="tpu_custom_call" | custom-call | flops 17250000896 | bytes 9971200 | tf_op jit(solution)/shard_map/attend_back/pallas_call | solution.py:82
  190.6 4.1 %collective-permute-done.49.refs_3_ = bf16[128,1024]{1,0:T(8,128)(2,1)S(1)} collective-permute-done((bf16[128,1024]{1,0:T(8,128)(2,1)S(1)}, bf16[128,1024]{1,0:T(8,128)(2,1)S(1)}, u32[]{:S(2)}, u32[]{:S(2)}) %collective-permute-start.49) | collective-permute-done | bytes 262176 | tf_op jit(solution)/shard_map/ppermute | solution.py:773
  194.6 5.4 %collective-permute-done.51.refs_2_ = bf16[512,512]{1,0:T(8,128)(2,1)S(1)} collective-permute-done((bf16[512,512]{1,0:T(8,128)(2,1)S(1)}, bf16[512,512]{1,0:T(8,128)(2,1)S(1)}, u32[]{:S(2)}, u32[]{:S(2)}) %collective-permute-start.51) | collective-permute-done | bytes 524320 | tf_op jit(solution)/shard_map/ppermute | solution.py:807
  200.0 5.5 %attn_grads.1 = (bf16[16,40,384]{2,1,0:T(8,128)(2,1)S(1)}, bf16[16,40,384]{2,1,0:T(8,128)(2,1)S(1)}) custom-call(bf16[1024,384]{1,0:T(8,128)(2,1)} %get-tuple-element.244.refs_0_, bf16[1024,1024]{1,0:T(8,128)(2,1)} %get-tuple-element.245.refs_1_, bf16[1024,384]{1,0:T(8,128)(2,1)} %get-tuple-element.243.refs_13_.refs_2_, ...), custom_call_target="tpu_custom_call" | custom-call | flops 6899999744 | bytes 5789696 | tf_op jit(solution)/shard_map/attn_grads/pallas_call | solution.py:82
  206.3 1.5 collective-permute-start.53
  207.8 1.7 pair.7
  209.5 2.4 ffn_sum.1
  211.9 3.4 %all-to-all-start.2 = ((bf16[8,32,512]{2,1,0:T(8,128)(2,1)}), bf16[8,32,512]{2,1,0:T(8,128)(2,1)S(1)}, u32[]{:S(2)}, u32[]{:S(2)}) async-start(bf16[8,32,512]{2,1,0:T(8,128)(2,1)} %get-tuple-element.262), calls=%async_computation.2 | async-start | bytes 524288 | tf_op jit(solution)/shard_map/all_to_all | solution.py:811
  215.4 2.6 out_grads.1
  218.6 1.9 collective-permute-start.55
  220.5 1.5 collective-permute-start.56
  223.1 1.6 fold.4
  224.7 4.2 %all-to-all-start.3 = ((bf16[16,40,384]{2,1,0:T(8,128)(2,1)}), bf16[16,40,384]{2,1,0:T(8,128)(2,1)S(1)}, u32[]{:S(2)}, u32[]{:S(2)}) async-start(bf16[16,40,384]{2,1,0:T(8,128)(2,1)} %fold.4), calls=%async_computation.3 | async-start | bytes 983040 | tf_op jit(solution)/shard_map/all_to_all | solution.py:1112
  229.8 6.3 %collective-permute-done.57.refs_3_ = bf16[128,1024]{1,0:T(8,128)(2,1)} collective-permute-done((bf16[128,1024]{1,0:T(8,128)(2,1)S(1)}, bf16[128,1024]{1,0:T(8,128)(2,1)}, u32[]{:S(2)}, u32[]{:S(2)}) %collective-permute-start.57) | collective-permute-done | bytes 262176 | tf_op jit(solution)/shard_map/ppermute | solution.py:773
  236.1 2.3 last.1
  238.5 1.7 out.1
  240.2 3.0 %collective-permute-start.60 = (bf16[64,1024]{1,0:T(8,128)(2,1)S(1)}, bf16[64,1024]{1,0:T(8,128)(2,1)S(1)}, u32[]{:S(2)}, u32[]{:S(2)}) collective-permute-start(bf16[64,1024]{1,0:T(8,128)(2,1)S(1)} %get-tuple-element.280), channel_id=1, source_target_pairs={{0,8},{1,9},{2,10},{3,11},{4,12},{5,13},{6,14},{7,15},{8,0},{9,1},... | collective-permute-start | bytes 393224 | tf_op jit(solution)/shard_map/ppermute | solution.py:773
  243.1 12.1 %collective-permute-done.58.refs_6_ = bf16[96,1024]{1,0:T(8,128)(2,1)S(1)} collective-permute-done((bf16[96,1024]{1,0:T(8,128)(2,1)S(1)}, bf16[96,1024]{1,0:T(8,128)(2,1)S(1)}, u32[]{:S(2)}, u32[]{:S(2)}) %collective-permute-start.58) | collective-permute-done | bytes 196640 | tf_op jit(solution)/shard_map/ppermute | solution.py:773
  255.9 2.1 collective-permute-done.60.refs_4_
  258.0 1.8 unpack.1
  (121 shorter events, 23.6 us)
Async XLA Ops:
  3.8 21.7 %all-to-all-start = ((bf16[16,40,384]{2,1,0:T(8,128)(2,1)}), bf16[16,40,384]{2,1,0:T(8,128)(2,1)S(1)}, u32[]{:S(2)}, u32[]{:S(2)}) async-start(bf16[16,40,384]{2,1,0:T(8,128)(2,1)} %pack.1), calls=%async_computation | async-start | bytes 983040 | tf_op jit(solution)/shard_map/all_to_all | solution.py:875
  11.2 21.6 %collective-permute-start.1 = (bf16[64,1024]{1,0:T(8,128)(2,1)S(1)}, bf16[64,1024]{1,0:T(8,128)(2,1)S(1)}, u32[]{:S(2)}, u32[]{:S(2)}) collective-permute-start(bf16[64,1024]{1,0:T(8,128)(2,1)S(1)} %get-tuple-element.158), channel_id=1, source_target_pairs={{0,8},{1,9},{2,10},{3,11},{4,12},{5,13},{6,14},{7,15},{8,0},{9,1},... | collective-permute-start | bytes 393224 | tf_op jit(solution)/shard_map/ppermute | solution.py:773
  14.0 21.8 %collective-permute-start.4 = (bf16[32,1024]{1,0:T(8,128)(2,1)S(1)}, bf16[32,1024]{1,0:T(8,128)(2,1)S(1)}, u32[]{:S(2)}, u32[]{:S(2)}) collective-permute-start(bf16[32,1024]{1,0:T(8,128)(2,1)S(1)} %copy-done.11), channel_id=1, source_target_pairs={{0,16},{1,24},{2,0},{3,8},{4,17},{5,25},{6,1},{7,9},{8,18},{9,26},... | collective-permute-start | bytes 196616 | tf_op jit(solution)/shard_map/ppermute | solution.py:844
  15.5 26.0 %collective-permute-start.3 = (bf16[32,1024]{1,0:T(8,128)(2,1)S(1)}, bf16[32,1024]{1,0:T(8,128)(2,1)S(1)}, u32[]{:S(2)}, u32[]{:S(2)}) collective-permute-start(bf16[32,1024]{1,0:T(8,128)(2,1)S(1)} %copy-done.11), channel_id=1, source_target_pairs={{0,0},{1,8},{2,16},{3,24},{4,1},{5,9},{6,17},{7,25},{8,2},{9,10},{... | collective-permute-start | bytes 196616 | tf_op jit(solution)/shard_map/ppermute | solution.py:844
  25.4 28.8 %collective-permute-start.2 = (bf16[16,40,384]{2,1,0:T(8,128)(2,1)S(1)}, bf16[16,40,384]{2,1,0:T(8,128)(2,1)S(1)}, u32[]{:S(2)}, u32[]{:S(2)}) collective-permute-start(bf16[16,40,384]{2,1,0:T(8,128)(2,1)S(1)} %all-to-all-done.refs_10_), channel_id=1, source_target_pairs={{0,16},{16,0},{1,17},{17,1},{2,18},{18,2},{3,19},{19,3},{4,20},{20... | collective-permute-start | bytes 1474568 | tf_op jit(solution)/shard_map/ppermute | solution.py:834
  32.8 21.4 %collective-permute-start.11 = (bf16[128,1024]{1,0:T(8,128)(2,1)S(1)}, bf16[128,1024]{1,0:T(8,128)(2,1)S(1)}, u32[]{:S(2)}, u32[]{:S(2)}) collective-permute-start(bf16[128,1024]{1,0:T(8,128)(2,1)S(1)} %constant_dynamic-update-slice_fusion.2.refs_2_.refs_4_), channel_id=1, source_target_pairs={{0,6},{1,7},{2,4},{3,5},{4,2},{5,3},{6,0},{7,1},{8,14},{9,15},{10,... | collective-permute-start | bytes 786440 | tf_op jit(solution)/shard_map/ppermute | solution.py:773
  32.9 21.4 %collective-permute-start.9 = (bf16[128,1024]{1,0:T(8,128)(2,1)S(1)}, bf16[128,1024]{1,0:T(8,128)(2,1)S(1)}, u32[]{:S(2)}, u32[]{:S(2)}) collective-permute-start(bf16[128,1024]{1,0:T(8,128)(2,1)S(1)} %constant_dynamic-update-slice_fusion.2.refs_2_.refs_4_), channel_id=1, source_target_pairs={{0,4},{1,5},{2,6},{3,7},{4,0},{5,1},{6,2},{7,3},{8,12},{9,13},{10,... | collective-permute-start | bytes 786440 | tf_op jit(solution)/shard_map/ppermute | solution.py:773
  35.8 18.4 %collective-permute-start.7 = (bf16[128,1024]{1,0:T(8,128)(2,1)S(1)}, bf16[128,1024]{1,0:T(8,128)(2,1)S(1)}, u32[]{:S(2)}, u32[]{:S(2)}) collective-permute-start(bf16[128,1024]{1,0:T(8,128)(2,1)S(1)} %constant_dynamic-update-slice_fusion.2.refs_2_.refs_4_), channel_id=1, source_target_pairs={{0,2},{1,3},{2,0},{3,1},{4,6},{5,7},{6,4},{7,5},{8,10},{9,11},{10,... | collective-permute-start | bytes 786440 | tf_op jit(solution)/shard_map/ppermute | solution.py:773
  38.1 22.0 %all-to-all-start.1 = ((bf16[8,32,512]{2,1,0:T(8,128)(2,1)}), bf16[8,32,512]{2,1,0:T(8,128)(2,1)S(1)}, u32[]{:S(2)}, u32[]{:S(2)}) async-start(bf16[8,32,512]{2,1,0:T(8,128)(2,1)} %pack_up.1), calls=%async_computation.1 | async-start | bytes 524288 | tf_op jit(solution)/shard_map/all_to_all | solution.py:811
  41.5 8.6 %collective-permute-start.5 = (bf16[2,32,1024]{2,1,0:T(8,128)(2,1)S(1)}, bf16[2,32,1024]{2,1,0:T(8,128)(2,1)S(1)}, u32[]{:S(2)}, u32[]{:S(2)}) collective-permute-start(bf16[2,32,1024]{2,1,0:T(8,128)(2,1)S(1)} %pad_maximum_fusion.refs_12_), channel_id=1, source_target_pairs={{0,8},{1,9},{2,10},{3,11},{4,12},{5,13},{6,14},{7,15},{8,0},{9,1},... | collective-permute-start | bytes 393224 | tf_op jit(solution)/shard_map/ppermute | solution.py:773
  50.8 9.2 %collective-permute-start = (bf16[64,1024]{1,0:T(8,128)(2,1)S(1)}, bf16[64,1024]{1,0:T(8,128)(2,1)S(1)}, u32[]{:S(2)}, u32[]{:S(2)}) collective-permute-start(bf16[64,1024]{1,0:T(8,128)(2,1)S(1)} %get-tuple-element.163), channel_id=1, source_target_pairs={{0,8},{1,9},{2,10},{3,11},{4,12},{5,13},{6,14},{7,15},{8,0},{9,1},... | collective-permute-start | bytes 393224 | tf_op jit(solution)/shard_map/ppermute | solution.py:773
  54.2 6.1 %collective-permute-start.6 = (bf16[128,1024]{1,0:T(8,128)(2,1)S(1)}, bf16[128,1024]{1,0:T(8,128)(2,1)S(1)}, u32[]{:S(2)}, u32[]{:S(2)}) collective-permute-start(bf16[128,1024]{1,0:T(8,128)(2,1)S(1)} %constant_dynamic-update-slice_fusion.2.refs_2_.refs_4_), channel_id=1, source_target_pairs={{0,1},{1,0},{2,3},{3,2},{4,5},{5,4},{6,7},{7,6},{8,9},{9,8},{10,11... | collective-permute-start | bytes 786440 | tf_op jit(solution)/shard_map/ppermute | solution.py:773
  54.3 6.0 %collective-permute-start.8 = (bf16[128,1024]{1,0:T(8,128)(2,1)S(1)}, bf16[128,1024]{1,0:T(8,128)(2,1)}, u32[]{:S(2)}, u32[]{:S(2)}) collective-permute-start(bf16[128,1024]{1,0:T(8,128)(2,1)S(1)} %collective-permute-done.7.refs_4_), channel_id=1, source_target_pairs={{0,1},{1,0},{2,3},{3,2},{4,5},{5,4},{6,7},{7,6},{8,9},{9,8},{10,11... | collective-permute-start | bytes 786440 | tf_op jit(solution)/shard_map/ppermute | solution.py:773
  54.8 5.5 %collective-permute-start.10 = (bf16[128,1024]{1,0:T(8,128)(2,1)S(1)}, bf16[128,1024]{1,0:T(8,128)(2,1)}, u32[]{:S(2)}, u32[]{:S(2)}) collective-permute-start(bf16[128,1024]{1,0:T(8,128)(2,1)S(1)} %collective-permute-done.9.refs_6_), channel_id=1, source_target_pairs={{0,1},{1,0},{2,3},{3,2},{4,5},{5,4},{6,7},{7,6},{8,9},{9,8},{10,11... | collective-permute-start | bytes 786440 | tf_op jit(solution)/shard_map/ppermute | solution.py:773
  54.9 5.4 %collective-permute-start.12 = (bf16[128,1024]{1,0:T(8,128)(2,1)S(1)}, bf16[128,1024]{1,0:T(8,128)(2,1)}, u32[]{:S(2)}, u32[]{:S(2)}) collective-permute-start(bf16[128,1024]{1,0:T(8,128)(2,1)S(1)} %collective-permute-done.11.refs_8_), channel_id=1, source_target_pairs={{0,1},{1,0},{2,3},{3,2},{4,5},{5,4},{6,7},{7,6},{8,9},{9,8},{10,11... | collective-permute-start | bytes 786440 | tf_op jit(solution)/shard_map/ppermute | solution.py:773
  60.2 22.7 %collective-permute-start.13 = (bf16[512,512]{1,0:T(8,128)(2,1)S(1)}, bf16[512,512]{1,0:T(8,128)(2,1)S(1)}, u32[]{:S(2)}, u32[]{:S(2)}) collective-permute-start(bf16[512,512]{1,0:T(8,128)(2,1)S(1)} %join.1.refs_8_), channel_id=1, source_target_pairs={{0,8},{1,9},{2,10},{3,11},{4,12},{5,13},{6,14},{7,15},{8,0},{9,1},... | collective-permute-start | bytes 1572872 | tf_op jit(solution)/shard_map/ppermute | solution.py:807
  60.3 22.5 %collective-permute-start.17 = (bf16[128,1024]{1,0:T(8,128)(2,1)S(1)}, bf16[128,1024]{1,0:T(8,128)(2,1)S(1)}, u32[]{:S(2)}, u32[]{:S(2)}) collective-permute-start(bf16[128,1024]{1,0:T(8,128)(2,1)S(1)} %constant_dynamic-update-slice_fusion.refs_0_.refs_6_), channel_id=1, source_target_pairs={{0,6},{1,7},{2,4},{3,5},{4,2},{5,3},{6,0},{7,1},{8,14},{9,15},{10,... | collective-permute-start | bytes 786440 | tf_op jit(solution)/shard_map/ppermute | solution.py:773
  63.4 20.3 %collective-permute-start.16 = (bf16[128,1024]{1,0:T(8,128)(2,1)S(1)}, bf16[128,1024]{1,0:T(8,128)(2,1)S(1)}, u32[]{:S(2)}, u32[]{:S(2)}) collective-permute-start(bf16[128,1024]{1,0:T(8,128)(2,1)S(1)} %constant_dynamic-update-slice_fusion.refs_0_.refs_6_), channel_id=1, source_target_pairs={{0,4},{1,5},{2,6},{3,7},{4,0},{5,1},{6,2},{7,3},{8,12},{9,13},{10,... | collective-permute-start | bytes 786440 | tf_op jit(solution)/shard_map/ppermute | solution.py:773
  63.4 20.3 %collective-permute-start.15 = (bf16[128,1024]{1,0:T(8,128)(2,1)S(1)}, bf16[128,1024]{1,0:T(8,128)(2,1)S(1)}, u32[]{:S(2)}, u32[]{:S(2)}) collective-permute-start(bf16[128,1024]{1,0:T(8,128)(2,1)S(1)} %constant_dynamic-update-slice_fusion.refs_0_.refs_6_), channel_id=1, source_target_pairs={{0,2},{1,3},{2,0},{3,1},{4,6},{5,7},{6,4},{7,5},{8,10},{9,11},{10,... | collective-permute-start | bytes 786440 | tf_op jit(solution)/shard_map/ppermute | solution.py:773
  64.1 19.6 %collective-permute-start.14 = (bf16[512,512]{1,0:T(8,128)(2,1)S(1)}, bf16[512,512]{1,0:T(8,128)(2,1)S(1)}, u32[]{:S(2)}, u32[]{:S(2)}) collective-permute-start(bf16[512,512]{1,0:T(8,128)(2,1)S(1)} %join.1.refs_8_), channel_id=1, source_target_pairs={{0,16},{1,17},{2,18},{3,19},{4,20},{5,21},{6,22},{7,23},{8,24},{9,... | collective-permute-start | bytes 1572872 | tf_op jit(solution)/shard_map/ppermute | solution.py:807
  83.7 2.7 %collective-permute-start.18 = (bf16[512,1024]{1,0:T(8,128)(2,1)S(1)}, bf16[512,1024]{1,0:T(8,128)(2,1)S(1)}, u32[]{:S(2)}, u32[]{:S(2)}) collective-permute-start(bf16[512,1024]{1,0:T(8,128)(2,1)S(1)} %get-tuple-element.186), channel_id=1, source_target_pairs={{0,1},{1,0},{2,3},{3,2},{4,5},{5,4},{6,7},{7,6},{8,9},{9,8},{10,11... | collective-permute-start | bytes 3145736 | tf_op jit(solution)/shard_map/ppermute | solution.py:773
  88.1 8.4 %collective-permute-start.19 = (bf16[128,1024]{1,0:T(8,128)(2,1)S(1)}, bf16[128,1024]{1,0:T(8,128)(2,1)S(1)}, u32[]{:S(2)}, u32[]{:S(2)}) collective-permute-start(bf16[128,1024]{1,0:T(8,128)(2,1)S(1)} %get-tuple-element.188), channel_id=1, source_target_pairs={{0,2},{1,3},{2,0},{3,1},{4,6},{5,7},{6,4},{7,5},{8,10},{9,11},{10,... | collective-permute-start | bytes 786440 | tf_op jit(solution)/shard_map/ppermute | solution.py:773
  89.6 9.2 %collective-permute-start.20 = (bf16[128,1024]{1,0:T(8,128)(2,1)S(1)}, bf16[128,1024]{1,0:T(8,128)(2,1)S(1)}, u32[]{:S(2)}, u32[]{:S(2)}) collective-permute-start(bf16[128,1024]{1,0:T(8,128)(2,1)S(1)} %get-tuple-element.189), channel_id=1, source_target_pairs={{0,4},{1,5},{2,6},{3,7},{4,0},{5,1},{6,2},{7,3},{8,12},{9,13},{10,... | collective-permute-start | bytes 786440 | tf_op jit(solution)/shard_map/ppermute | solution.py:773
  89.6 13.7 %collective-permute-start.21 = (bf16[128,1024]{1,0:T(8,128)(2,1)S(1)}, bf16[128,1024]{1,0:T(8,128)(2,1)S(1)}, u32[]{:S(2)}, u32[]{:S(2)}) collective-permute-start(bf16[128,1024]{1,0:T(8,128)(2,1)S(1)} %get-tuple-element.190), channel_id=1, source_target_pairs={{0,6},{1,7},{2,4},{3,5},{4,2},{5,3},{6,0},{7,1},{8,14},{9,15},{10,... | collective-permute-start | bytes 786440 | tf_op jit(solution)/shard_map/ppermute | solution.py:773
  91.6 17.3 %collective-permute-start.28 = (bf16[512,512]{1,0:T(8,128)(2,1)S(1)}, bf16[512,512]{1,0:T(8,128)(2,1)S(1)}, u32[]{:S(2)}, u32[]{:S(2)}) collective-permute-start(bf16[512,512]{1,0:T(8,128)(2,1)S(1)} %collective-permute-done.13.refs_9_), channel_id=1, source_target_pairs={{0,16},{1,17},{2,18},{3,19},{4,20},{5,21},{6,22},{7,23},{8,24},{9,... | collective-permute-start | bytes 1572872 | tf_op jit(solution)/shard_map/ppermute | solution.py:807
  92.2 13.2 %collective-permute-start.24 = (bf16[128,1024]{1,0:T(8,128)(2,1)S(1)}, bf16[128,1024]{1,0:T(8,128)(2,1)S(1)}, u32[]{:S(2)}, u32[]{:S(2)}) collective-permute-start(bf16[128,1024]{1,0:T(8,128)(2,1)S(1)} %constant_dynamic-update-slice_fusion.refs_0_.refs_6_), channel_id=1, source_target_pairs={{0,1},{1,0},{2,3},{3,2},{4,5},{5,4},{6,7},{7,6},{8,9},{9,8},{10,11... | collective-permute-start | bytes 786440 | tf_op jit(solution)/shard_map/ppermute | solution.py:773
  96.5 10.2 %collective-permute-start.25 = (bf16[128,1024]{1,0:T(8,128)(2,1)S(1)}, bf16[128,1024]{1,0:T(8,128)(2,1)S(1)}, u32[]{:S(2)}, u32[]{:S(2)}) collective-permute-start(bf16[128,1024]{1,0:T(8,128)(2,1)S(1)} %collective-permute-done.15.refs_2_), channel_id=1, source_target_pairs={{0,1},{1,0},{2,3},{3,2},{4,5},{5,4},{6,7},{7,6},{8,9},{9,8},{10,11... | collective-permute-start | bytes 786440 | tf_op jit(solution)/shard_map/ppermute | solution.py:773
  98.8 9.6 %collective-permute-start.26 = (bf16[128,1024]{1,0:T(8,128)(2,1)S(1)}, bf16[128,1024]{1,0:T(8,128)(2,1)S(1)}, u32[]{:S(2)}, u32[]{:S(2)}) collective-permute-start(bf16[128,1024]{1,0:T(8,128)(2,1)S(1)} %collective-permute-done.16.refs_4_), channel_id=1, source_target_pairs={{0,1},{1,0},{2,3},{3,2},{4,5},{5,4},{6,7},{7,6},{8,9},{9,8},{10,11... | collective-permute-start | bytes 786440 | tf_op jit(solution)/shard_map/ppermute | solution.py:773
  103.3 5.7 %collective-permute-start.27 = (bf16[128,1024]{1,0:T(8,128)(2,1)S(1)}, bf16[128,1024]{1,0:T(8,128)(2,1)S(1)}, u32[]{:S(2)}, u32[]{:S(2)}) collective-permute-start(bf16[128,1024]{1,0:T(8,128)(2,1)S(1)} %collective-permute-done.17.refs_6_), channel_id=1, source_target_pairs={{0,1},{1,0},{2,3},{3,2},{4,5},{5,4},{6,7},{7,6},{8,9},{9,8},{10,11... | collective-permute-start | bytes 786440 | tf_op jit(solution)/shard_map/ppermute | solution.py:773
  105.4 10.1 %collective-permute-start.32 = (bf16[128,1024]{1,0:T(8,128)(2,1)S(1)}, bf16[128,1024]{1,0:T(8,128)(2,1)S(1)}, u32[]{:S(2)}, u32[]{:S(2)}) collective-permute-start(bf16[128,1024]{1,0:T(8,128)(2,1)S(1)} %get-tuple-element.192.refs_0_), channel_id=1, source_target_pairs={{0,6},{1,7},{2,4},{3,5},{4,2},{5,3},{6,0},{7,1},{8,14},{9,15},{10,... | collective-permute-start | bytes 786440 | tf_op jit(solution)/shard_map/ppermute | solution.py:773
  106.7 14.1 %collective-permute-start.30 = (bf16[128,1024]{1,0:T(8,128)(2,1)S(1)}, bf16[128,1024]{1,0:T(8,128)(2,1)S(1)}, u32[]{:S(2)}, u32[]{:S(2)}) collective-permute-start(bf16[128,1024]{1,0:T(8,128)(2,1)S(1)} %get-tuple-element.192.refs_0_), channel_id=1, source_target_pairs={{0,4},{1,5},{2,6},{3,7},{4,0},{5,1},{6,2},{7,3},{8,12},{9,13},{10,... | collective-permute-start | bytes 786440 | tf_op jit(solution)/shard_map/ppermute | solution.py:773
  108.4 12.3 %collective-permute-start.23 = (bf16[128,1024]{1,0:T(8,128)(2,1)S(1)}, bf16[128,1024]{1,0:T(8,128)(2,1)S(1)}, u32[]{:S(2)}, u32[]{:S(2)}) collective-permute-start(bf16[128,1024]{1,0:T(8,128)(2,1)S(1)} %get-tuple-element.192.refs_0_), channel_id=1, source_target_pairs={{0,2},{1,3},{2,0},{3,1},{4,6},{5,7},{6,4},{7,5},{8,10},{9,11},{10,... | collective-permute-start | bytes 786440 | tf_op jit(solution)/shard_map/ppermute | solution.py:773
  109.0 12.3 %collective-permute-start.22 = (bf16[128,1024]{1,0:T(8,128)(2,1)S(1)}, bf16[128,1024]{1,0:T(8,128)(2,1)S(1)}, u32[]{:S(2)}, u32[]{:S(2)}) collective-permute-start(bf16[128,1024]{1,0:T(8,128)(2,1)S(1)} %get-tuple-element.192.refs_0_), channel_id=1, source_target_pairs={{0,1},{1,0},{2,3},{3,2},{4,5},{5,4},{6,7},{7,6},{8,9},{9,8},{10,11... | collective-permute-start | bytes 786440 | tf_op jit(solution)/shard_map/ppermute | solution.py:773
  120.8 1.9 collective-permute-start.31
  121.3 1.8 collective-permute-start.33
  131.1 2.7 %collective-permute-start.34 = (bf16[512,1024]{1,0:T(8,128)(2,1)S(1)}, bf16[512,1024]{1,0:T(8,128)(2,1)S(1)}, u32[]{:S(2)}, u32[]{:S(2)}) collective-permute-start(bf16[512,1024]{1,0:T(8,128)(2,1)S(1)} %get-tuple-element.205), channel_id=1, source_target_pairs={{0,1},{1,0},{2,3},{3,2},{4,5},{5,4},{6,7},{7,6},{8,9},{9,8},{10,11... | collective-permute-start | bytes 3145736 | tf_op jit(solution)/shard_map/ppermute | solution.py:773
  135.6 13.8 %collective-permute-start.35 = (bf16[128,1024]{1,0:T(8,128)(2,1)S(1)}, bf16[128,1024]{1,0:T(8,128)(2,1)S(1)}, u32[]{:S(2)}, u32[]{:S(2)}) collective-permute-start(bf16[128,1024]{1,0:T(8,128)(2,1)S(1)} %get-tuple-element.211), channel_id=1, source_target_pairs={{0,2},{1,3},{2,0},{3,1},{4,6},{5,7},{6,4},{7,5},{8,10},{9,11},{10,... | collective-permute-start | bytes 786440 | tf_op jit(solution)/shard_map/ppermute | solution.py:773
  137.0 12.3 %collective-permute-start.36 = (bf16[128,1024]{1,0:T(8,128)(2,1)S(1)}, bf16[128,1024]{1,0:T(8,128)(2,1)S(1)}, u32[]{:S(2)}, u32[]{:S(2)}) collective-permute-start(bf16[128,1024]{1,0:T(8,128)(2,1)S(1)} %get-tuple-element.212), channel_id=1, source_target_pairs={{0,4},{1,5},{2,6},{3,7},{4,0},{5,1},{6,2},{7,3},{8,12},{9,13},{10,... | collective-permute-start | bytes 786440 | tf_op jit(solution)/shard_map/ppermute | solution.py:773
  137.3 13.4 %collective-permute-start.37 = (bf16[128,1024]{1,0:T(8,128)(2,1)S(1)}, bf16[128,1024]{1,0:T(8,128)(2,1)S(1)}, u32[]{:S(2)}, u32[]{:S(2)}) collective-permute-start(bf16[128,1024]{1,0:T(8,128)(2,1)S(1)} %get-tuple-element.213), channel_id=1, source_target_pairs={{0,6},{1,7},{2,4},{3,5},{4,2},{5,3},{6,0},{7,1},{8,14},{9,15},{10,... | collective-permute-start | bytes 786440 | tf_op jit(solution)/shard_map/ppermute | solution.py:773
  153.3 4.2 %collective-permute-start.38 = (bf16[512,1024]{1,0:T(8,128)(2,1)S(1)}, bf16[512,1024]{1,0:T(8,128)(2,1)S(1)}, u32[]{:S(2)}, u32[]{:S(2)}) collective-permute-start(bf16[512,1024]{1,0:T(8,128)(2,1)S(1)} %get-tuple-element.221), channel_id=1, source_target_pairs={{0,1},{1,0},{2,3},{3,2},{4,5},{5,4},{6,7},{7,6},{8,9},{9,8},{10,11... | collective-permute-start | bytes 3145736 | tf_op jit(solution)/shard_map/ppermute | solution.py:773
  153.4 14.3 %collective-permute-start.41 = (bf16[512,512]{1,0:T(8,128)(2,1)S(1)}, bf16[512,512]{1,0:T(8,128)(2,1)S(1)}, u32[]{:S(2)}, u32[]{:S(2)}) collective-permute-start(bf16[512,512]{1,0:T(8,128)(2,1)S(1)} %get-tuple-element.228), channel_id=1, source_target_pairs={{0,16},{1,17},{2,18},{3,19},{4,20},{5,21},{6,22},{7,23},{8,24},{9,... | collective-permute-start | bytes 1572872 | tf_op jit(solution)/shard_map/ppermute | solution.py:807
  154.0 14.0 %collective-permute-start.45 = (bf16[128,1024]{1,0:T(8,128)(2,1)S(1)}, bf16[128,1024]{1,0:T(8,128)(2,1)S(1)}, u32[]{:S(2)}, u32[]{:S(2)}) collective-permute-start(bf16[128,1024]{1,0:T(8,128)(2,1)S(1)} %get-tuple-element.232.refs_2_), channel_id=1, source_target_pairs={{0,6},{1,7},{2,4},{3,5},{4,2},{5,3},{6,0},{7,1},{8,14},{9,15},{10,... | collective-permute-start | bytes 786440 | tf_op jit(solution)/shard_map/ppermute | solution.py:773
  155.2 13.5 %collective-permute-start.43 = (bf16[128,1024]{1,0:T(8,128)(2,1)S(1)}, bf16[128,1024]{1,0:T(8,128)(2,1)S(1)}, u32[]{:S(2)}, u32[]{:S(2)}) collective-permute-start(bf16[128,1024]{1,0:T(8,128)(2,1)S(1)} %get-tuple-element.232.refs_2_), channel_id=1, source_target_pairs={{0,4},{1,5},{2,6},{3,7},{4,0},{5,1},{6,2},{7,3},{8,12},{9,13},{10,... | collective-permute-start | bytes 786440 | tf_op jit(solution)/shard_map/ppermute | solution.py:773
  156.4 12.5 %collective-permute-start.40 = (bf16[128,1024]{1,0:T(8,128)(2,1)S(1)}, bf16[128,1024]{1,0:T(8,128)(2,1)S(1)}, u32[]{:S(2)}, u32[]{:S(2)}) collective-permute-start(bf16[128,1024]{1,0:T(8,128)(2,1)S(1)} %get-tuple-element.232.refs_2_), channel_id=1, source_target_pairs={{0,2},{1,3},{2,0},{3,1},{4,6},{5,7},{6,4},{7,5},{8,10},{9,11},{10,... | collective-permute-start | bytes 786440 | tf_op jit(solution)/shard_map/ppermute | solution.py:773
  157.5 13.4 %collective-permute-start.39 = (bf16[128,1024]{1,0:T(8,128)(2,1)S(1)}, bf16[128,1024]{1,0:T(8,128)(2,1)S(1)}, u32[]{:S(2)}, u32[]{:S(2)}) collective-permute-start(bf16[128,1024]{1,0:T(8,128)(2,1)S(1)} %get-tuple-element.232.refs_2_), channel_id=1, source_target_pairs={{0,1},{1,0},{2,3},{3,2},{4,5},{5,4},{6,7},{7,6},{8,9},{9,8},{10,11... | collective-permute-start | bytes 786440 | tf_op jit(solution)/shard_map/ppermute | solution.py:773
  168.9 2.0 collective-permute-start.42
  169.0 2.0 collective-permute-start.44
  169.4 1.8 collective-permute-start.46
  169.5 19.8 %collective-permute-start.50 = (bf16[512,512]{1,0:T(8,128)(2,1)S(1)}, bf16[512,512]{1,0:T(8,128)(2,1)S(1)}, u32[]{:S(2)}, u32[]{:S(2)}) collective-permute-start(bf16[512,512]{1,0:T(8,128)(2,1)S(1)} %get-tuple-element.257), channel_id=1, source_target_pairs={{0,16},{1,17},{2,18},{3,19},{4,20},{5,21},{6,22},{7,23},{8,24},{9,... | collective-permute-start | bytes 1572872 | tf_op jit(solution)/shard_map/ppermute | solution.py:807
  171.2 18.1 %collective-permute-start.47 = (bf16[128,1024]{1,0:T(8,128)(2,1)S(1)}, bf16[128,1024]{1,0:T(8,128)(2,1)S(1)}, u32[]{:S(2)}, u32[]{:S(2)}) collective-permute-start(bf16[128,1024]{1,0:T(8,128)(2,1)S(1)} %get-tuple-element.254), channel_id=1, source_target_pairs={{0,2},{1,3},{2,0},{3,1},{4,6},{5,7},{6,4},{7,5},{8,10},{9,11},{10,... | collective-permute-start | bytes 786440 | tf_op jit(solution)/shard_map/ppermute | solution.py:773
  172.4 18.1 %collective-permute-start.48 = (bf16[128,1024]{1,0:T(8,128)(2,1)S(1)}, bf16[128,1024]{1,0:T(8,128)(2,1)S(1)}, u32[]{:S(2)}, u32[]{:S(2)}) collective-permute-start(bf16[128,1024]{1,0:T(8,128)(2,1)S(1)} %get-tuple-element.255), channel_id=1, source_target_pairs={{0,4},{1,5},{2,6},{3,7},{4,0},{5,1},{6,2},{7,3},{8,12},{9,13},{10,... | collective-permute-start | bytes 786440 | tf_op jit(solution)/shard_map/ppermute | solution.py:773
  172.9 21.7 %collective-permute-start.49 = (bf16[128,1024]{1,0:T(8,128)(2,1)S(1)}, bf16[128,1024]{1,0:T(8,128)(2,1)S(1)}, u32[]{:S(2)}, u32[]{:S(2)}) collective-permute-start(bf16[128,1024]{1,0:T(8,128)(2,1)S(1)} %get-tuple-element.256), channel_id=1, source_target_pairs={{0,6},{1,7},{2,4},{3,5},{4,2},{5,3},{6,0},{7,1},{8,14},{9,15},{10,... | collective-permute-start | bytes 786440 | tf_op jit(solution)/shard_map/ppermute | solution.py:773
  174.7 25.3 %collective-permute-start.51 = (bf16[512,512]{1,0:T(8,128)(2,1)S(1)}, bf16[512,512]{1,0:T(8,128)(2,1)S(1)}, u32[]{:S(2)}, u32[]{:S(2)}) collective-permute-start(bf16[512,512]{1,0:T(8,128)(2,1)S(1)} %fold.3), channel_id=1, source_target_pairs={{0,8},{1,9},{2,10},{3,11},{4,12},{5,13},{6,14},{7,15},{8,0},{9,1},... | collective-permute-start | bytes 1572872 | tf_op jit(solution)/shard_map/ppermute | solution.py:807
  200.0 7.8 %collective-permute-start.52 = (bf16[512,1024]{1,0:T(8,128)(2,1)S(1)}, bf16[512,1024]{1,0:T(8,128)(2,1)S(1)}, u32[]{:S(2)}, u32[]{:S(2)}) collective-permute-start(bf16[512,1024]{1,0:T(8,128)(2,1)S(1)} %get-tuple-element.259), channel_id=1, source_target_pairs={{0,1},{1,0},{2,3},{3,2},{4,5},{5,4},{6,7},{7,6},{8,9},{9,8},{10,11... | collective-permute-start | bytes 3145736 | tf_op jit(solution)/shard_map/ppermute | solution.py:773
  206.3 15.8 %collective-permute-start.53 = (bf16[16,40,384]{2,1,0:T(8,128)(2,1)S(1)}, bf16[16,40,384]{2,1,0:T(8,128)(2,1)S(1)}, u32[]{:S(2)}, u32[]{:S(2)}) collective-permute-start(bf16[16,40,384]{2,1,0:T(8,128)(2,1)S(1)} %get-tuple-element.264), channel_id=1, source_target_pairs={{0,16},{16,0},{1,17},{17,1},{2,18},{18,2},{3,19},{19,3},{4,20},{20... | collective-permute-start | bytes 1474568 | tf_op jit(solution)/shard_map/ppermute | solution.py:834
  211.9 10.1 %all-to-all-start.2 = ((bf16[8,32,512]{2,1,0:T(8,128)(2,1)}), bf16[8,32,512]{2,1,0:T(8,128)(2,1)S(1)}, u32[]{:S(2)}, u32[]{:S(2)}) async-start(bf16[8,32,512]{2,1,0:T(8,128)(2,1)} %get-tuple-element.262), calls=%async_computation.2 | async-start | bytes 524288 | tf_op jit(solution)/shard_map/all_to_all | solution.py:811
  217.9 11.0 %collective-permute-start.54 = (bf16[2,32,1024]{2,1,0:T(8,128)(2,1)S(1)}, bf16[2,32,1024]{2,1,0:T(8,128)(2,1)S(1)}, u32[]{:S(2)}, u32[]{:S(2)}) collective-permute-start(bf16[2,32,1024]{2,1,0:T(8,128)(2,1)S(1)} %get-tuple-element.270), channel_id=1, source_target_pairs={{0,16},{16,0},{1,17},{17,1},{2,18},{18,2},{3,19},{19,3},{4,20},{20... | collective-permute-start | bytes 393224 | tf_op jit(solution)/shard_map/ppermute | solution.py:834
  218.6 11.0 %collective-permute-start.55 = (bf16[128,1024]{1,0:T(8,128)(2,1)S(1)}, bf16[128,1024]{1,0:T(8,128)(2,1)}, u32[]{:S(2)}, u32[]{:S(2)}) collective-permute-start(bf16[128,1024]{1,0:T(8,128)(2,1)S(1)} %get-tuple-element.271), channel_id=1, source_target_pairs={{0,2},{1,3},{2,0},{3,1},{4,6},{5,7},{6,4},{7,5},{8,10},{9,11},{10,... | collective-permute-start | bytes 786440 | tf_op jit(solution)/shard_map/ppermute | solution.py:773
  220.5 9.3 %collective-permute-start.56 = (bf16[128,1024]{1,0:T(8,128)(2,1)S(1)}, bf16[128,1024]{1,0:T(8,128)(2,1)}, u32[]{:S(2)}, u32[]{:S(2)}) collective-permute-start(bf16[128,1024]{1,0:T(8,128)(2,1)S(1)} %get-tuple-element.272), channel_id=1, source_target_pairs={{0,4},{1,5},{2,6},{3,7},{4,0},{5,1},{6,2},{7,3},{8,12},{9,13},{10,... | collective-permute-start | bytes 786440 | tf_op jit(solution)/shard_map/ppermute | solution.py:773
  222.0 14.1 %collective-permute-start.57 = (bf16[128,1024]{1,0:T(8,128)(2,1)S(1)}, bf16[128,1024]{1,0:T(8,128)(2,1)}, u32[]{:S(2)}, u32[]{:S(2)}) collective-permute-start(bf16[128,1024]{1,0:T(8,128)(2,1)S(1)} %get-tuple-element.273), channel_id=1, source_target_pairs={{0,6},{1,7},{2,4},{3,5},{4,2},{5,3},{6,0},{7,1},{8,14},{9,15},{10,... | collective-permute-start | bytes 786440 | tf_op jit(solution)/shard_map/ppermute | solution.py:773
  224.7 33.3 %all-to-all-start.3 = ((bf16[16,40,384]{2,1,0:T(8,128)(2,1)}), bf16[16,40,384]{2,1,0:T(8,128)(2,1)S(1)}, u32[]{:S(2)}, u32[]{:S(2)}) async-start(bf16[16,40,384]{2,1,0:T(8,128)(2,1)} %fold.4), calls=%async_computation.3 | async-start | bytes 983040 | tf_op jit(solution)/shard_map/all_to_all | solution.py:1112
  238.4 16.8 %collective-permute-start.58 = (bf16[96,1024]{1,0:T(8,128)(2,1)S(1)}, bf16[96,1024]{1,0:T(8,128)(2,1)S(1)}, u32[]{:S(2)}, u32[]{:S(2)}) collective-permute-start(bf16[96,1024]{1,0:T(8,128)(2,1)S(1)} %get-tuple-element.276), channel_id=1, source_target_pairs={{0,8},{1,9},{2,10},{3,11},{4,12},{5,13},{6,14},{7,15},{8,0},{9,1},... | collective-permute-start | bytes 589832 | tf_op jit(solution)/shard_map/ppermute | solution.py:773
  240.2 17.9 %collective-permute-start.60 = (bf16[64,1024]{1,0:T(8,128)(2,1)S(1)}, bf16[64,1024]{1,0:T(8,128)(2,1)S(1)}, u32[]{:S(2)}, u32[]{:S(2)}) collective-permute-start(bf16[64,1024]{1,0:T(8,128)(2,1)S(1)} %get-tuple-element.280), channel_id=1, source_target_pairs={{0,8},{1,9},{2,10},{3,11},{4,12},{5,13},{6,14},{7,15},{8,0},{9,1},... | collective-permute-start | bytes 393224 | tf_op jit(solution)/shard_map/ppermute | solution.py:773
  255.2 2.8 %collective-permute-start.59 = (bf16[32,1024]{1,0:T(8,128)(2,1)S(1)}, bf16[32,1024]{1,0:T(8,128)(2,1)S(1)}, u32[]{:S(2)}, u32[]{:S(2)}) collective-permute-start(bf16[32,1024]{1,0:T(8,128)(2,1)S(1)} %fusion), channel_id=1, source_target_pairs={{0,0},{8,1},{16,2},{24,3},{1,4},{9,5},{17,6},{25,7},{2,8},{10,9},{... | collective-permute-start | bytes 196616 | tf_op jit(solution)/shard_map/ppermute | solution.py:1141
  (13 other events, 87.2 us)
where the time goes:
time: 265 us; the launch traced here: 260 us
  waiting for transfers between devices  101 us (38%)
  Pallas kernels  84.4 us (32%)
  starting transfers between devices  71 us (27%)
    pallas_call x25, Pallas kernels, call(): pl.pallas_call(body, out_shape=tuple((o.array if isinstance(o, Near) else...  84.4 us
    ppermute x49, waiting for transfers between devices, xor(): return lax.ppermute(value, 'seq', [(i, i ^ bit) for i in range(seq_size)])  73.3 us
    ppermute x49, starting transfers between devices, xor(): return lax.ppermute(value, 'seq', [(i, i ^ bit) for i in range(seq_size)])  41.3 us
    ppermute x6, waiting for transfers between devices, to_group(): return lax.ppermute(value, both, pairs)  18.1 us
    all_to_all x1, waiting for transfers between devices, on_device(): attn_w = lax.all_to_all(packed, 'seq', 0, 0, tiled=True)  9.27 us
    all_to_all x1, starting transfers between devices, on_device(): attn_w = lax.all_to_all(packed, 'seq', 0, 0, tiled=True)  7.4 us
    all_to_all x2, starting transfers between devices, members(): lax.all_to_all(value, 'seq', 0, 0, tiled=True, axis_index_groups=index)  6.85 us
  transfers between devices with their start and end apart: 65, of which 28 were waited for; matrix products, arithmetic and copies ran while one was open for 0% of the time, Pallas kernels for 25%

commit v1 on v0

--- a/solution.py
+++ b/solution.py
@@ -125,14 +125,11 @@
     return pl.ds(pl.multiple_of(index * rows, rows), rows)
 
 
-def send_rows(move, place, n, rows, source, send_s, keep, send):
-    for r in range(1, n, 2):
+def send_rows(move, place, n, rows, source, stage, keep, send):
+    for r in list(range(1, n, 2)) + list(range(0, n, 2)):
         here = slice((r // 2) * rows, (r // 2 + 1) * rows)
-        send_s[here, :] = source[rows_at(place.j ^ r, rows), :].astype(bf16)
-        move.put(send_s.at[here, :], send.at[here, :])
-    for r in range(0, n, 2):
-        here = slice((r // 2) * rows, (r // 2 + 1) * rows)
-        move.put(source.at[rows_at(place.j ^ r, rows), :], keep.at[here, :])
+        stage[r % 2, here, :] = source[rows_at(place.j ^ r, rows), :].astype(bf16)
+        move.put(stage.at[r % 2, here, :], (send if r % 2 else keep).at[here, :])
 
 
 def rows_kernel(place, frames, out_grad, x_own, x_send, dy_own, dy_send, sems):
@@ -446,7 +443,7 @@
         here = slice(i * rows, (i + 1) * rows)
         for copy in loads[i]:
             copy.wait()
-        stage[i][...] = (keep_s[here, :] + recv_s[here, :].astype(f32)).astype(outs[i].dtype)
+        stage[i][...] = (keep_s[here, :].astype(f32) + recv_s[here, :].astype(f32)).astype(outs[i].dtype)
         move.put(stage[i], outs[i])
     move.drain()
 
@@ -900,7 +897,8 @@
     ffn_ws = [ffn_w, ffn_half, to_group(ffn_go, 2)]
     dy_even = gather_direct(dy_go)
     x_sds = sds((total, width), bf16)
-    keep_sds, send_sds = sds((total // 2, width), f32), sds((total // 2, width), bf16)
+    keep_sds = send_sds = sds((total // 2, width), bf16)
+    s_half = pltpu.VMEM((2, total // 2, width), bf16)
     outs = [
         x_sds,
         x_sds,
@@ -914,7 +912,7 @@
         keep_sds,
         send_sds,
     ]
-    s_hat, s_h, s_qkv, s_o, s_lse, s_w, s_vec, s_bias, s_wo, _, s_send = [vmem(o) for o in outs]
+    s_hat, s_h, s_qkv, s_o, s_lse, s_w, s_vec, s_bias, s_wo, _, _ = [vmem(o) for o in outs]
     s_rows = pltpu.VMEM((total, width), f32)
     s_got = pltpu.VMEM((ndev, block_rows, 3 * hd), bf16)
     s_wo3 = pltpu.VMEM((groups, rs, width), bf16)
@@ -925,7 +923,7 @@
         outs[:-1] + near(outs[-1:]),
         "first",
         cost(17),
-        scratch=[vmem(x_sds), s_hat, s_h, s_qkv, s_o, s_lse, s_got, s_w, s_vec, s_bias, s_wo3, s_wo, s_rows, s_send]
+        scratch=[vmem(x_sds), s_hat, s_h, s_qkv, s_o, s_lse, s_got, s_w, s_vec, s_bias, s_wo3, s_wo, s_rows, s_half]
         + [pltpu.VMEM((total, 128), f32)],
         sems=3 * n + groups + dp_size + 10,
         lengths=(order, lengths),
@@ -973,7 +971,7 @@
         outs[:4] + near(outs[4:5]) + outs[5:],
         "ffn",
         cost(9),
-        scratch=[vmem(a) for a in [w_up, bias_up, dg] + outs[:3]] + [s_rows, vmem(outs[4]), vmem(outs[5])],
+        scratch=[vmem(a) for a in [w_up, bias_up, dg] + outs[:3]] + [s_rows, s_half, vmem(outs[5])],
         sems=3 * n + 7,
         limit=28 * scale,
     )
@@ -987,7 +985,7 @@
         [keep_sds, Near(send_sds)],
         "down",
         cost(4),
-        scratch=[vmem(g), vmem(w_down), s_rows, vmem(send_sds)],
+        scratch=[vmem(g), vmem(w_down), s_rows, s_half],
         sems=n + 2,
         limit=16 * scale,
     )
@@ -997,7 +995,7 @@
         [h2_all, du, dy_all, g_then],
         [sds(ffn_sds.shape, f32)] + near([ffn_sds] * (groups - 1)),
         "ffn_grads",
-        cost(5),
+        cost(0),
         scratch=[vmem(a) for a in (x_sds, act_sds, x_sds, act_sds)]
         + [pltpu.VMEM((groups,) + ffn_sds.shape, f32), pltpu.VMEM((groups - 1,) + ffn_sds.shape, bf16)],
         sems=4 + groups,
@@ -1038,10 +1036,10 @@
         near(das) + ins,
         outs[:2] + near(outs[2:3]) + outs[3:],
         "attend_back",
-        cost(15),
+        cost(0),
         scratch=[vmem(x_sds)]
         + [vmem(a) for a in (qkv, lse, wo, w_qkv, outs[0])]
-        + [s_rows, vmem(outs[2]), vmem(outs[3]), pltpu.VMEM((total, hd), bf16), pltpu.VMEM((total, 128), f32)]
+        + [s_rows, s_half, vmem(outs[3]), pltpu.VMEM((total, hd), bf16), pltpu.VMEM((total, 128), f32)]
         + [pltpu.VMEM((total, HEAD), f32)] * 2,
         sems=2 * n + 9,
         lengths=(order, lengths),

time: 265 us -> 262 us (0.989)
  transfers between devices with their start and end apart: 65 -> 65, of which waited for: 28 -> 27; matrix products, arithmetic and copies ran while one was open for 0% -> 0% of each run, Pallas kernels for 25% -> 25%
where the time goes in v1:
time: 262 us; the launch traced here: 257 us
  waiting for transfers between devices  99.2 us (38%)
  Pallas kernels  81.8 us (31%)
  starting transfers between devices  72.3 us (28%)
    pallas_call x25, Pallas kernels, call(): pl.pallas_call(body, out_shape=tuple((o.array if isinstance(o, Near) else...  81.8 us
    ppermute x49, waiting for transfers between devices, xor(): return lax.ppermute(value, 'seq', [(i, i ^ bit) for i in range(seq_size)])  73.9 us
    ppermute x49, starting transfers between devices, xor(): return lax.ppermute(value, 'seq', [(i, i ^ bit) for i in range(seq_size)])  41.3 us
    ppermute x6, waiting for transfers between devices, to_group(): return lax.ppermute(value, both, pairs)  16.1 us
    all_to_all x1, waiting for transfers between devices, on_device(): attn_w = lax.all_to_all(packed, 'seq', 0, 0, tiled=True)  9.27 us
    all_to_all x1, starting transfers between devices, on_device(): attn_w = lax.all_to_all(packed, 'seq', 0, 0, tiled=True)  7.4 us
    all_to_all x2, starting transfers between devices, members(): lax.all_to_all(value, 'seq', 0, 0, tiled=True, axis_index_groups=index)  6.85 us
    all_to_all x1, starting transfers between devices, on_device(): back = lax.all_to_all(attn_sum, 'seq', 0, 0, tiled=True)  5.48 us
  transfers between devices with their start and end apart: 65, of which 27 were waited for; matrix products, arithmetic and copies ran while one was open for 0% of the time, Pallas kernels for 25%

profile of v1, /device:TPU:0, one launch (start us, length us, event | category | flops | bytes accessed | tf_op | source)
XLA Modules:
  0.0 257.3 jit_solution(4871226394858104913)
XLA Ops:
  1.8 1.9 pack.1
  3.8 7.4 %all-to-all-start = ((bf16[16,40,384]{2,1,0:T(8,128)(2,1)}), bf16[16,40,384]{2,1,0:T(8,128)(2,1)S(1)}, u32[]{:S(2)}, u32[]{:S(2)}) async-start(bf16[16,40,384]{2,1,0:T(8,128)(2,1)} %pack.1), calls=%async_computation | async-start | bytes 983040 | tf_op jit(solution)/shard_map/all_to_all | solution.py:872
  11.2 2.8 %collective-permute-start.1 = (bf16[64,1024]{1,0:T(8,128)(2,1)S(1)}, bf16[64,1024]{1,0:T(8,128)(2,1)S(1)}, u32[]{:S(2)}, u32[]{:S(2)}) collective-permute-start(bf16[64,1024]{1,0:T(8,128)(2,1)S(1)} %get-tuple-element.158), channel_id=1, source_target_pairs={{0,8},{1,9},{2,10},{3,11},{4,12},{5,13},{6,14},{7,15},{8,0},{9,1},... | collective-permute-start | bytes 393224 | tf_op jit(solution)/shard_map/ppermute | solution.py:770
  14.0 1.5 collective-permute-start.4
  16.1 9.3 %all-to-all-done.refs_10_ = bf16[16,40,384]{2,1,0:T(8,128)(2,1)S(1)} async-done(((bf16[16,40,384]{2,1,0:T(8,128)(2,1)}), bf16[16,40,384]{2,1,0:T(8,128)(2,1)S(1)}, u32[]{:S(2)}, u32[]{:S(2)}) %all-to-all-start) | async-done | bytes 491552 | tf_op jit(solution)/shard_map/all_to_all | solution.py:872
  25.4 1.5 collective-permute-start.2
  26.9 5.8 %collective-permute-done.1 = bf16[64,1024]{1,0:T(8,128)(2,1)S(1)} collective-permute-done((bf16[64,1024]{1,0:T(8,128)(2,1)S(1)}, bf16[64,1024]{1,0:T(8,128)(2,1)S(1)}, u32[]{:S(2)}, u32[]{:S(2)}) %collective-permute-start.1) | collective-permute-done | bytes 131104 | tf_op jit(solution)/shard_map/ppermute | solution.py:770
  32.9 2.9 %collective-permute-start.9 = (bf16[128,1024]{1,0:T(8,128)(2,1)S(1)}, bf16[128,1024]{1,0:T(8,128)(2,1)S(1)}, u32[]{:S(2)}, u32[]{:S(2)}) collective-permute-start(bf16[128,1024]{1,0:T(8,128)(2,1)S(1)} %constant_dynamic-update-slice_fusion.2.refs_2_.refs_4_), channel_id=1, source_target_pairs={{0,4},{1,5},{2,6},{3,7},{4,0},{5,1},{6,2},{7,3},{8,12},{9,13},{10,... | collective-permute-start | bytes 786440 | tf_op jit(solution)/shard_map/ppermute | solution.py:770
  36.3 1.7 pack_up.1
  38.1 3.4 %all-to-all-start.1 = ((bf16[8,32,512]{2,1,0:T(8,128)(2,1)}), bf16[8,32,512]{2,1,0:T(8,128)(2,1)S(1)}, u32[]{:S(2)}, u32[]{:S(2)}) async-start(bf16[8,32,512]{2,1,0:T(8,128)(2,1)} %pack_up.1), calls=%async_computation.1 | async-start | bytes 524288 | tf_op jit(solution)/shard_map/all_to_all | solution.py:808
  42.7 7.4 %collective-permute-done.5.refs_13_ = bf16[2,32,1024]{2,1,0:T(8,128)(2,1)S(1)} collective-permute-done((bf16[2,32,1024]{2,1,0:T(8,128)(2,1)S(1)}, bf16[2,32,1024]{2,1,0:T(8,128)(2,1)S(1)}, u32[]{:S(2)}, u32[]{:S(2)}) %collective-permute-start.5) | collective-permute-done | bytes 131104 | tf_op jit(solution)/shard_map/ppermute | solution.py:770
  50.8 3.4 %collective-permute-start = (bf16[64,1024]{1,0:T(8,128)(2,1)S(1)}, bf16[64,1024]{1,0:T(8,128)(2,1)S(1)}, u32[]{:S(2)}, u32[]{:S(2)}) collective-permute-start(bf16[64,1024]{1,0:T(8,128)(2,1)S(1)} %get-tuple-element.163), channel_id=1, source_target_pairs={{0,8},{1,9},{2,10},{3,11},{4,12},{5,13},{6,14},{7,15},{8,0},{9,1},... | collective-permute-start | bytes 393224 | tf_op jit(solution)/shard_map/ppermute | solution.py:770
  55.3 4.7 %collective-permute-done = bf16[64,1024]{1,0:T(8,128)(2,1)S(1)} collective-permute-done((bf16[64,1024]{1,0:T(8,128)(2,1)S(1)}, bf16[64,1024]{1,0:T(8,128)(2,1)S(1)}, u32[]{:S(2)}, u32[]{:S(2)}) %collective-permute-start) | collective-permute-done | bytes 131104 | tf_op jit(solution)/shard_map/ppermute | solution.py:770
  60.3 3.1 %collective-permute-start.17 = (bf16[128,1024]{1,0:T(8,128)(2,1)S(1)}, bf16[128,1024]{1,0:T(8,128)(2,1)S(1)}, u32[]{:S(2)}, u32[]{:S(2)}) collective-permute-start(bf16[128,1024]{1,0:T(8,128)(2,1)S(1)} %constant_dynamic-update-slice_fusion.refs_0_.refs_6_), channel_id=1, source_target_pairs={{0,6},{1,7},{2,4},{3,5},{4,2},{5,3},{6,0},{7,1},{8,14},{9,15},{10,... | collective-permute-start | bytes 786440 | tf_op jit(solution)/shard_map/ppermute | solution.py:770
  64.1 1.5 collective-permute-start.14
  65.6 12.8 %first.1 = (bf16[1024,1024]{1,0:T(8,128)(2,1)}, bf16[1024,1024]{1,0:T(8,128)(2,1)}, bf16[1024,384]{1,0:T(8,128)(2,1)}, bf16[1024,128]{1,0:T(8,128)(2,1)}, f32[2,...) custom-call(s32[2]{0:T(128)S(1)} %copy-done, ...), custom_call_target="tpu_custom_call" | custom-call | flops 19549999104 | bytes 10531584 | tf_op jit(solution)/shard_map/first/pallas_call | solution.py:82
  78.4 4.5 %collective-permute-done.13.refs_9_ = bf16[512,512]{1,0:T(8,128)(2,1)S(1)} collective-permute-done((bf16[512,512]{1,0:T(8,128)(2,1)S(1)}, bf16[512,512]{1,0:T(8,128)(2,1)S(1)}, u32[]{:S(2)}, u32[]{:S(2)}) %collective-permute-start.13) | collective-permute-done | bytes 524320 | tf_op jit(solution)/shard_map/ppermute | solution.py:804
  83.7 2.7 %collective-permute-done.18.refs_1_ = bf16[512,1024]{1,0:T(8,128)(2,1)S(1)} collective-permute-done((bf16[512,1024]{1,0:T(8,128)(2,1)S(1)}, bf16[512,1024]{1,0:T(8,128)(2,1)S(1)}, u32[]{:S(2)}, u32[]{:S(2)}) %collective-permute-start.18) | collective-permute-done | bytes 1048608 | tf_op jit(solution)/shard_map/ppermute | solution.py:770
  86.4 1.4 pair.4
  87.8 1.5 collective-permute-start.19
  89.3 2.0 collective-permute-start.21
  91.9 4.3 %collective-permute-done.19.refs_1_ = bf16[128,1024]{1,0:T(8,128)(2,1)S(1)} collective-permute-done((bf16[128,1024]{1,0:T(8,128)(2,1)S(1)}, bf16[128,1024]{1,0:T(8,128)(2,1)S(1)}, u32[]{:S(2)}, u32[]{:S(2)}) %collective-permute-start.19) | collective-permute-done | bytes 262176 | tf_op jit(solution)/shard_map/ppermute | solution.py:770
  96.2 2.3 collective-permute-done.20.refs_2_
  98.5 4.5 %collective-permute-done.21.refs_3_ = bf16[128,1024]{1,0:T(8,128)(2,1)S(1)} collective-permute-done((bf16[128,1024]{1,0:T(8,128)(2,1)S(1)}, bf16[128,1024]{1,0:T(8,128)(2,1)S(1)}, u32[]{:S(2)}, u32[]{:S(2)}) %collective-permute-start.21) | collective-permute-done | bytes 262176 | tf_op jit(solution)/shard_map/ppermute | solution.py:770
  103.0 2.1 mid.1
  106.4 1.7 collective-permute-start.30
  108.7 4.0 %down_back.1 = (bf16[1024,1024]{1,0:T(8,128)(2,1)}, f32[1024,512]{1,0:T(8,128)}, bf16[1024,512]{1,0:T(8,128)(2,1)}, bf16[512,1024]{1,0:T(8,128)(2,1)}) custom-call(bf16[128,1024]{1,0:T(8,128)(2,1)S(1)} %constant_dynamic-update-slice_fusion.refs_0_.refs_6_, bf16[128,1024]{1,0:T(8,128)(2,1)S(1)} %collective-permute-done.24.refs_1_, ...), custom_call_target="tpu_custom_call" | custom-call | flops 5750000128 | bytes 10485760 | tf_op jit(solution)/shard_map/down_back/pallas_call | solution.py:82
  112.6 2.6 collective-permute-done.32.refs_6_
  115.2 5.2 %collective-permute-done.30.refs_4_ = bf16[128,1024]{1,0:T(8,128)(2,1)S(1)} collective-permute-done((bf16[128,1024]{1,0:T(8,128)(2,1)S(1)}, bf16[128,1024]{1,0:T(8,128)(2,1)S(1)}, u32[]{:S(2)}, u32[]{:S(2)}) %collective-permute-start.30) | collective-permute-done | bytes 262176 | tf_op jit(solution)/shard_map/ppermute | solution.py:770
  122.7 7.7 %ffn.1 = (bf16[1024,1024]{1,0:T(8,128)(2,1)}, bf16[1024,512]{1,0:T(8,128)(2,1)}, bf16[1024,512]{1,0:T(8,128)(2,1)}, bf16[512,1024]{1,0:T(8,128)(2,1)}, bf16[512,1024]{1,0:T(8,128)(2,1)S(1)}, /*index=5*/f32[1,512]{1,0:T(1,128)}) custom-call(bf16[128,1024]{1,0:T(8,128)(2,1)S(1)} %get-tuple-element.192.refs_0_, ...), custom_call_target="tpu_custom_call" | custom-call | flops 10350000128 | bytes 11538432 | tf_op jit(solution)/shard_map/ffn/pallas_call | solution.py:82
  130.6 2.5 collective-permute-done.34.refs_1_
  133.1 1.4 pair.5
  134.6 1.5 collective-permute-start.35
  136.3 1.8 collective-permute-start.37
  138.1 5.8 %ffn_grads.1 = (f32[512,512]{1,0:T(8,128)}, bf16[512,512]{1,0:T(8,128)(2,1)S(1)}, bf16[512,512]{1,0:T(8,128)(2,1)S(1)}, bf16[512,512]{1,0:T(8,128)(2,1)S(1)}) custom-call(bf16[1024,1024]{1,0:T(8,128)(2,1)} %get-tuple-element.215.refs_0_, bf16[1024,512]{1,0:T(8,128)(2,1)} %get-tuple-element.216.refs_1_, bf16[1024,1024]{1,0:T(8,128)(2,1)} %get-tuple-element.217.refs_2_, ...), custom_call_target="tpu_custom_call" | custom-call | bytes 8912896 | tf_op jit(solution)/shard_map/ffn_grads/pallas_call | solution.py:82
  144.0 4.1 %down.1 = (bf16[512,1024]{1,0:T(8,128)(2,1)}, bf16[512,1024]{1,0:T(8,128)(2,1)S(1)}) custom-call(bf16[1024,512]{1,0:T(8,128)(2,1)} %get-tuple-element.207.refs_0_.refs_3_, bf16[512,1024]{1,0:T(8,128)(2,1)} %get-tuple-element.208.refs_1_), custom_call_target="tpu_custom_call" | custom-call | flops 4600000000 | bytes 4194304 | tf_op jit(solution)/shard_map/down/pallas_call | solution.py:82
  148.1 1.7 collective-permute-done.37.refs_3_
  149.8 2.6 mid_back.1
  154.2 1.3 collective-permute-start.43
  156.5 1.4 pair.6
  158.0 8.8 %collective-permute-done.41.refs_1_ = bf16[512,512]{1,0:T(8,128)(2,1)S(1)} collective-permute-done((bf16[512,512]{1,0:T(8,128)(2,1)S(1)}, bf16[512,512]{1,0:T(8,128)(2,1)S(1)}, u32[]{:S(2)}, u32[]{:S(2)}) %collective-permute-start.41) | collective-permute-done | bytes 524320 | tf_op jit(solution)/shard_map/ppermute | solution.py:804
  168.5 1.5 collective-permute-start.50
  170.8 1.4 collective-permute-start.47
  174.3 13.6 %attend_back.1 = (bf16[1024,384]{1,0:T(8,128)(2,1)}, bf16[512,1024]{1,0:T(8,128)(2,1)}, bf16[512,1024]{1,0:T(8,128)(2,1)S(1)}, f32[1,384]{1,0:T(1,128)}, bf16[1024,1024]{1,0:T(8,128)(2,1)}) custom-call(s32[2]{0:T(128)S(1)} %copy-done, s32[4]{0:T(128)S(1)} %copy-done.1, bf16[128,1024]{1,0:T(8,128)(2,1)S(1)} %get-tuple-element.232.refs_2_, ...), custom_call_target="tpu_custom_call" | custom-call | bytes 8922624 | tf_op jit(solution)/shard_map/attend_back/pallas_call | solution.py:82
  188.8 4.8 %collective-permute-done.49.refs_3_ = bf16[128,1024]{1,0:T(8,128)(2,1)S(1)} collective-permute-done((bf16[128,1024]{1,0:T(8,128)(2,1)S(1)}, bf16[128,1024]{1,0:T(8,128)(2,1)S(1)}, u32[]{:S(2)}, u32[]{:S(2)}) %collective-permute-start.49) | collective-permute-done | bytes 262176 | tf_op jit(solution)/shard_map/ppermute | solution.py:770
  193.6 2.8 %collective-permute-done.51.refs_2_ = bf16[512,512]{1,0:T(8,128)(2,1)S(1)} collective-permute-done((bf16[512,512]{1,0:T(8,128)(2,1)S(1)}, bf16[512,512]{1,0:T(8,128)(2,1)S(1)}, u32[]{:S(2)}, u32[]{:S(2)}) %collective-permute-start.51) | collective-permute-done | bytes 524320 | tf_op jit(solution)/shard_map/ppermute | solution.py:804
  196.4 5.5 %attn_grads.1 = (bf16[16,40,384]{2,1,0:T(8,128)(2,1)S(1)}, bf16[16,40,384]{2,1,0:T(8,128)(2,1)S(1)}) custom-call(bf16[1024,384]{1,0:T(8,128)(2,1)} %get-tuple-element.244.refs_0_, bf16[1024,1024]{1,0:T(8,128)(2,1)} %get-tuple-element.245.refs_1_, bf16[1024,384]{1,0:T(8,128)(2,1)} %get-tuple-element.243.refs_13_.refs_2_, ...), custom_call_target="tpu_custom_call" | custom-call | flops 6899999744 | bytes 5789696 | tf_op jit(solution)/shard_map/attn_grads/pallas_call | solution.py:82
  202.7 1.4 collective-permute-start.53
  204.1 1.4 pair.7
  205.5 2.4 ffn_sum.1
  207.9 3.4 %all-to-all-start.2 = ((bf16[8,32,512]{2,1,0:T(8,128)(2,1)}), bf16[8,32,512]{2,1,0:T(8,128)(2,1)S(1)}, u32[]{:S(2)}, u32[]{:S(2)}) async-start(bf16[8,32,512]{2,1,0:T(8,128)(2,1)} %get-tuple-element.262), calls=%async_computation.2 | async-start | bytes 524288 | tf_op jit(solution)/shard_map/all_to_all | solution.py:808
  211.4 2.6 out_grads.1
  214.6 1.9 collective-permute-start.55
  216.6 1.5 collective-permute-start.56
  219.2 1.5 fold.4
  220.7 5.5 %all-to-all-start.3 = ((bf16[16,40,384]{2,1,0:T(8,128)(2,1)}), bf16[16,40,384]{2,1,0:T(8,128)(2,1)S(1)}, u32[]{:S(2)}, u32[]{:S(2)}) async-start(bf16[16,40,384]{2,1,0:T(8,128)(2,1)} %fold.4), calls=%async_computation.3 | async-start | bytes 983040 | tf_op jit(solution)/shard_map/all_to_all | solution.py:1110
  226.8 3.6 %collective-permute-done.57.refs_3_ = bf16[128,1024]{1,0:T(8,128)(2,1)} collective-permute-done((bf16[128,1024]{1,0:T(8,128)(2,1)S(1)}, bf16[128,1024]{1,0:T(8,128)(2,1)}, u32[]{:S(2)}, u32[]{:S(2)}) %collective-permute-start.57) | collective-permute-done | bytes 262176 | tf_op jit(solution)/shard_map/ppermute | solution.py:770
  230.4 2.3 last.1
  232.7 1.7 collective-permute-start.58
  234.4 1.7 out.1
  236.1 1.4 collective-permute-start.60
  237.4 15.0 %collective-permute-done.58.refs_6_ = bf16[96,1024]{1,0:T(8,128)(2,1)S(1)} collective-permute-done((bf16[96,1024]{1,0:T(8,128)(2,1)S(1)}, bf16[96,1024]{1,0:T(8,128)(2,1)S(1)}, u32[]{:S(2)}, u32[]{:S(2)}) %collective-permute-start.58) | collective-permute-done | bytes 196640 | tf_op jit(solution)/shard_map/ppermute | solution.py:770
  253.2 2.1 collective-permute-done.60.refs_4_
  255.3 1.8 unpack.1
  (121 shorter events, 24.6 us)
Async XLA Ops:
  3.8 21.7 %all-to-all-start = ((bf16[16,40,384]{2,1,0:T(8,128)(2,1)}), bf16[16,40,384]{2,1,0:T(8,128)(2,1)S(1)}, u32[]{:S(2)}, u32[]{:S(2)}) async-start(bf16[16,40,384]{2,1,0:T(8,128)(2,1)} %pack.1), calls=%async_computation | async-start | bytes 983040 | tf_op jit(solution)/shard_map/all_to_all | solution.py:872
  11.2 21.6 %collective-permute-start.1 = (bf16[64,1024]{1,0:T(8,128)(2,1)S(1)}, bf16[64,1024]{1,0:T(8,128)(2,1)S(1)}, u32[]{:S(2)}, u32[]{:S(2)}) collective-permute-start(bf16[64,1024]{1,0:T(8,128)(2,1)S(1)} %get-tuple-element.158), channel_id=1, source_target_pairs={{0,8},{1,9},{2,10},{3,11},{4,12},{5,13},{6,14},{7,15},{8,0},{9,1},... | collective-permute-start | bytes 393224 | tf_op jit(solution)/shard_map/ppermute | solution.py:770
  14.0 21.8 %collective-permute-start.4 = (bf16[32,1024]{1,0:T(8,128)(2,1)S(1)}, bf16[32,1024]{1,0:T(8,128)(2,1)S(1)}, u32[]{:S(2)}, u32[]{:S(2)}) collective-permute-start(bf16[32,1024]{1,0:T(8,128)(2,1)S(1)} %copy-done.11), channel_id=1, source_target_pairs={{0,16},{1,24},{2,0},{3,8},{4,17},{5,25},{6,1},{7,9},{8,18},{9,26},... | collective-permute-start | bytes 196616 | tf_op jit(solution)/shard_map/ppermute | solution.py:841
  15.5 26.0 %collective-permute-start.3 = (bf16[32,1024]{1,0:T(8,128)(2,1)S(1)}, bf16[32,1024]{1,0:T(8,128)(2,1)S(1)}, u32[]{:S(2)}, u32[]{:S(2)}) collective-permute-start(bf16[32,1024]{1,0:T(8,128)(2,1)S(1)} %copy-done.11), channel_id=1, source_target_pairs={{0,0},{1,8},{2,16},{3,24},{4,1},{5,9},{6,17},{7,25},{8,2},{9,10},{... | collective-permute-start | bytes 196616 | tf_op jit(solution)/shard_map/ppermute | solution.py:841
  25.4 28.8 %collective-permute-start.2 = (bf16[16,40,384]{2,1,0:T(8,128)(2,1)S(1)}, bf16[16,40,384]{2,1,0:T(8,128)(2,1)S(1)}, u32[]{:S(2)}, u32[]{:S(2)}) collective-permute-start(bf16[16,40,384]{2,1,0:T(8,128)(2,1)S(1)} %all-to-all-done.refs_10_), channel_id=1, source_target_pairs={{0,16},{16,0},{1,17},{17,1},{2,18},{18,2},{3,19},{19,3},{4,20},{20... | collective-permute-start | bytes 1474568 | tf_op jit(solution)/shard_map/ppermute | solution.py:831
  32.8 21.4 %collective-permute-start.11 = (bf16[128,1024]{1,0:T(8,128)(2,1)S(1)}, bf16[128,1024]{1,0:T(8,128)(2,1)S(1)}, u32[]{:S(2)}, u32[]{:S(2)}) collective-permute-start(bf16[128,1024]{1,0:T(8,128)(2,1)S(1)} %constant_dynamic-update-slice_fusion.2.refs_2_.refs_4_), channel_id=1, source_target_pairs={{0,6},{1,7},{2,4},{3,5},{4,2},{5,3},{6,0},{7,1},{8,14},{9,15},{10,... | collective-permute-start | bytes 786440 | tf_op jit(solution)/shard_map/ppermute | solution.py:770
  32.9 21.4 %collective-permute-start.9 = (bf16[128,1024]{1,0:T(8,128)(2,1)S(1)}, bf16[128,1024]{1,0:T(8,128)(2,1)S(1)}, u32[]{:S(2)}, u32[]{:S(2)}) collective-permute-start(bf16[128,1024]{1,0:T(8,128)(2,1)S(1)} %constant_dynamic-update-slice_fusion.2.refs_2_.refs_4_), channel_id=1, source_target_pairs={{0,4},{1,5},{2,6},{3,7},{4,0},{5,1},{6,2},{7,3},{8,12},{9,13},{10,... | collective-permute-start | bytes 786440 | tf_op jit(solution)/shard_map/ppermute | solution.py:770
  35.8 18.4 %collective-permute-start.7 = (bf16[128,1024]{1,0:T(8,128)(2,1)S(1)}, bf16[128,1024]{1,0:T(8,128)(2,1)S(1)}, u32[]{:S(2)}, u32[]{:S(2)}) collective-permute-start(bf16[128,1024]{1,0:T(8,128)(2,1)S(1)} %constant_dynamic-update-slice_fusion.2.refs_2_.refs_4_), channel_id=1, source_target_pairs={{0,2},{1,3},{2,0},{3,1},{4,6},{5,7},{6,4},{7,5},{8,10},{9,11},{10,... | collective-permute-start | bytes 786440 | tf_op jit(solution)/shard_map/ppermute | solution.py:770
  38.1 22.0 %all-to-all-start.1 = ((bf16[8,32,512]{2,1,0:T(8,128)(2,1)}), bf16[8,32,512]{2,1,0:T(8,128)(2,1)S(1)}, u32[]{:S(2)}, u32[]{:S(2)}) async-start(bf16[8,32,512]{2,1,0:T(8,128)(2,1)} %pack_up.1), calls=%async_computation.1 | async-start | bytes 524288 | tf_op jit(solution)/shard_map/all_to_all | solution.py:808
  41.5 8.6 %collective-permute-start.5 = (bf16[2,32,1024]{2,1,0:T(8,128)(2,1)S(1)}, bf16[2,32,1024]{2,1,0:T(8,128)(2,1)S(1)}, u32[]{:S(2)}, u32[]{:S(2)}) collective-permute-start(bf16[2,32,1024]{2,1,0:T(8,128)(2,1)S(1)} %pad_maximum_fusion.refs_12_), channel_id=1, source_target_pairs={{0,8},{1,9},{2,10},{3,11},{4,12},{5,13},{6,14},{7,15},{8,0},{9,1},... | collective-permute-start | bytes 393224 | tf_op jit(solution)/shard_map/ppermute | solution.py:770
  50.8 9.2 %collective-permute-start = (bf16[64,1024]{1,0:T(8,128)(2,1)S(1)}, bf16[64,1024]{1,0:T(8,128)(2,1)S(1)}, u32[]{:S(2)}, u32[]{:S(2)}) collective-permute-start(bf16[64,1024]{1,0:T(8,128)(2,1)S(1)} %get-tuple-element.163), channel_id=1, source_target_pairs={{0,8},{1,9},{2,10},{3,11},{4,12},{5,13},{6,14},{7,15},{8,0},{9,1},... | collective-permute-start | bytes 393224 | tf_op jit(solution)/shard_map/ppermute | solution.py:770
  54.2 6.1 %collective-permute-start.6 = (bf16[128,1024]{1,0:T(8,128)(2,1)S(1)}, bf16[128,1024]{1,0:T(8,128)(2,1)S(1)}, u32[]{:S(2)}, u32[]{:S(2)}) collective-permute-start(bf16[128,1024]{1,0:T(8,128)(2,1)S(1)} %constant_dynamic-update-slice_fusion.2.refs_2_.refs_4_), channel_id=1, source_target_pairs={{0,1},{1,0},{2,3},{3,2},{4,5},{5,4},{6,7},{7,6},{8,9},{9,8},{10,11... | collective-permute-start | bytes 786440 | tf_op jit(solution)/shard_map/ppermute | solution.py:770
  54.3 6.0 %collective-permute-start.8 = (bf16[128,1024]{1,0:T(8,128)(2,1)S(1)}, bf16[128,1024]{1,0:T(8,128)(2,1)}, u32[]{:S(2)}, u32[]{:S(2)}) collective-permute-start(bf16[128,1024]{1,0:T(8,128)(2,1)S(1)} %collective-permute-done.7.refs_4_), channel_id=1, source_target_pairs={{0,1},{1,0},{2,3},{3,2},{4,5},{5,4},{6,7},{7,6},{8,9},{9,8},{10,11... | collective-permute-start | bytes 786440 | tf_op jit(solution)/shard_map/ppermute | solution.py:770
  54.8 5.5 %collective-permute-start.10 = (bf16[128,1024]{1,0:T(8,128)(2,1)S(1)}, bf16[128,1024]{1,0:T(8,128)(2,1)}, u32[]{:S(2)}, u32[]{:S(2)}) collective-permute-start(bf16[128,1024]{1,0:T(8,128)(2,1)S(1)} %collective-permute-done.9.refs_6_), channel_id=1, source_target_pairs={{0,1},{1,0},{2,3},{3,2},{4,5},{5,4},{6,7},{7,6},{8,9},{9,8},{10,11... | collective-permute-start | bytes 786440 | tf_op jit(solution)/shard_map/ppermute | solution.py:770
  54.9 5.4 %collective-permute-start.12 = (bf16[128,1024]{1,0:T(8,128)(2,1)S(1)}, bf16[128,1024]{1,0:T(8,128)(2,1)}, u32[]{:S(2)}, u32[]{:S(2)}) collective-permute-start(bf16[128,1024]{1,0:T(8,128)(2,1)S(1)} %collective-permute-done.11.refs_8_), channel_id=1, source_target_pairs={{0,1},{1,0},{2,3},{3,2},{4,5},{5,4},{6,7},{7,6},{8,9},{9,8},{10,11... | collective-permute-start | bytes 786440 | tf_op jit(solution)/shard_map/ppermute | solution.py:770
  60.2 22.7 %collective-permute-start.13 = (bf16[512,512]{1,0:T(8,128)(2,1)S(1)}, bf16[512,512]{1,0:T(8,128)(2,1)S(1)}, u32[]{:S(2)}, u32[]{:S(2)}) collective-permute-start(bf16[512,512]{1,0:T(8,128)(2,1)S(1)} %join.1.refs_8_), channel_id=1, source_target_pairs={{0,8},{1,9},{2,10},{3,11},{4,12},{5,13},{6,14},{7,15},{8,0},{9,1},... | collective-permute-start | bytes 1572872 | tf_op jit(solution)/shard_map/ppermute | solution.py:804
  60.3 22.5 %collective-permute-start.17 = (bf16[128,1024]{1,0:T(8,128)(2,1)S(1)}, bf16[128,1024]{1,0:T(8,128)(2,1)S(1)}, u32[]{:S(2)}, u32[]{:S(2)}) collective-permute-start(bf16[128,1024]{1,0:T(8,128)(2,1)S(1)} %constant_dynamic-update-slice_fusion.refs_0_.refs_6_), channel_id=1, source_target_pairs={{0,6},{1,7},{2,4},{3,5},{4,2},{5,3},{6,0},{7,1},{8,14},{9,15},{10,... | collective-permute-start | bytes 786440 | tf_op jit(solution)/shard_map/ppermute | solution.py:770
  63.4 20.3 %collective-permute-start.16 = (bf16[128,1024]{1,0:T(8,128)(2,1)S(1)}, bf16[128,1024]{1,0:T(8,128)(2,1)S(1)}, u32[]{:S(2)}, u32[]{:S(2)}) collective-permute-start(bf16[128,1024]{1,0:T(8,128)(2,1)S(1)} %constant_dynamic-update-slice_fusion.refs_0_.refs_6_), channel_id=1, source_target_pairs={{0,4},{1,5},{2,6},{3,7},{4,0},{5,1},{6,2},{7,3},{8,12},{9,13},{10,... | collective-permute-start | bytes 786440 | tf_op jit(solution)/shard_map/ppermute | solution.py:770
  63.4 20.3 %collective-permute-start.15 = (bf16[128,1024]{1,0:T(8,128)(2,1)S(1)}, bf16[128,1024]{1,0:T(8,128)(2,1)S(1)}, u32[]{:S(2)}, u32[]{:S(2)}) collective-permute-start(bf16[128,1024]{1,0:T(8,128)(2,1)S(1)} %constant_dynamic-update-slice_fusion.refs_0_.refs_6_), channel_id=1, source_target_pairs={{0,2},{1,3},{2,0},{3,1},{4,6},{5,7},{6,4},{7,5},{8,10},{9,11},{10,... | collective-permute-start | bytes 786440 | tf_op jit(solution)/shard_map/ppermute | solution.py:770
  64.1 19.6 %collective-permute-start.14 = (bf16[512,512]{1,0:T(8,128)(2,1)S(1)}, bf16[512,512]{1,0:T(8,128)(2,1)S(1)}, u32[]{:S(2)}, u32[]{:S(2)}) collective-permute-start(bf16[512,512]{1,0:T(8,128)(2,1)S(1)} %join.1.refs_8_), channel_id=1, source_target_pairs={{0,16},{1,17},{2,18},{3,19},{4,20},{5,21},{6,22},{7,23},{8,24},{9,... | collective-permute-start | bytes 1572872 | tf_op jit(solution)/shard_map/ppermute | solution.py:804
  83.7 2.7 %collective-permute-start.18 = (bf16[512,1024]{1,0:T(8,128)(2,1)S(1)}, bf16[512,1024]{1,0:T(8,128)(2,1)S(1)}, u32[]{:S(2)}, u32[]{:S(2)}) collective-permute-start(bf16[512,1024]{1,0:T(8,128)(2,1)S(1)} %get-tuple-element.186), channel_id=1, source_target_pairs={{0,1},{1,0},{2,3},{3,2},{4,5},{5,4},{6,7},{7,6},{8,9},{9,8},{10,11... | collective-permute-start | bytes 3145736 | tf_op jit(solution)/shard_map/ppermute | solution.py:770
  87.8 8.4 %collective-permute-start.19 = (bf16[128,1024]{1,0:T(8,128)(2,1)S(1)}, bf16[128,1024]{1,0:T(8,128)(2,1)S(1)}, u32[]{:S(2)}, u32[]{:S(2)}) collective-permute-start(bf16[128,1024]{1,0:T(8,128)(2,1)S(1)} %get-tuple-element.188), channel_id=1, source_target_pairs={{0,2},{1,3},{2,0},{3,1},{4,6},{5,7},{6,4},{7,5},{8,10},{9,11},{10,... | collective-permute-start | bytes 786440 | tf_op jit(solution)/shard_map/ppermute | solution.py:770
  89.3 9.2 %collective-permute-start.20 = (bf16[128,1024]{1,0:T(8,128)(2,1)S(1)}, bf16[128,1024]{1,0:T(8,128)(2,1)S(1)}, u32[]{:S(2)}, u32[]{:S(2)}) collective-permute-start(bf16[128,1024]{1,0:T(8,128)(2,1)S(1)} %get-tuple-element.189), channel_id=1, source_target_pairs={{0,4},{1,5},{2,6},{3,7},{4,0},{5,1},{6,2},{7,3},{8,12},{9,13},{10,... | collective-permute-start | bytes 786440 | tf_op jit(solution)/shard_map/ppermute | solution.py:770
  89.3 13.7 %collective-permute-start.21 = (bf16[128,1024]{1,0:T(8,128)(2,1)S(1)}, bf16[128,1024]{1,0:T(8,128)(2,1)S(1)}, u32[]{:S(2)}, u32[]{:S(2)}) collective-permute-start(bf16[128,1024]{1,0:T(8,128)(2,1)S(1)} %get-tuple-element.190), channel_id=1, source_target_pairs={{0,6},{1,7},{2,4},{3,5},{4,2},{5,3},{6,0},{7,1},{8,14},{9,15},{10,... | collective-permute-start | bytes 786440 | tf_op jit(solution)/shard_map/ppermute | solution.py:770
  91.3 17.3 %collective-permute-start.28 = (bf16[512,512]{1,0:T(8,128)(2,1)S(1)}, bf16[512,512]{1,0:T(8,128)(2,1)S(1)}, u32[]{:S(2)}, u32[]{:S(2)}) collective-permute-start(bf16[512,512]{1,0:T(8,128)(2,1)S(1)} %collective-permute-done.13.refs_9_), channel_id=1, source_target_pairs={{0,16},{1,17},{2,18},{3,19},{4,20},{5,21},{6,22},{7,23},{8,24},{9,... | collective-permute-start | bytes 1572872 | tf_op jit(solution)/shard_map/ppermute | solution.py:804
  91.9 13.2 %collective-permute-start.24 = (bf16[128,1024]{1,0:T(8,128)(2,1)S(1)}, bf16[128,1024]{1,0:T(8,128)(2,1)S(1)}, u32[]{:S(2)}, u32[]{:S(2)}) collective-permute-start(bf16[128,1024]{1,0:T(8,128)(2,1)S(1)} %constant_dynamic-update-slice_fusion.refs_0_.refs_6_), channel_id=1, source_target_pairs={{0,1},{1,0},{2,3},{3,2},{4,5},{5,4},{6,7},{7,6},{8,9},{9,8},{10,11... | collective-permute-start | bytes 786440 | tf_op jit(solution)/shard_map/ppermute | solution.py:770
  96.2 10.2 %collective-permute-start.25 = (bf16[128,1024]{1,0:T(8,128)(2,1)S(1)}, bf16[128,1024]{1,0:T(8,128)(2,1)S(1)}, u32[]{:S(2)}, u32[]{:S(2)}) collective-permute-start(bf16[128,1024]{1,0:T(8,128)(2,1)S(1)} %collective-permute-done.15.refs_2_), channel_id=1, source_target_pairs={{0,1},{1,0},{2,3},{3,2},{4,5},{5,4},{6,7},{7,6},{8,9},{9,8},{10,11... | collective-permute-start | bytes 786440 | tf_op jit(solution)/shard_map/ppermute | solution.py:770
  98.5 9.6 %collective-permute-start.26 = (bf16[128,1024]{1,0:T(8,128)(2,1)S(1)}, bf16[128,1024]{1,0:T(8,128)(2,1)S(1)}, u32[]{:S(2)}, u32[]{:S(2)}) collective-permute-start(bf16[128,1024]{1,0:T(8,128)(2,1)S(1)} %collective-permute-done.16.refs_4_), channel_id=1, source_target_pairs={{0,1},{1,0},{2,3},{3,2},{4,5},{5,4},{6,7},{7,6},{8,9},{9,8},{10,11... | collective-permute-start | bytes 786440 | tf_op jit(solution)/shard_map/ppermute | solution.py:770
  103.0 5.7 %collective-permute-start.27 = (bf16[128,1024]{1,0:T(8,128)(2,1)S(1)}, bf16[128,1024]{1,0:T(8,128)(2,1)S(1)}, u32[]{:S(2)}, u32[]{:S(2)}) collective-permute-start(bf16[128,1024]{1,0:T(8,128)(2,1)S(1)} %collective-permute-done.17.refs_6_), channel_id=1, source_target_pairs={{0,1},{1,0},{2,3},{3,2},{4,5},{5,4},{6,7},{7,6},{8,9},{9,8},{10,11... | collective-permute-start | bytes 786440 | tf_op jit(solution)/shard_map/ppermute | solution.py:770
  105.1 10.1 %collective-permute-start.32 = (bf16[128,1024]{1,0:T(8,128)(2,1)S(1)}, bf16[128,1024]{1,0:T(8,128)(2,1)S(1)}, u32[]{:S(2)}, u32[]{:S(2)}) collective-permute-start(bf16[128,1024]{1,0:T(8,128)(2,1)S(1)} %get-tuple-element.192.refs_0_), channel_id=1, source_target_pairs={{0,6},{1,7},{2,4},{3,5},{4,2},{5,3},{6,0},{7,1},{8,14},{9,15},{10,... | collective-permute-start | bytes 786440 | tf_op jit(solution)/shard_map/ppermute | solution.py:770
  106.4 14.1 %collective-permute-start.30 = (bf16[128,1024]{1,0:T(8,128)(2,1)S(1)}, bf16[128,1024]{1,0:T(8,128)(2,1)S(1)}, u32[]{:S(2)}, u32[]{:S(2)}) collective-permute-start(bf16[128,1024]{1,0:T(8,128)(2,1)S(1)} %get-tuple-element.192.refs_0_), channel_id=1, source_target_pairs={{0,4},{1,5},{2,6},{3,7},{4,0},{5,1},{6,2},{7,3},{8,12},{9,13},{10,... | collective-permute-start | bytes 786440 | tf_op jit(solution)/shard_map/ppermute | solution.py:770
  108.1 12.3 %collective-permute-start.23 = (bf16[128,1024]{1,0:T(8,128)(2,1)S(1)}, bf16[128,1024]{1,0:T(8,128)(2,1)S(1)}, u32[]{:S(2)}, u32[]{:S(2)}) collective-permute-start(bf16[128,1024]{1,0:T(8,128)(2,1)S(1)} %get-tuple-element.192.refs_0_), channel_id=1, source_target_pairs={{0,2},{1,3},{2,0},{3,1},{4,6},{5,7},{6,4},{7,5},{8,10},{9,11},{10,... | collective-permute-start | bytes 786440 | tf_op jit(solution)/shard_map/ppermute | solution.py:770
  108.7 12.3 %collective-permute-start.22 = (bf16[128,1024]{1,0:T(8,128)(2,1)S(1)}, bf16[128,1024]{1,0:T(8,128)(2,1)S(1)}, u32[]{:S(2)}, u32[]{:S(2)}) collective-permute-start(bf16[128,1024]{1,0:T(8,128)(2,1)S(1)} %get-tuple-element.192.refs_0_), channel_id=1, source_target_pairs={{0,1},{1,0},{2,3},{3,2},{4,5},{5,4},{6,7},{7,6},{8,9},{9,8},{10,11... | collective-permute-start | bytes 786440 | tf_op jit(solution)/shard_map/ppermute | solution.py:770
  120.5 1.9 collective-permute-start.31
  121.0 1.8 collective-permute-start.33
  130.4 2.7 %collective-permute-start.34 = (bf16[512,1024]{1,0:T(8,128)(2,1)S(1)}, bf16[512,1024]{1,0:T(8,128)(2,1)S(1)}, u32[]{:S(2)}, u32[]{:S(2)}) collective-permute-start(bf16[512,1024]{1,0:T(8,128)(2,1)S(1)} %get-tuple-element.205), channel_id=1, source_target_pairs={{0,1},{1,0},{2,3},{3,2},{4,5},{5,4},{6,7},{7,6},{8,9},{9,8},{10,11... | collective-permute-start | bytes 3145736 | tf_op jit(solution)/shard_map/ppermute | solution.py:770
  134.6 13.5 %collective-permute-start.35 = (bf16[128,1024]{1,0:T(8,128)(2,1)S(1)}, bf16[128,1024]{1,0:T(8,128)(2,1)S(1)}, u32[]{:S(2)}, u32[]{:S(2)}) collective-permute-start(bf16[128,1024]{1,0:T(8,128)(2,1)S(1)} %get-tuple-element.211), channel_id=1, source_target_pairs={{0,2},{1,3},{2,0},{3,1},{4,6},{5,7},{6,4},{7,5},{8,10},{9,11},{10,... | collective-permute-start | bytes 786440 | tf_op jit(solution)/shard_map/ppermute | solution.py:770
  136.0 12.0 %collective-permute-start.36 = (bf16[128,1024]{1,0:T(8,128)(2,1)S(1)}, bf16[128,1024]{1,0:T(8,128)(2,1)S(1)}, u32[]{:S(2)}, u32[]{:S(2)}) collective-permute-start(bf16[128,1024]{1,0:T(8,128)(2,1)S(1)} %get-tuple-element.212), channel_id=1, source_target_pairs={{0,4},{1,5},{2,6},{3,7},{4,0},{5,1},{6,2},{7,3},{8,12},{9,13},{10,... | collective-permute-start | bytes 786440 | tf_op jit(solution)/shard_map/ppermute | solution.py:770
  136.3 13.4 %collective-permute-start.37 = (bf16[128,1024]{1,0:T(8,128)(2,1)S(1)}, bf16[128,1024]{1,0:T(8,128)(2,1)S(1)}, u32[]{:S(2)}, u32[]{:S(2)}) collective-permute-start(bf16[128,1024]{1,0:T(8,128)(2,1)S(1)} %get-tuple-element.213), channel_id=1, source_target_pairs={{0,6},{1,7},{2,4},{3,5},{4,2},{5,3},{6,0},{7,1},{8,14},{9,15},{10,... | collective-permute-start | bytes 786440 | tf_op jit(solution)/shard_map/ppermute | solution.py:770
  152.3 4.2 %collective-permute-start.38 = (bf16[512,1024]{1,0:T(8,128)(2,1)S(1)}, bf16[512,1024]{1,0:T(8,128)(2,1)S(1)}, u32[]{:S(2)}, u32[]{:S(2)}) collective-permute-start(bf16[512,1024]{1,0:T(8,128)(2,1)S(1)} %get-tuple-element.221), channel_id=1, source_target_pairs={{0,1},{1,0},{2,3},{3,2},{4,5},{5,4},{6,7},{7,6},{8,9},{9,8},{10,11... | collective-permute-start | bytes 3145736 | tf_op jit(solution)/shard_map/ppermute | solution.py:770
  152.4 14.3 %collective-permute-start.41 = (bf16[512,512]{1,0:T(8,128)(2,1)S(1)}, bf16[512,512]{1,0:T(8,128)(2,1)S(1)}, u32[]{:S(2)}, u32[]{:S(2)}) collective-permute-start(bf16[512,512]{1,0:T(8,128)(2,1)S(1)} %get-tuple-element.228), channel_id=1, source_target_pairs={{0,16},{1,17},{2,18},{3,19},{4,20},{5,21},{6,22},{7,23},{8,24},{9,... | collective-permute-start | bytes 1572872 | tf_op jit(solution)/shard_map/ppermute | solution.py:804
  153.0 14.0 %collective-permute-start.45 = (bf16[128,1024]{1,0:T(8,128)(2,1)S(1)}, bf16[128,1024]{1,0:T(8,128)(2,1)S(1)}, u32[]{:S(2)}, u32[]{:S(2)}) collective-permute-start(bf16[128,1024]{1,0:T(8,128)(2,1)S(1)} %get-tuple-element.232.refs_2_), channel_id=1, source_target_pairs={{0,6},{1,7},{2,4},{3,5},{4,2},{5,3},{6,0},{7,1},{8,14},{9,15},{10,... | collective-permute-start | bytes 786440 | tf_op jit(solution)/shard_map/ppermute | solution.py:770
  154.2 13.5 %collective-permute-start.43 = (bf16[128,1024]{1,0:T(8,128)(2,1)S(1)}, bf16[128,1024]{1,0:T(8,128)(2,1)S(1)}, u32[]{:S(2)}, u32[]{:S(2)}) collective-permute-start(bf16[128,1024]{1,0:T(8,128)(2,1)S(1)} %get-tuple-element.232.refs_2_), channel_id=1, source_target_pairs={{0,4},{1,5},{2,6},{3,7},{4,0},{5,1},{6,2},{7,3},{8,12},{9,13},{10,... | collective-permute-start | bytes 786440 | tf_op jit(solution)/shard_map/ppermute | solution.py:770
  155.4 12.5 %collective-permute-start.40 = (bf16[128,1024]{1,0:T(8,128)(2,1)S(1)}, bf16[128,1024]{1,0:T(8,128)(2,1)S(1)}, u32[]{:S(2)}, u32[]{:S(2)}) collective-permute-start(bf16[128,1024]{1,0:T(8,128)(2,1)S(1)} %get-tuple-element.232.refs_2_), channel_id=1, source_target_pairs={{0,2},{1,3},{2,0},{3,1},{4,6},{5,7},{6,4},{7,5},{8,10},{9,11},{10,... | collective-permute-start | bytes 786440 | tf_op jit(solution)/shard_map/ppermute | solution.py:770
  156.5 13.4 %collective-permute-start.39 = (bf16[128,1024]{1,0:T(8,128)(2,1)S(1)}, bf16[128,1024]{1,0:T(8,128)(2,1)S(1)}, u32[]{:S(2)}, u32[]{:S(2)}) collective-permute-start(bf16[128,1024]{1,0:T(8,128)(2,1)S(1)} %get-tuple-element.232.refs_2_), channel_id=1, source_target_pairs={{0,1},{1,0},{2,3},{3,2},{4,5},{5,4},{6,7},{7,6},{8,9},{9,8},{10,11... | collective-permute-start | bytes 786440 | tf_op jit(solution)/shard_map/ppermute | solution.py:770
  167.9 2.0 collective-permute-start.42
  167.9 2.0 collective-permute-start.44
  168.4 1.8 collective-permute-start.46
  168.5 19.5 %collective-permute-start.50 = (bf16[512,512]{1,0:T(8,128)(2,1)S(1)}, bf16[512,512]{1,0:T(8,128)(2,1)S(1)}, u32[]{:S(2)}, u32[]{:S(2)}) collective-permute-start(bf16[512,512]{1,0:T(8,128)(2,1)S(1)} %get-tuple-element.257), channel_id=1, source_target_pairs={{0,16},{1,17},{2,18},{3,19},{4,20},{5,21},{6,22},{7,23},{8,24},{9,... | collective-permute-start | bytes 1572872 | tf_op jit(solution)/shard_map/ppermute | solution.py:804
  170.2 26.2 %collective-permute-start.51 = (bf16[512,512]{1,0:T(8,128)(2,1)S(1)}, bf16[512,512]{1,0:T(8,128)(2,1)S(1)}, u32[]{:S(2)}, u32[]{:S(2)}) collective-permute-start(bf16[512,512]{1,0:T(8,128)(2,1)S(1)} %fold.3), channel_id=1, source_target_pairs={{0,8},{1,9},{2,10},{3,11},{4,12},{5,13},{6,14},{7,15},{8,0},{9,1},... | collective-permute-start | bytes 1572872 | tf_op jit(solution)/shard_map/ppermute | solution.py:804
  170.8 17.1 %collective-permute-start.47 = (bf16[128,1024]{1,0:T(8,128)(2,1)S(1)}, bf16[128,1024]{1,0:T(8,128)(2,1)S(1)}, u32[]{:S(2)}, u32[]{:S(2)}) collective-permute-start(bf16[128,1024]{1,0:T(8,128)(2,1)S(1)} %get-tuple-element.254), channel_id=1, source_target_pairs={{0,2},{1,3},{2,0},{3,1},{4,6},{5,7},{6,4},{7,5},{8,10},{9,11},{10,... | collective-permute-start | bytes 786440 | tf_op jit(solution)/shard_map/ppermute | solution.py:770
  172.2 16.5 %collective-permute-start.48 = (bf16[128,1024]{1,0:T(8,128)(2,1)S(1)}, bf16[128,1024]{1,0:T(8,128)(2,1)S(1)}, u32[]{:S(2)}, u32[]{:S(2)}) collective-permute-start(bf16[128,1024]{1,0:T(8,128)(2,1)S(1)} %get-tuple-element.255), channel_id=1, source_target_pairs={{0,4},{1,5},{2,6},{3,7},{4,0},{5,1},{6,2},{7,3},{8,12},{9,13},{10,... | collective-permute-start | bytes 786440 | tf_op jit(solution)/shard_map/ppermute | solution.py:770
  173.2 20.4 %collective-permute-start.49 = (bf16[128,1024]{1,0:T(8,128)(2,1)S(1)}, bf16[128,1024]{1,0:T(8,128)(2,1)S(1)}, u32[]{:S(2)}, u32[]{:S(2)}) collective-permute-start(bf16[128,1024]{1,0:T(8,128)(2,1)S(1)} %get-tuple-element.256), channel_id=1, source_target_pairs={{0,6},{1,7},{2,4},{3,5},{4,2},{5,3},{6,0},{7,1},{8,14},{9,15},{10,... | collective-permute-start | bytes 786440 | tf_op jit(solution)/shard_map/ppermute | solution.py:770
  196.4 7.7 %collective-permute-start.52 = (bf16[512,1024]{1,0:T(8,128)(2,1)S(1)}, bf16[512,1024]{1,0:T(8,128)(2,1)S(1)}, u32[]{:S(2)}, u32[]{:S(2)}) collective-permute-start(bf16[512,1024]{1,0:T(8,128)(2,1)S(1)} %get-tuple-element.259), channel_id=1, source_target_pairs={{0,1},{1,0},{2,3},{3,2},{4,5},{5,4},{6,7},{7,6},{8,9},{9,8},{10,11... | collective-permute-start | bytes 3145736 | tf_op jit(solution)/shard_map/ppermute | solution.py:770
  202.7 15.5 %collective-permute-start.53 = (bf16[16,40,384]{2,1,0:T(8,128)(2,1)S(1)}, bf16[16,40,384]{2,1,0:T(8,128)(2,1)S(1)}, u32[]{:S(2)}, u32[]{:S(2)}) collective-permute-start(bf16[16,40,384]{2,1,0:T(8,128)(2,1)S(1)} %get-tuple-element.264), channel_id=1, source_target_pairs={{0,16},{16,0},{1,17},{17,1},{2,18},{18,2},{3,19},{19,3},{4,20},{20... | collective-permute-start | bytes 1474568 | tf_op jit(solution)/shard_map/ppermute | solution.py:831
  207.9 10.2 %all-to-all-start.2 = ((bf16[8,32,512]{2,1,0:T(8,128)(2,1)}), bf16[8,32,512]{2,1,0:T(8,128)(2,1)S(1)}, u32[]{:S(2)}, u32[]{:S(2)}) async-start(bf16[8,32,512]{2,1,0:T(8,128)(2,1)} %get-tuple-element.262), calls=%async_computation.2 | async-start | bytes 524288 | tf_op jit(solution)/shard_map/all_to_all | solution.py:808
  213.9 12.3 %collective-permute-start.54 = (bf16[2,32,1024]{2,1,0:T(8,128)(2,1)S(1)}, bf16[2,32,1024]{2,1,0:T(8,128)(2,1)S(1)}, u32[]{:S(2)}, u32[]{:S(2)}) collective-permute-start(bf16[2,32,1024]{2,1,0:T(8,128)(2,1)S(1)} %get-tuple-element.270), channel_id=1, source_target_pairs={{0,16},{16,0},{1,17},{17,1},{2,18},{18,2},{3,19},{19,3},{4,20},{20... | collective-permute-start | bytes 393224 | tf_op jit(solution)/shard_map/ppermute | solution.py:831
  214.6 12.2 %collective-permute-start.55 = (bf16[128,1024]{1,0:T(8,128)(2,1)S(1)}, bf16[128,1024]{1,0:T(8,128)(2,1)}, u32[]{:S(2)}, u32[]{:S(2)}) collective-permute-start(bf16[128,1024]{1,0:T(8,128)(2,1)S(1)} %get-tuple-element.271), channel_id=1, source_target_pairs={{0,2},{1,3},{2,0},{3,1},{4,6},{5,7},{6,4},{7,5},{8,10},{9,11},{10,... | collective-permute-start | bytes 786440 | tf_op jit(solution)/shard_map/ppermute | solution.py:770
  216.6 10.3 %collective-permute-start.56 = (bf16[128,1024]{1,0:T(8,128)(2,1)S(1)}, bf16[128,1024]{1,0:T(8,128)(2,1)}, u32[]{:S(2)}, u32[]{:S(2)}) collective-permute-start(bf16[128,1024]{1,0:T(8,128)(2,1)S(1)} %get-tuple-element.272), channel_id=1, source_target_pairs={{0,4},{1,5},{2,6},{3,7},{4,0},{5,1},{6,2},{7,3},{8,12},{9,13},{10,... | collective-permute-start | bytes 786440 | tf_op jit(solution)/shard_map/ppermute | solution.py:770
  218.0 12.4 %collective-permute-start.57 = (bf16[128,1024]{1,0:T(8,128)(2,1)S(1)}, bf16[128,1024]{1,0:T(8,128)(2,1)}, u32[]{:S(2)}, u32[]{:S(2)}) collective-permute-start(bf16[128,1024]{1,0:T(8,128)(2,1)S(1)} %get-tuple-element.273), channel_id=1, source_target_pairs={{0,6},{1,7},{2,4},{3,5},{4,2},{5,3},{6,0},{7,1},{8,14},{9,15},{10,... | collective-permute-start | bytes 786440 | tf_op jit(solution)/shard_map/ppermute | solution.py:770
  220.7 34.6 %all-to-all-start.3 = ((bf16[16,40,384]{2,1,0:T(8,128)(2,1)}), bf16[16,40,384]{2,1,0:T(8,128)(2,1)S(1)}, u32[]{:S(2)}, u32[]{:S(2)}) async-start(bf16[16,40,384]{2,1,0:T(8,128)(2,1)} %fold.4), calls=%async_computation.3 | async-start | bytes 983040 | tf_op jit(solution)/shard_map/all_to_all | solution.py:1110
  232.7 19.8 %collective-permute-start.58 = (bf16[96,1024]{1,0:T(8,128)(2,1)S(1)}, bf16[96,1024]{1,0:T(8,128)(2,1)S(1)}, u32[]{:S(2)}, u32[]{:S(2)}) collective-permute-start(bf16[96,1024]{1,0:T(8,128)(2,1)S(1)} %get-tuple-element.276), channel_id=1, source_target_pairs={{0,8},{1,9},{2,10},{3,11},{4,12},{5,13},{6,14},{7,15},{8,0},{9,1},... | collective-permute-start | bytes 589832 | tf_op jit(solution)/shard_map/ppermute | solution.py:770
  236.1 19.2 %collective-permute-start.60 = (bf16[64,1024]{1,0:T(8,128)(2,1)S(1)}, bf16[64,1024]{1,0:T(8,128)(2,1)S(1)}, u32[]{:S(2)}, u32[]{:S(2)}) collective-permute-start(bf16[64,1024]{1,0:T(8,128)(2,1)S(1)} %get-tuple-element.280), channel_id=1, source_target_pairs={{0,8},{1,9},{2,10},{3,11},{4,12},{5,13},{6,14},{7,15},{8,0},{9,1},... | collective-permute-start | bytes 393224 | tf_op jit(solution)/shard_map/ppermute | solution.py:770
  252.5 2.8 %collective-permute-start.59 = (bf16[32,1024]{1,0:T(8,128)(2,1)S(1)}, bf16[32,1024]{1,0:T(8,128)(2,1)S(1)}, u32[]{:S(2)}, u32[]{:S(2)}) collective-permute-start(bf16[32,1024]{1,0:T(8,128)(2,1)S(1)} %fusion), channel_id=1, source_target_pairs={{0,0},{8,1},{16,2},{24,3},{1,4},{9,5},{17,6},{25,7},{2,8},{10,9},{... | collective-permute-start | bytes 196616 | tf_op jit(solution)/shard_map/ppermute | solution.py:1139
  (13 other events, 83.3 us)

commit v2 on v1

--- a/solution.py
+++ b/solution.py
@@ -53,8 +53,16 @@
         self.shape, self.dtype = array.shape, array.dtype
 
 
+class Held(Near):
+    pass
+
+
 def near(arrays):
     return [Near(a) for a in arrays]
+
+
+def held_in(arrays):
+    return [Held(a) for a in arrays]
 
 
 class Place:
@@ -70,6 +78,11 @@
     here = pl.BlockSpec(memory_space=pltpu.HBM)
     anywhere = pl.BlockSpec(memory_space=pl.ANY)
     scalars = pl.BlockSpec(memory_space=pltpu.SMEM)
+    inside = pl.BlockSpec(memory_space=pltpu.VMEM)
+
+    def spec(a):
+        return inside if isinstance(a, Held) else anywhere if isinstance(a, Near) else here
+
     nbytes = sum(a.shape[0] * a.shape[1] * a.dtype.itemsize for a in list(args) + list(outs))
 
     def body(*refs):
@@ -82,8 +95,8 @@
     return pl.pallas_call(
         body,
         out_shape=tuple(o.array if isinstance(o, Near) else pltpu.HBM(o.shape, o.dtype) for o in outs),
-        in_specs=[scalars] * len(lengths) + [anywhere if isinstance(a, Near) else here for a in args],
-        out_specs=tuple(anywhere if isinstance(o, Near) else here for o in outs),
+        in_specs=[scalars] * len(lengths) + [spec(a) for a in args],
+        out_specs=tuple(spec(o) for o in outs),
         scratch_shapes=list(scratch) + [pltpu.SemaphoreType.DMA((sems,))],
         compiler_params=pltpu.CompilerParams(vmem_limit_bytes=(limit or 8 * grid[2]) * MIB),
         cost_estimate=pl.CostEstimate(flops=int(flops), bytes_accessed=int(nbytes), transcendentals=0),
@@ -296,23 +309,18 @@
 
 def mid_kernel(count, place, *refs):
     ins, x, vec = refs[:count], refs[count], refs[count + 1]
-    y_out, h_out = refs[count + 2 : count + 4]
-    held = refs[count + 4 : 2 * count + 4]
-    x_s, vec_s, y_s, h_s, sems = refs[2 * count + 4 :]
-    move = Mover(sems)
-    loads = [move.start(a, b) for a, b in zip(ins, held)]
-    loads += [move.start(x, x_s), move.start(vec, vec_s)]
-    for copy in loads:
-        copy.wait()
-    y = held[0][...]
+    y_out, h_out, vec_s, y_s, sems = refs[count + 2 :]
+    move = Mover(sems)
+    load = move.start(vec, vec_s)
+    y = ins[0][...]
     for i in range(1, count):
-        y = y + held[i][...].astype(f32)
-    y = x_s[...].astype(f32) + y + vec_s[4:5, :]
+        y = y + ins[i][...].astype(f32)
+    load.wait()
+    y = x[...].astype(f32) + y + vec_s[4:5, :]
     y_s[...] = y
+    move.put(y_s, y_out)
     scaled, _ = normalize(y)
-    h_s[...] = (scaled * vec_s[5:6, :] + vec_s[6:7, :]).astype(bf16)
-    move.put(h_s, h_out)
-    move.put(y_s, y_out)
+    h_out[...] = (scaled * vec_s[5:6, :] + vec_s[6:7, :]).astype(bf16)
     move.drain()
 
 
@@ -425,40 +433,24 @@
 
 
 def pair_kernel(place, keep, recv, *refs):
-    count = (len(refs) - 3) // 2
-    outs = refs[:count]
-    keep_s, recv_s = refs[count : count + 2]
-    stage, sems = refs[count + 2 : 2 * count + 2], refs[2 * count + 2]
+    *outs, keep_s, sems = refs
     move = Mover(sems)
     rows = outs[0].shape[0]
-    order = list(range(1, count)) + [0]
+    order = list(range(1, len(outs))) + [0]
     loads = {}
     for i in order:
         here = slice(i * rows, (i + 1) * rows)
-        loads[i] = (
-            move.start(keep.at[here, :], keep_s.at[here, :]),
-            move.start(recv.at[here, :], recv_s.at[here, :]),
-        )
+        loads[i] = move.start(keep.at[here, :], keep_s.at[here, :])
     for i in order:
         here = slice(i * rows, (i + 1) * rows)
-        for copy in loads[i]:
-            copy.wait()
-        stage[i][...] = (keep_s[here, :].astype(f32) + recv_s[here, :].astype(f32)).astype(outs[i].dtype)
-        move.put(stage[i], outs[i])
-    move.drain()
+        loads[i].wait()
+        outs[i][...] = (keep_s[here, :].astype(f32) + recv[here, :].astype(f32)).astype(outs[i].dtype)
 
 
 def fold_kernel(count, place, *refs):
-    ins, outs = refs[: 2 * count], refs[2 * count : 3 * count]
-    held, stage, sems = refs[3 * count : 5 * count], refs[5 * count : 6 * count], refs[6 * count]
-    move = Mover(sems)
-    loads = [move.start(a, b) for a, b in zip(ins, held)]
-    for i in range(count):
-        loads[i].wait()
-        loads[count + i].wait()
-        stage[i][...] = (held[i][...].astype(f32) + held[count + i][...].astype(f32)).astype(bf16)
-        move.put(stage[i], outs[i])
-    move.drain()
+    kept, got, outs = refs[:count], refs[count : 2 * count], refs[2 * count : 3 * count]
+    for a, b, out in zip(kept, got, outs):
+        out[...] = (a[...].astype(f32) + b[...].astype(f32)).astype(bf16)
 
 
 def out_kernel(count, place, *refs):
@@ -480,23 +472,20 @@
 
 
 def mid_back_kernel(count, place, *refs):
-    ins = refs[: count + 3]
-    dy1_out, da_out, small_out = refs[count + 3 : count + 6]
-    held = refs[count + 6 : 2 * count + 9]
-    dy1_s, da_s, small, sems = refs[2 * count + 9 :]
-    move = Mover(sems)
-    for copy in [move.start(a, b) for a, b in zip(ins, held)]:
-        copy.wait()
-    dh = held[0][...]
+    ins, (y_in, vec_in, dy) = refs[:count], refs[count : count + 3]
+    dy1_out, da_out, small_out, y, vec, dy1_s, small, sems = refs[count + 3 :]
+    move = Mover(sems)
+    loads = [move.start(y_in, y), move.start(vec_in, vec)]
+    dh = ins[0][...]
     for i in range(1, count):
-        dh = dh + held[i][...].astype(f32)
-    y, vec, dy = held[count : count + 3]
+        dh = dh + ins[i][...].astype(f32)
+    for copy in loads:
+        copy.wait()
     scaled, inv_std = normalize(y[...])
     dyf = dy[...].astype(f32)
     dy1 = dyf + norm_back(dh, scaled, inv_std, vec[5:6, :])
     da = dy1.astype(bf16)
-    da_s[...] = da
-    move.put(da_s, da_out)
+    da_out[...] = da
     dy1_s[...] = dy1
     move.put(dy1_s, dy1_out)
     small[0:1, :] = jnp.sum(dh * scaled, axis=0, keepdims=True)
@@ -784,12 +773,12 @@
         return call(
         grid,
             pair_kernel,
-            [keep, Near(recv)],
-            near(outs),
+            [keep, Held(recv)],
+            held_in(outs),
             "pair",
             cost(1),
-            scratch=[vmem(keep), vmem(recv)] + [vmem(o) for o in outs],
-            sems=3 * count,
+            scratch=[vmem(keep)],
+            sems=count,
         )
 
     def scatter(pieces):
@@ -812,12 +801,12 @@
         return call(
             grid,
             functools.partial(fold_kernel, len(kept)),
-            near(list(kept) + list(got)),
-            near(outs),
+            held_in(list(kept) + list(got)),
+            held_in(outs),
             "fold",
             cost(2),
-            scratch=[vmem(a) for a in list(kept) + list(got) + outs],
-            sems=3 * len(kept),
+            sems=1,
+            limit=16,
         )
 
     def spread(pieces):
@@ -939,12 +928,12 @@
     y1, h2 = call(
         grid,
         functools.partial(mid_kernel, count),
-        near(ys + [x]) + [vec],
-        [y_sds, Near(row_sds)],
+        held_in(ys + [x]) + [vec],
+        [y_sds, Held(row_sds)],
         "mid",
         cost(2),
-        scratch=[vmem(a) for a in ys + [row_sds, vec, y_sds, row_sds]],
-        sems=count + 4,
+        scratch=[vmem(vec), vmem(y_sds)],
+        sems=2,
     )
     h2_even = gather_direct(h2)
 
@@ -1007,12 +996,12 @@
     dy1, da, small_two = call(
         grid,
         functools.partial(mid_back_kernel, count),
-        near(dh2) + [after(y1, ffn_parts[0], out_keep), vec, Near(dy)],
-        outs[:1] + near(outs[1:2]) + outs[2:],
+        held_in(dh2) + [after(y1, ffn_parts[0], out_keep), vec, Held(dy)],
+        outs[:1] + held_in(outs[1:2]) + outs[2:],
         "mid_back",
         cost(3),
-        scratch=[vmem(a) for a in dh2 + [y1, vec, row_sds] + outs],
-        sems=count + 6,
+        scratch=[vmem(y1), vmem(vec), vmem(y_sds), vmem(small_sds)],
+        sems=4,
     )
     da_even = gather_direct(da)
     bit = groups // 2

time: 262 us -> 261 us (level)
  transfers between devices with their start and end apart: 65 -> 65, of which waited for: 27 -> 28; matrix products, arithmetic and copies ran while one was open for 0% -> 0% of each run, Pallas kernels for 25% -> 24%
where the time goes in v2:
time: 261 us; the launch traced here: 256 us
  waiting for transfers between devices  99.3 us (38%)
  Pallas kernels  79.3 us (30%)
  starting transfers between devices  73 us (28%)
    pallas_call x25, Pallas kernels, call(): pl.pallas_call(body, out_shape=tuple((o.array if isinstance(o, Near) else...  79.3 us
    ppermute x49, waiting for transfers between devices, xor(): return lax.ppermute(value, 'seq', [(i, i ^ bit) for i in range(seq_size)])  73.8 us
    ppermute x49, starting transfers between devices, xor(): return lax.ppermute(value, 'seq', [(i, i ^ bit) for i in range(seq_size)])  42 us
    ppermute x6, waiting for transfers between devices, to_group(): return lax.ppermute(value, both, pairs)  16.2 us
    all_to_all x1, waiting for transfers between devices, on_device(): attn_w = lax.all_to_all(packed, 'seq', 0, 0, tiled=True)  9.27 us
    all_to_all x1, starting transfers between devices, on_device(): attn_w = lax.all_to_all(packed, 'seq', 0, 0, tiled=True)  7.4 us
    all_to_all x2, starting transfers between devices, members(): lax.all_to_all(value, 'seq', 0, 0, tiled=True, axis_index_groups=index)  6.85 us
    all_to_all x1, starting transfers between devices, on_device(): back = lax.all_to_all(attn_sum, 'seq', 0, 0, tiled=True)  5.47 us
  transfers between devices with their start and end apart: 65, of which 28 were waited for; matrix products, arithmetic and copies ran while one was open for 0% of the time, Pallas kernels for 24%

profile of v2, /device:TPU:0, one launch (start us, length us, event | category | flops | bytes accessed | tf_op | source)
XLA Modules:
  0.0 255.6 jit_solution(17060662090783627588)
XLA Ops:
  1.8 1.9 pack.1
  3.8 7.4 %all-to-all-start = ((bf16[16,40,384]{2,1,0:T(8,128)(2,1)}), bf16[16,40,384]{2,1,0:T(8,128)(2,1)S(1)}, u32[]{:S(2)}, u32[]{:S(2)}) async-start(bf16[16,40,384]{2,1,0:T(8,128)(2,1)} %pack.1), calls=%async_computation | async-start | bytes 983040 | tf_op jit(solution)/shard_map/all_to_all | solution.py:861
  11.2 2.8 %collective-permute-start.1 = (bf16[64,1024]{1,0:T(8,128)(2,1)S(1)}, bf16[64,1024]{1,0:T(8,128)(2,1)S(1)}, u32[]{:S(2)}, u32[]{:S(2)}) collective-permute-start(bf16[64,1024]{1,0:T(8,128)(2,1)S(1)} %get-tuple-element.158), channel_id=1, source_target_pairs={{0,8},{1,9},{2,10},{3,11},{4,12},{5,13},{6,14},{7,15},{8,0},{9,1},... | collective-permute-start | bytes 393224 | tf_op jit(solution)/shard_map/ppermute | solution.py:759
  14.0 1.5 collective-permute-start.4
  16.1 9.3 %all-to-all-done.refs_10_ = bf16[16,40,384]{2,1,0:T(8,128)(2,1)S(1)} async-done(((bf16[16,40,384]{2,1,0:T(8,128)(2,1)}), bf16[16,40,384]{2,1,0:T(8,128)(2,1)S(1)}, u32[]{:S(2)}, u32[]{:S(2)}) %all-to-all-start) | async-done | bytes 491552 | tf_op jit(solution)/shard_map/all_to_all | solution.py:861
  25.4 1.5 collective-permute-start.2
  26.9 5.8 %collective-permute-done.1 = bf16[64,1024]{1,0:T(8,128)(2,1)S(1)} collective-permute-done((bf16[64,1024]{1,0:T(8,128)(2,1)S(1)}, bf16[64,1024]{1,0:T(8,128)(2,1)S(1)}, u32[]{:S(2)}, u32[]{:S(2)}) %collective-permute-start.1) | collective-permute-done | bytes 131104 | tf_op jit(solution)/shard_map/ppermute | solution.py:759
  32.9 2.9 %collective-permute-start.9 = (bf16[128,1024]{1,0:T(8,128)(2,1)S(1)}, bf16[128,1024]{1,0:T(8,128)(2,1)S(1)}, u32[]{:S(2)}, u32[]{:S(2)}) collective-permute-start(bf16[128,1024]{1,0:T(8,128)(2,1)S(1)} %constant_dynamic-update-slice_fusion.2.refs_2_.refs_4_), channel_id=1, source_target_pairs={{0,4},{1,5},{2,6},{3,7},{4,0},{5,1},{6,2},{7,3},{8,12},{9,13},{10,... | collective-permute-start | bytes 786440 | tf_op jit(solution)/shard_map/ppermute | solution.py:759
  36.3 1.7 pack_up.1
  38.1 3.4 %all-to-all-start.1 = ((bf16[8,32,512]{2,1,0:T(8,128)(2,1)}), bf16[8,32,512]{2,1,0:T(8,128)(2,1)S(1)}, u32[]{:S(2)}, u32[]{:S(2)}) async-start(bf16[8,32,512]{2,1,0:T(8,128)(2,1)} %pack_up.1), calls=%async_computation.1 | async-start | bytes 524288 | tf_op jit(solution)/shard_map/all_to_all | solution.py:797
  41.5 1.2 collective-permute-start.5
  42.7 7.4 %collective-permute-done.5.refs_13_ = bf16[2,32,1024]{2,1,0:T(8,128)(2,1)S(1)} collective-permute-done((bf16[2,32,1024]{2,1,0:T(8,128)(2,1)S(1)}, bf16[2,32,1024]{2,1,0:T(8,128)(2,1)S(1)}, u32[]{:S(2)}, u32[]{:S(2)}) %collective-permute-start.5) | collective-permute-done | bytes 131104 | tf_op jit(solution)/shard_map/ppermute | solution.py:759
  50.8 3.4 %collective-permute-start = (bf16[64,1024]{1,0:T(8,128)(2,1)S(1)}, bf16[64,1024]{1,0:T(8,128)(2,1)S(1)}, u32[]{:S(2)}, u32[]{:S(2)}) collective-permute-start(bf16[64,1024]{1,0:T(8,128)(2,1)S(1)} %get-tuple-element.163), channel_id=1, source_target_pairs={{0,8},{1,9},{2,10},{3,11},{4,12},{5,13},{6,14},{7,15},{8,0},{9,1},... | collective-permute-start | bytes 393224 | tf_op jit(solution)/shard_map/ppermute | solution.py:759
  55.3 4.7 %collective-permute-done = bf16[64,1024]{1,0:T(8,128)(2,1)S(1)} collective-permute-done((bf16[64,1024]{1,0:T(8,128)(2,1)S(1)}, bf16[64,1024]{1,0:T(8,128)(2,1)S(1)}, u32[]{:S(2)}, u32[]{:S(2)}) %collective-permute-start) | collective-permute-done | bytes 131104 | tf_op jit(solution)/shard_map/ppermute | solution.py:759
  60.3 3.1 %collective-permute-start.17 = (bf16[128,1024]{1,0:T(8,128)(2,1)S(1)}, bf16[128,1024]{1,0:T(8,128)(2,1)S(1)}, u32[]{:S(2)}, u32[]{:S(2)}) collective-permute-start(bf16[128,1024]{1,0:T(8,128)(2,1)S(1)} %constant_dynamic-update-slice_fusion.refs_0_.refs_6_), channel_id=1, source_target_pairs={{0,6},{1,7},{2,4},{3,5},{4,2},{5,3},{6,0},{7,1},{8,14},{9,15},{10,... | collective-permute-start | bytes 786440 | tf_op jit(solution)/shard_map/ppermute | solution.py:759
  64.1 1.5 collective-permute-start.14
  65.6 12.8 %first.1 = (bf16[1024,1024]{1,0:T(8,128)(2,1)}, bf16[1024,1024]{1,0:T(8,128)(2,1)}, bf16[1024,384]{1,0:T(8,128)(2,1)}, bf16[1024,128]{1,0:T(8,128)(2,1)}, f32[2,...) custom-call(s32[2]{0:T(128)S(1)} %copy-done, ...), custom_call_target="tpu_custom_call" | custom-call | flops 19549999104 | bytes 10531584 | tf_op jit(solution)/shard_map/first/pallas_call | solution.py:95
  78.4 4.5 %collective-permute-done.13.refs_9_ = bf16[512,512]{1,0:T(8,128)(2,1)S(1)} collective-permute-done((bf16[512,512]{1,0:T(8,128)(2,1)S(1)}, bf16[512,512]{1,0:T(8,128)(2,1)S(1)}, u32[]{:S(2)}, u32[]{:S(2)}) %collective-permute-start.13) | collective-permute-done | bytes 524320 | tf_op jit(solution)/shard_map/ppermute | solution.py:793
  83.7 2.7 %collective-permute-done.18.refs_1_ = bf16[512,1024]{1,0:T(8,128)(2,1)S(1)} collective-permute-done((bf16[512,1024]{1,0:T(8,128)(2,1)S(1)}, bf16[512,1024]{1,0:T(8,128)(2,1)S(1)}, u32[]{:S(2)}, u32[]{:S(2)}) %collective-permute-start.18) | collective-permute-done | bytes 1048608 | tf_op jit(solution)/shard_map/ppermute | solution.py:759
  86.4 1.3 pair.4
  87.7 1.5 collective-permute-start.19
  89.2 2.0 collective-permute-start.21
  91.8 4.3 %collective-permute-done.19.refs_1_ = bf16[128,1024]{1,0:T(8,128)(2,1)S(1)} collective-permute-done((bf16[128,1024]{1,0:T(8,128)(2,1)S(1)}, bf16[128,1024]{1,0:T(8,128)(2,1)S(1)}, u32[]{:S(2)}, u32[]{:S(2)}) %collective-permute-start.19) | collective-permute-done | bytes 262176 | tf_op jit(solution)/shard_map/ppermute | solution.py:759
  96.1 2.3 collective-permute-done.20.refs_2_
  98.4 4.5 %collective-permute-done.21.refs_3_ = bf16[128,1024]{1,0:T(8,128)(2,1)S(1)} collective-permute-done((bf16[128,1024]{1,0:T(8,128)(2,1)S(1)}, bf16[128,1024]{1,0:T(8,128)(2,1)S(1)}, u32[]{:S(2)}, u32[]{:S(2)}) %collective-permute-start.21) | collective-permute-done | bytes 262176 | tf_op jit(solution)/shard_map/ppermute | solution.py:759
  102.9 1.6 mid.1
  104.5 1.3 collective-permute-start.32
  105.8 1.7 collective-permute-start.30
  108.1 4.0 %down_back.1 = (bf16[1024,1024]{1,0:T(8,128)(2,1)}, f32[1024,512]{1,0:T(8,128)}, bf16[1024,512]{1,0:T(8,128)(2,1)}, bf16[512,1024]{1,0:T(8,128)(2,1)}) custom-call(bf16[128,1024]{1,0:T(8,128)(2,1)S(1)} %constant_dynamic-update-slice_fusion.refs_0_.refs_6_, bf16[128,1024]{1,0:T(8,128)(2,1)S(1)} %collective-permute-done.24.refs_1_, ...), custom_call_target="tpu_custom_call" | custom-call | flops 5750000128 | bytes 10485760 | tf_op jit(solution)/shard_map/down_back/pallas_call | solution.py:95
  112.1 2.6 %collective-permute-done.32.refs_6_ = bf16[128,1024]{1,0:T(8,128)(2,1)S(1)} collective-permute-done((bf16[128,1024]{1,0:T(8,128)(2,1)S(1)}, bf16[128,1024]{1,0:T(8,128)(2,1)S(1)}, u32[]{:S(2)}, u32[]{:S(2)}) %collective-permute-start.32) | collective-permute-done | bytes 262176 | tf_op jit(solution)/shard_map/ppermute | solution.py:759
  114.6 5.2 %collective-permute-done.30.refs_4_ = bf16[128,1024]{1,0:T(8,128)(2,1)S(1)} collective-permute-done((bf16[128,1024]{1,0:T(8,128)(2,1)S(1)}, bf16[128,1024]{1,0:T(8,128)(2,1)S(1)}, u32[]{:S(2)}, u32[]{:S(2)}) %collective-permute-start.30) | collective-permute-done | bytes 262176 | tf_op jit(solution)/shard_map/ppermute | solution.py:759
  122.2 7.7 %ffn.1 = (bf16[1024,1024]{1,0:T(8,128)(2,1)}, bf16[1024,512]{1,0:T(8,128)(2,1)}, bf16[1024,512]{1,0:T(8,128)(2,1)}, bf16[512,1024]{1,0:T(8,128)(2,1)}, bf16[512,1024]{1,0:T(8,128)(2,1)S(1)}, /*index=5*/f32[1,512]{1,0:T(1,128)}) custom-call(bf16[128,1024]{1,0:T(8,128)(2,1)S(1)} %get-tuple-element.192.refs_0_, ...), custom_call_target="tpu_custom_call" | custom-call | flops 10350000128 | bytes 11538432 | tf_op jit(solution)/shard_map/ffn/pallas_call | solution.py:95
  130.0 2.5 collective-permute-done.34.refs_1_
  132.6 1.3 pair.5
  133.9 1.5 collective-permute-start.35
  135.6 1.8 collective-permute-start.37
  137.4 5.8 %ffn_grads.1 = (f32[512,512]{1,0:T(8,128)}, bf16[512,512]{1,0:T(8,128)(2,1)S(1)}, bf16[512,512]{1,0:T(8,128)(2,1)S(1)}, bf16[512,512]{1,0:T(8,128)(2,1)S(1)}) custom-call(bf16[1024,1024]{1,0:T(8,128)(2,1)} %get-tuple-element.215.refs_0_, bf16[1024,512]{1,0:T(8,128)(2,1)} %get-tuple-element.216.refs_1_, bf16[1024,1024]{1,0:T(8,128)(2,1)} %get-tuple-element.217.refs_2_, ...), custom_call_target="tpu_custom_call" | custom-call | bytes 8912896 | tf_op jit(solution)/shard_map/ffn_grads/pallas_call | solution.py:95
  143.3 4.1 %down.1 = (bf16[512,1024]{1,0:T(8,128)(2,1)}, bf16[512,1024]{1,0:T(8,128)(2,1)S(1)}) custom-call(bf16[1024,512]{1,0:T(8,128)(2,1)} %get-tuple-element.207.refs_0_.refs_3_, bf16[512,1024]{1,0:T(8,128)(2,1)} %get-tuple-element.208.refs_1_), custom_call_target="tpu_custom_call" | custom-call | flops 4600000000 | bytes 4194304 | tf_op jit(solution)/shard_map/down/pallas_call | solution.py:95
  147.4 1.7 collective-permute-done.37.refs_3_
  149.1 2.3 mid_back.1
  153.2 1.3 collective-permute-start.43
  155.6 1.3 pair.6
  156.9 8.9 %collective-permute-done.41.refs_1_ = bf16[512,512]{1,0:T(8,128)(2,1)S(1)} collective-permute-done((bf16[512,512]{1,0:T(8,128)(2,1)S(1)}, bf16[512,512]{1,0:T(8,128)(2,1)S(1)}, u32[]{:S(2)}, u32[]{:S(2)}) %collective-permute-start.41) | collective-permute-done | bytes 524320 | tf_op jit(solution)/shard_map/ppermute | solution.py:793
  167.5 1.5 collective-permute-start.50
  169.9 1.4 collective-permute-start.47
  173.4 13.6 %attend_back.1 = (bf16[1024,384]{1,0:T(8,128)(2,1)}, bf16[512,1024]{1,0:T(8,128)(2,1)}, bf16[512,1024]{1,0:T(8,128)(2,1)S(1)}, f32[1,384]{1,0:T(1,128)}, bf16[1024,1024]{1,0:T(8,128)(2,1)}) custom-call(s32[2]{0:T(128)S(1)} %copy-done, s32[4]{0:T(128)S(1)} %copy-done.1, bf16[128,1024]{1,0:T(8,128)(2,1)S(1)} %get-tuple-element.232.refs_2_, ...), custom_call_target="tpu_custom_call" | custom-call | bytes 8922624 | tf_op jit(solution)/shard_map/attend_back/pallas_call | solution.py:95
  187.9 4.8 %collective-permute-done.49.refs_3_ = bf16[128,1024]{1,0:T(8,128)(2,1)S(1)} collective-permute-done((bf16[128,1024]{1,0:T(8,128)(2,1)S(1)}, bf16[128,1024]{1,0:T(8,128)(2,1)S(1)}, u32[]{:S(2)}, u32[]{:S(2)}) %collective-permute-start.49) | collective-permute-done | bytes 262176 | tf_op jit(solution)/shard_map/ppermute | solution.py:759
  192.7 2.8 %collective-permute-done.51.refs_2_ = bf16[512,512]{1,0:T(8,128)(2,1)S(1)} collective-permute-done((bf16[512,512]{1,0:T(8,128)(2,1)S(1)}, bf16[512,512]{1,0:T(8,128)(2,1)S(1)}, u32[]{:S(2)}, u32[]{:S(2)}) %collective-permute-start.51) | collective-permute-done | bytes 524320 | tf_op jit(solution)/shard_map/ppermute | solution.py:793
  195.5 5.5 %attn_grads.1 = (bf16[16,40,384]{2,1,0:T(8,128)(2,1)S(1)}, bf16[16,40,384]{2,1,0:T(8,128)(2,1)S(1)}) custom-call(bf16[1024,384]{1,0:T(8,128)(2,1)} %get-tuple-element.244.refs_0_, bf16[1024,1024]{1,0:T(8,128)(2,1)} %get-tuple-element.245.refs_1_, bf16[1024,384]{1,0:T(8,128)(2,1)} %get-tuple-element.243.refs_13_.refs_2_, ...), custom_call_target="tpu_custom_call" | custom-call | flops 6899999744 | bytes 5789696 | tf_op jit(solution)/shard_map/attn_grads/pallas_call | solution.py:95
  201.7 1.4 collective-permute-start.53
  203.1 1.3 pair.7
  204.4 2.4 ffn_sum.1
  206.9 3.4 %all-to-all-start.2 = ((bf16[8,32,512]{2,1,0:T(8,128)(2,1)}), bf16[8,32,512]{2,1,0:T(8,128)(2,1)S(1)}, u32[]{:S(2)}, u32[]{:S(2)}) async-start(bf16[8,32,512]{2,1,0:T(8,128)(2,1)} %get-tuple-element.262), calls=%async_computation.2 | async-start | bytes 524288 | tf_op jit(solution)/shard_map/all_to_all | solution.py:797
  210.3 2.6 %out_grads.1 = (bf16[2,32,1024]{2,1,0:T(8,128)(2,1)S(1)}, bf16[2,32,1024]{2,1,0:T(8,128)(2,1)S(1)}) custom-call(bf16[1024,1024]{1,0:T(8,128)(2,1)} %get-tuple-element.265.refs_0_, bf16[1024,128]{1,0:T(8,128)(2,1)} %get-tuple-element.267.refs_1_), custom_call_target="tpu_custom_call" | custom-call | flops 2300000000 | bytes 2359552 | tf_op jit(solution)/shard_map/out_grads/pallas_call | solution.py:95
  213.6 1.9 collective-permute-start.55
  215.5 1.5 collective-permute-start.56
  219.0 5.5 %all-to-all-start.3 = ((bf16[16,40,384]{2,1,0:T(8,128)(2,1)}), bf16[16,40,384]{2,1,0:T(8,128)(2,1)S(1)}, u32[]{:S(2)}, u32[]{:S(2)}) async-start(bf16[16,40,384]{2,1,0:T(8,128)(2,1)} %fold.4), calls=%async_computation.3 | async-start | bytes 983040 | tf_op jit(solution)/shard_map/all_to_all | solution.py:1099
  224.8 4.5 %collective-permute-done.57.refs_3_ = bf16[128,1024]{1,0:T(8,128)(2,1)} collective-permute-done((bf16[128,1024]{1,0:T(8,128)(2,1)S(1)}, bf16[128,1024]{1,0:T(8,128)(2,1)}, u32[]{:S(2)}, u32[]{:S(2)}) %collective-permute-start.57) | collective-permute-done | bytes 262176 | tf_op jit(solution)/shard_map/ppermute | solution.py:759
  229.4 2.3 last.1
  231.6 3.6 %collective-permute-start.58 = (bf16[96,1024]{1,0:T(8,128)(2,1)S(1)}, bf16[96,1024]{1,0:T(8,128)(2,1)S(1)}, u32[]{:S(2)}, u32[]{:S(2)}) collective-permute-start(bf16[96,1024]{1,0:T(8,128)(2,1)S(1)} %get-tuple-element.276), channel_id=1, source_target_pairs={{0,8},{1,9},{2,10},{3,11},{4,12},{5,13},{6,14},{7,15},{8,0},{9,1},... | collective-permute-start | bytes 589832 | tf_op jit(solution)/shard_map/ppermute | solution.py:759
  235.3 1.7 out.1
  237.1 13.7 %collective-permute-done.58.refs_6_ = bf16[96,1024]{1,0:T(8,128)(2,1)S(1)} collective-permute-done((bf16[96,1024]{1,0:T(8,128)(2,1)S(1)}, bf16[96,1024]{1,0:T(8,128)(2,1)S(1)}, u32[]{:S(2)}, u32[]{:S(2)}) %collective-permute-start.58) | collective-permute-done | bytes 196640 | tf_op jit(solution)/shard_map/ppermute | solution.py:759
  251.5 2.1 collective-permute-done.60.refs_4_
  253.6 1.8 unpack.1
  (121 shorter events, 22.8 us)
Async XLA Ops:
  3.8 21.7 %all-to-all-start = ((bf16[16,40,384]{2,1,0:T(8,128)(2,1)}), bf16[16,40,384]{2,1,0:T(8,128)(2,1)S(1)}, u32[]{:S(2)}, u32[]{:S(2)}) async-start(bf16[16,40,384]{2,1,0:T(8,128)(2,1)} %pack.1), calls=%async_computation | async-start | bytes 983040 | tf_op jit(solution)/shard_map/all_to_all | solution.py:861
  11.2 21.6 %collective-permute-start.1 = (bf16[64,1024]{1,0:T(8,128)(2,1)S(1)}, bf16[64,1024]{1,0:T(8,128)(2,1)S(1)}, u32[]{:S(2)}, u32[]{:S(2)}) collective-permute-start(bf16[64,1024]{1,0:T(8,128)(2,1)S(1)} %get-tuple-element.158), channel_id=1, source_target_pairs={{0,8},{1,9},{2,10},{3,11},{4,12},{5,13},{6,14},{7,15},{8,0},{9,1},... | collective-permute-start | bytes 393224 | tf_op jit(solution)/shard_map/ppermute | solution.py:759
  14.0 21.8 %collective-permute-start.4 = (bf16[32,1024]{1,0:T(8,128)(2,1)S(1)}, bf16[32,1024]{1,0:T(8,128)(2,1)S(1)}, u32[]{:S(2)}, u32[]{:S(2)}) collective-permute-start(bf16[32,1024]{1,0:T(8,128)(2,1)S(1)} %copy-done.11), channel_id=1, source_target_pairs={{0,16},{1,24},{2,0},{3,8},{4,17},{5,25},{6,1},{7,9},{8,18},{9,26},... | collective-permute-start | bytes 196616 | tf_op jit(solution)/shard_map/ppermute | solution.py:830
  15.5 26.0 %collective-permute-start.3 = (bf16[32,1024]{1,0:T(8,128)(2,1)S(1)}, bf16[32,1024]{1,0:T(8,128)(2,1)S(1)}, u32[]{:S(2)}, u32[]{:S(2)}) collective-permute-start(bf16[32,1024]{1,0:T(8,128)(2,1)S(1)} %copy-done.11), channel_id=1, source_target_pairs={{0,0},{1,8},{2,16},{3,24},{4,1},{5,9},{6,17},{7,25},{8,2},{9,10},{... | collective-permute-start | bytes 196616 | tf_op jit(solution)/shard_map/ppermute | solution.py:830
  25.4 28.8 %collective-permute-start.2 = (bf16[16,40,384]{2,1,0:T(8,128)(2,1)S(1)}, bf16[16,40,384]{2,1,0:T(8,128)(2,1)S(1)}, u32[]{:S(2)}, u32[]{:S(2)}) collective-permute-start(bf16[16,40,384]{2,1,0:T(8,128)(2,1)S(1)} %all-to-all-done.refs_10_), channel_id=1, source_target_pairs={{0,16},{16,0},{1,17},{17,1},{2,18},{18,2},{3,19},{19,3},{4,20},{20... | collective-permute-start | bytes 1474568 | tf_op jit(solution)/shard_map/ppermute | solution.py:820
  32.8 21.4 %collective-permute-start.11 = (bf16[128,1024]{1,0:T(8,128)(2,1)S(1)}, bf16[128,1024]{1,0:T(8,128)(2,1)S(1)}, u32[]{:S(2)}, u32[]{:S(2)}) collective-permute-start(bf16[128,1024]{1,0:T(8,128)(2,1)S(1)} %constant_dynamic-update-slice_fusion.2.refs_2_.refs_4_), channel_id=1, source_target_pairs={{0,6},{1,7},{2,4},{3,5},{4,2},{5,3},{6,0},{7,1},{8,14},{9,15},{10,... | collective-permute-start | bytes 786440 | tf_op jit(solution)/shard_map/ppermute | solution.py:759
  32.9 21.4 %collective-permute-start.9 = (bf16[128,1024]{1,0:T(8,128)(2,1)S(1)}, bf16[128,1024]{1,0:T(8,128)(2,1)S(1)}, u32[]{:S(2)}, u32[]{:S(2)}) collective-permute-start(bf16[128,1024]{1,0:T(8,128)(2,1)S(1)} %constant_dynamic-update-slice_fusion.2.refs_2_.refs_4_), channel_id=1, source_target_pairs={{0,4},{1,5},{2,6},{3,7},{4,0},{5,1},{6,2},{7,3},{8,12},{9,13},{10,... | collective-permute-start | bytes 786440 | tf_op jit(solution)/shard_map/ppermute | solution.py:759
  35.8 18.4 %collective-permute-start.7 = (bf16[128,1024]{1,0:T(8,128)(2,1)S(1)}, bf16[128,1024]{1,0:T(8,128)(2,1)S(1)}, u32[]{:S(2)}, u32[]{:S(2)}) collective-permute-start(bf16[128,1024]{1,0:T(8,128)(2,1)S(1)} %constant_dynamic-update-slice_fusion.2.refs_2_.refs_4_), channel_id=1, source_target_pairs={{0,2},{1,3},{2,0},{3,1},{4,6},{5,7},{6,4},{7,5},{8,10},{9,11},{10,... | collective-permute-start | bytes 786440 | tf_op jit(solution)/shard_map/ppermute | solution.py:759
  38.1 22.0 %all-to-all-start.1 = ((bf16[8,32,512]{2,1,0:T(8,128)(2,1)}), bf16[8,32,512]{2,1,0:T(8,128)(2,1)S(1)}, u32[]{:S(2)}, u32[]{:S(2)}) async-start(bf16[8,32,512]{2,1,0:T(8,128)(2,1)} %pack_up.1), calls=%async_computation.1 | async-start | bytes 524288 | tf_op jit(solution)/shard_map/all_to_all | solution.py:797
  41.5 8.6 %collective-permute-start.5 = (bf16[2,32,1024]{2,1,0:T(8,128)(2,1)S(1)}, bf16[2,32,1024]{2,1,0:T(8,128)(2,1)S(1)}, u32[]{:S(2)}, u32[]{:S(2)}) collective-permute-start(bf16[2,32,1024]{2,1,0:T(8,128)(2,1)S(1)} %pad_maximum_fusion.refs_12_), channel_id=1, source_target_pairs={{0,8},{1,9},{2,10},{3,11},{4,12},{5,13},{6,14},{7,15},{8,0},{9,1},... | collective-permute-start | bytes 393224 | tf_op jit(solution)/shard_map/ppermute | solution.py:759
  50.8 9.2 %collective-permute-start = (bf16[64,1024]{1,0:T(8,128)(2,1)S(1)}, bf16[64,1024]{1,0:T(8,128)(2,1)S(1)}, u32[]{:S(2)}, u32[]{:S(2)}) collective-permute-start(bf16[64,1024]{1,0:T(8,128)(2,1)S(1)} %get-tuple-element.163), channel_id=1, source_target_pairs={{0,8},{1,9},{2,10},{3,11},{4,12},{5,13},{6,14},{7,15},{8,0},{9,1},... | collective-permute-start | bytes 393224 | tf_op jit(solution)/shard_map/ppermute | solution.py:759
  54.2 6.1 %collective-permute-start.6 = (bf16[128,1024]{1,0:T(8,128)(2,1)S(1)}, bf16[128,1024]{1,0:T(8,128)(2,1)S(1)}, u32[]{:S(2)}, u32[]{:S(2)}) collective-permute-start(bf16[128,1024]{1,0:T(8,128)(2,1)S(1)} %constant_dynamic-update-slice_fusion.2.refs_2_.refs_4_), channel_id=1, source_target_pairs={{0,1},{1,0},{2,3},{3,2},{4,5},{5,4},{6,7},{7,6},{8,9},{9,8},{10,11... | collective-permute-start | bytes 786440 | tf_op jit(solution)/shard_map/ppermute | solution.py:759
  54.3 6.0 %collective-permute-start.8 = (bf16[128,1024]{1,0:T(8,128)(2,1)S(1)}, bf16[128,1024]{1,0:T(8,128)(2,1)}, u32[]{:S(2)}, u32[]{:S(2)}) collective-permute-start(bf16[128,1024]{1,0:T(8,128)(2,1)S(1)} %collective-permute-done.7.refs_4_), channel_id=1, source_target_pairs={{0,1},{1,0},{2,3},{3,2},{4,5},{5,4},{6,7},{7,6},{8,9},{9,8},{10,11... | collective-permute-start | bytes 786440 | tf_op jit(solution)/shard_map/ppermute | solution.py:759
  54.8 5.5 %collective-permute-start.10 = (bf16[128,1024]{1,0:T(8,128)(2,1)S(1)}, bf16[128,1024]{1,0:T(8,128)(2,1)}, u32[]{:S(2)}, u32[]{:S(2)}) collective-permute-start(bf16[128,1024]{1,0:T(8,128)(2,1)S(1)} %collective-permute-done.9.refs_6_), channel_id=1, source_target_pairs={{0,1},{1,0},{2,3},{3,2},{4,5},{5,4},{6,7},{7,6},{8,9},{9,8},{10,11... | collective-permute-start | bytes 786440 | tf_op jit(solution)/shard_map/ppermute | solution.py:759
  54.9 5.4 %collective-permute-start.12 = (bf16[128,1024]{1,0:T(8,128)(2,1)S(1)}, bf16[128,1024]{1,0:T(8,128)(2,1)}, u32[]{:S(2)}, u32[]{:S(2)}) collective-permute-start(bf16[128,1024]{1,0:T(8,128)(2,1)S(1)} %collective-permute-done.11.refs_8_), channel_id=1, source_target_pairs={{0,1},{1,0},{2,3},{3,2},{4,5},{5,4},{6,7},{7,6},{8,9},{9,8},{10,11... | collective-permute-start | bytes 786440 | tf_op jit(solution)/shard_map/ppermute | solution.py:759
  60.2 22.7 %collective-permute-start.13 = (bf16[512,512]{1,0:T(8,128)(2,1)S(1)}, bf16[512,512]{1,0:T(8,128)(2,1)S(1)}, u32[]{:S(2)}, u32[]{:S(2)}) collective-permute-start(bf16[512,512]{1,0:T(8,128)(2,1)S(1)} %join.1.refs_8_), channel_id=1, source_target_pairs={{0,8},{1,9},{2,10},{3,11},{4,12},{5,13},{6,14},{7,15},{8,0},{9,1},... | collective-permute-start | bytes 1572872 | tf_op jit(solution)/shard_map/ppermute | solution.py:793
  60.3 22.5 %collective-permute-start.17 = (bf16[128,1024]{1,0:T(8,128)(2,1)S(1)}, bf16[128,1024]{1,0:T(8,128)(2,1)S(1)}, u32[]{:S(2)}, u32[]{:S(2)}) collective-permute-start(bf16[128,1024]{1,0:T(8,128)(2,1)S(1)} %constant_dynamic-update-slice_fusion.refs_0_.refs_6_), channel_id=1, source_target_pairs={{0,6},{1,7},{2,4},{3,5},{4,2},{5,3},{6,0},{7,1},{8,14},{9,15},{10,... | collective-permute-start | bytes 786440 | tf_op jit(solution)/shard_map/ppermute | solution.py:759
  63.4 20.3 %collective-permute-start.16 = (bf16[128,1024]{1,0:T(8,128)(2,1)S(1)}, bf16[128,1024]{1,0:T(8,128)(2,1)S(1)}, u32[]{:S(2)}, u32[]{:S(2)}) collective-permute-start(bf16[128,1024]{1,0:T(8,128)(2,1)S(1)} %constant_dynamic-update-slice_fusion.refs_0_.refs_6_), channel_id=1, source_target_pairs={{0,4},{1,5},{2,6},{3,7},{4,0},{5,1},{6,2},{7,3},{8,12},{9,13},{10,... | collective-permute-start | bytes 786440 | tf_op jit(solution)/shard_map/ppermute | solution.py:759
  63.4 20.3 %collective-permute-start.15 = (bf16[128,1024]{1,0:T(8,128)(2,1)S(1)}, bf16[128,1024]{1,0:T(8,128)(2,1)S(1)}, u32[]{:S(2)}, u32[]{:S(2)}) collective-permute-start(bf16[128,1024]{1,0:T(8,128)(2,1)S(1)} %constant_dynamic-update-slice_fusion.refs_0_.refs_6_), channel_id=1, source_target_pairs={{0,2},{1,3},{2,0},{3,1},{4,6},{5,7},{6,4},{7,5},{8,10},{9,11},{10,... | collective-permute-start | bytes 786440 | tf_op jit(solution)/shard_map/ppermute | solution.py:759
  64.1 19.6 %collective-permute-start.14 = (bf16[512,512]{1,0:T(8,128)(2,1)S(1)}, bf16[512,512]{1,0:T(8,128)(2,1)S(1)}, u32[]{:S(2)}, u32[]{:S(2)}) collective-permute-start(bf16[512,512]{1,0:T(8,128)(2,1)S(1)} %join.1.refs_8_), channel_id=1, source_target_pairs={{0,16},{1,17},{2,18},{3,19},{4,20},{5,21},{6,22},{7,23},{8,24},{9,... | collective-permute-start | bytes 1572872 | tf_op jit(solution)/shard_map/ppermute | solution.py:793
  83.7 2.7 %collective-permute-start.18 = (bf16[512,1024]{1,0:T(8,128)(2,1)S(1)}, bf16[512,1024]{1,0:T(8,128)(2,1)S(1)}, u32[]{:S(2)}, u32[]{:S(2)}) collective-permute-start(bf16[512,1024]{1,0:T(8,128)(2,1)S(1)} %get-tuple-element.186), channel_id=1, source_target_pairs={{0,1},{1,0},{2,3},{3,2},{4,5},{5,4},{6,7},{7,6},{8,9},{9,8},{10,11... | collective-permute-start | bytes 3145736 | tf_op jit(solution)/shard_map/ppermute | solution.py:759
  87.7 8.4 %collective-permute-start.19 = (bf16[128,1024]{1,0:T(8,128)(2,1)S(1)}, bf16[128,1024]{1,0:T(8,128)(2,1)S(1)}, u32[]{:S(2)}, u32[]{:S(2)}) collective-permute-start(bf16[128,1024]{1,0:T(8,128)(2,1)S(1)} %get-tuple-element.188), channel_id=1, source_target_pairs={{0,2},{1,3},{2,0},{3,1},{4,6},{5,7},{6,4},{7,5},{8,10},{9,11},{10,... | collective-permute-start | bytes 786440 | tf_op jit(solution)/shard_map/ppermute | solution.py:759
  89.2 9.2 %collective-permute-start.20 = (bf16[128,1024]{1,0:T(8,128)(2,1)S(1)}, bf16[128,1024]{1,0:T(8,128)(2,1)S(1)}, u32[]{:S(2)}, u32[]{:S(2)}) collective-permute-start(bf16[128,1024]{1,0:T(8,128)(2,1)S(1)} %get-tuple-element.189), channel_id=1, source_target_pairs={{0,4},{1,5},{2,6},{3,7},{4,0},{5,1},{6,2},{7,3},{8,12},{9,13},{10,... | collective-permute-start | bytes 786440 | tf_op jit(solution)/shard_map/ppermute | solution.py:759
  89.2 13.7 %collective-permute-start.21 = (bf16[128,1024]{1,0:T(8,128)(2,1)S(1)}, bf16[128,1024]{1,0:T(8,128)(2,1)S(1)}, u32[]{:S(2)}, u32[]{:S(2)}) collective-permute-start(bf16[128,1024]{1,0:T(8,128)(2,1)S(1)} %get-tuple-element.190), channel_id=1, source_target_pairs={{0,6},{1,7},{2,4},{3,5},{4,2},{5,3},{6,0},{7,1},{8,14},{9,15},{10,... | collective-permute-start | bytes 786440 | tf_op jit(solution)/shard_map/ppermute | solution.py:759
  91.2 16.9 %collective-permute-start.28 = (bf16[512,512]{1,0:T(8,128)(2,1)S(1)}, bf16[512,512]{1,0:T(8,128)(2,1)S(1)}, u32[]{:S(2)}, u32[]{:S(2)}) collective-permute-start(bf16[512,512]{1,0:T(8,128)(2,1)S(1)} %collective-permute-done.13.refs_9_), channel_id=1, source_target_pairs={{0,16},{1,17},{2,18},{3,19},{4,20},{5,21},{6,22},{7,23},{8,24},{9,... | collective-permute-start | bytes 1572872 | tf_op jit(solution)/shard_map/ppermute | solution.py:793
  91.8 12.7 %collective-permute-start.24 = (bf16[128,1024]{1,0:T(8,128)(2,1)S(1)}, bf16[128,1024]{1,0:T(8,128)(2,1)S(1)}, u32[]{:S(2)}, u32[]{:S(2)}) collective-permute-start(bf16[128,1024]{1,0:T(8,128)(2,1)S(1)} %constant_dynamic-update-slice_fusion.refs_0_.refs_6_), channel_id=1, source_target_pairs={{0,1},{1,0},{2,3},{3,2},{4,5},{5,4},{6,7},{7,6},{8,9},{9,8},{10,11... | collective-permute-start | bytes 786440 | tf_op jit(solution)/shard_map/ppermute | solution.py:759
  96.1 9.7 %collective-permute-start.25 = (bf16[128,1024]{1,0:T(8,128)(2,1)S(1)}, bf16[128,1024]{1,0:T(8,128)(2,1)S(1)}, u32[]{:S(2)}, u32[]{:S(2)}) collective-permute-start(bf16[128,1024]{1,0:T(8,128)(2,1)S(1)} %collective-permute-done.15.refs_2_), channel_id=1, source_target_pairs={{0,1},{1,0},{2,3},{3,2},{4,5},{5,4},{6,7},{7,6},{8,9},{9,8},{10,11... | collective-permute-start | bytes 786440 | tf_op jit(solution)/shard_map/ppermute | solution.py:759
  98.4 9.1 %collective-permute-start.26 = (bf16[128,1024]{1,0:T(8,128)(2,1)S(1)}, bf16[128,1024]{1,0:T(8,128)(2,1)S(1)}, u32[]{:S(2)}, u32[]{:S(2)}) collective-permute-start(bf16[128,1024]{1,0:T(8,128)(2,1)S(1)} %collective-permute-done.16.refs_4_), channel_id=1, source_target_pairs={{0,1},{1,0},{2,3},{3,2},{4,5},{5,4},{6,7},{7,6},{8,9},{9,8},{10,11... | collective-permute-start | bytes 786440 | tf_op jit(solution)/shard_map/ppermute | solution.py:759
  102.9 5.2 %collective-permute-start.27 = (bf16[128,1024]{1,0:T(8,128)(2,1)S(1)}, bf16[128,1024]{1,0:T(8,128)(2,1)S(1)}, u32[]{:S(2)}, u32[]{:S(2)}) collective-permute-start(bf16[128,1024]{1,0:T(8,128)(2,1)S(1)} %collective-permute-done.17.refs_6_), channel_id=1, source_target_pairs={{0,1},{1,0},{2,3},{3,2},{4,5},{5,4},{6,7},{7,6},{8,9},{9,8},{10,11... | collective-permute-start | bytes 786440 | tf_op jit(solution)/shard_map/ppermute | solution.py:759
  104.5 10.1 %collective-permute-start.32 = (bf16[128,1024]{1,0:T(8,128)(2,1)S(1)}, bf16[128,1024]{1,0:T(8,128)(2,1)S(1)}, u32[]{:S(2)}, u32[]{:S(2)}) collective-permute-start(bf16[128,1024]{1,0:T(8,128)(2,1)S(1)} %get-tuple-element.192.refs_0_), channel_id=1, source_target_pairs={{0,6},{1,7},{2,4},{3,5},{4,2},{5,3},{6,0},{7,1},{8,14},{9,15},{10,... | collective-permute-start | bytes 786440 | tf_op jit(solution)/shard_map/ppermute | solution.py:759
  105.8 14.1 %collective-permute-start.30 = (bf16[128,1024]{1,0:T(8,128)(2,1)S(1)}, bf16[128,1024]{1,0:T(8,128)(2,1)S(1)}, u32[]{:S(2)}, u32[]{:S(2)}) collective-permute-start(bf16[128,1024]{1,0:T(8,128)(2,1)S(1)} %get-tuple-element.192.refs_0_), channel_id=1, source_target_pairs={{0,4},{1,5},{2,6},{3,7},{4,0},{5,1},{6,2},{7,3},{8,12},{9,13},{10,... | collective-permute-start | bytes 786440 | tf_op jit(solution)/shard_map/ppermute | solution.py:759
  107.5 12.3 %collective-permute-start.23 = (bf16[128,1024]{1,0:T(8,128)(2,1)S(1)}, bf16[128,1024]{1,0:T(8,128)(2,1)S(1)}, u32[]{:S(2)}, u32[]{:S(2)}) collective-permute-start(bf16[128,1024]{1,0:T(8,128)(2,1)S(1)} %get-tuple-element.192.refs_0_), channel_id=1, source_target_pairs={{0,2},{1,3},{2,0},{3,1},{4,6},{5,7},{6,4},{7,5},{8,10},{9,11},{10,... | collective-permute-start | bytes 786440 | tf_op jit(solution)/shard_map/ppermute | solution.py:759
  108.1 12.3 %collective-permute-start.22 = (bf16[128,1024]{1,0:T(8,128)(2,1)S(1)}, bf16[128,1024]{1,0:T(8,128)(2,1)S(1)}, u32[]{:S(2)}, u32[]{:S(2)}) collective-permute-start(bf16[128,1024]{1,0:T(8,128)(2,1)S(1)} %get-tuple-element.192.refs_0_), channel_id=1, source_target_pairs={{0,1},{1,0},{2,3},{3,2},{4,5},{5,4},{6,7},{7,6},{8,9},{9,8},{10,11... | collective-permute-start | bytes 786440 | tf_op jit(solution)/shard_map/ppermute | solution.py:759
  119.9 1.9 collective-permute-start.31
  120.4 1.8 collective-permute-start.33
  129.8 2.7 %collective-permute-start.34 = (bf16[512,1024]{1,0:T(8,128)(2,1)S(1)}, bf16[512,1024]{1,0:T(8,128)(2,1)S(1)}, u32[]{:S(2)}, u32[]{:S(2)}) collective-permute-start(bf16[512,1024]{1,0:T(8,128)(2,1)S(1)} %get-tuple-element.205), channel_id=1, source_target_pairs={{0,1},{1,0},{2,3},{3,2},{4,5},{5,4},{6,7},{7,6},{8,9},{9,8},{10,11... | collective-permute-start | bytes 3145736 | tf_op jit(solution)/shard_map/ppermute | solution.py:759
  133.9 13.5 %collective-permute-start.35 = (bf16[128,1024]{1,0:T(8,128)(2,1)S(1)}, bf16[128,1024]{1,0:T(8,128)(2,1)S(1)}, u32[]{:S(2)}, u32[]{:S(2)}) collective-permute-start(bf16[128,1024]{1,0:T(8,128)(2,1)S(1)} %get-tuple-element.211), channel_id=1, source_target_pairs={{0,2},{1,3},{2,0},{3,1},{4,6},{5,7},{6,4},{7,5},{8,10},{9,11},{10,... | collective-permute-start | bytes 786440 | tf_op jit(solution)/shard_map/ppermute | solution.py:759
  135.4 12.0 %collective-permute-start.36 = (bf16[128,1024]{1,0:T(8,128)(2,1)S(1)}, bf16[128,1024]{1,0:T(8,128)(2,1)S(1)}, u32[]{:S(2)}, u32[]{:S(2)}) collective-permute-start(bf16[128,1024]{1,0:T(8,128)(2,1)S(1)} %get-tuple-element.212), channel_id=1, source_target_pairs={{0,4},{1,5},{2,6},{3,7},{4,0},{5,1},{6,2},{7,3},{8,12},{9,13},{10,... | collective-permute-start | bytes 786440 | tf_op jit(solution)/shard_map/ppermute | solution.py:759
  135.6 13.5 %collective-permute-start.37 = (bf16[128,1024]{1,0:T(8,128)(2,1)S(1)}, bf16[128,1024]{1,0:T(8,128)(2,1)S(1)}, u32[]{:S(2)}, u32[]{:S(2)}) collective-permute-start(bf16[128,1024]{1,0:T(8,128)(2,1)S(1)} %get-tuple-element.213), channel_id=1, source_target_pairs={{0,6},{1,7},{2,4},{3,5},{4,2},{5,3},{6,0},{7,1},{8,14},{9,15},{10,... | collective-permute-start | bytes 786440 | tf_op jit(solution)/shard_map/ppermute | solution.py:759
  151.4 4.2 %collective-permute-start.38 = (bf16[512,1024]{1,0:T(8,128)(2,1)S(1)}, bf16[512,1024]{1,0:T(8,128)(2,1)S(1)}, u32[]{:S(2)}, u32[]{:S(2)}) collective-permute-start(bf16[512,1024]{1,0:T(8,128)(2,1)S(1)} %get-tuple-element.221), channel_id=1, source_target_pairs={{0,1},{1,0},{2,3},{3,2},{4,5},{5,4},{6,7},{7,6},{8,9},{9,8},{10,11... | collective-permute-start | bytes 3145736 | tf_op jit(solution)/shard_map/ppermute | solution.py:759
  151.5 14.3 %collective-permute-start.41 = (bf16[512,512]{1,0:T(8,128)(2,1)S(1)}, bf16[512,512]{1,0:T(8,128)(2,1)S(1)}, u32[]{:S(2)}, u32[]{:S(2)}) collective-permute-start(bf16[512,512]{1,0:T(8,128)(2,1)S(1)} %get-tuple-element.228), channel_id=1, source_target_pairs={{0,16},{1,17},{2,18},{3,19},{4,20},{5,21},{6,22},{7,23},{8,24},{9,... | collective-permute-start | bytes 1572872 | tf_op jit(solution)/shard_map/ppermute | solution.py:793
  152.1 13.9 %collective-permute-start.45 = (bf16[128,1024]{1,0:T(8,128)(2,1)S(1)}, bf16[128,1024]{1,0:T(8,128)(2,1)S(1)}, u32[]{:S(2)}, u32[]{:S(2)}) collective-permute-start(bf16[128,1024]{1,0:T(8,128)(2,1)S(1)} %get-tuple-element.232.refs_2_), channel_id=1, source_target_pairs={{0,6},{1,7},{2,4},{3,5},{4,2},{5,3},{6,0},{7,1},{8,14},{9,15},{10,... | collective-permute-start | bytes 786440 | tf_op jit(solution)/shard_map/ppermute | solution.py:759
  153.2 13.5 %collective-permute-start.43 = (bf16[128,1024]{1,0:T(8,128)(2,1)S(1)}, bf16[128,1024]{1,0:T(8,128)(2,1)S(1)}, u32[]{:S(2)}, u32[]{:S(2)}) collective-permute-start(bf16[128,1024]{1,0:T(8,128)(2,1)S(1)} %get-tuple-element.232.refs_2_), channel_id=1, source_target_pairs={{0,4},{1,5},{2,6},{3,7},{4,0},{5,1},{6,2},{7,3},{8,12},{9,13},{10,... | collective-permute-start | bytes 786440 | tf_op jit(solution)/shard_map/ppermute | solution.py:759
  154.5 12.5 %collective-permute-start.40 = (bf16[128,1024]{1,0:T(8,128)(2,1)S(1)}, bf16[128,1024]{1,0:T(8,128)(2,1)S(1)}, u32[]{:S(2)}, u32[]{:S(2)}) collective-permute-start(bf16[128,1024]{1,0:T(8,128)(2,1)S(1)} %get-tuple-element.232.refs_2_), channel_id=1, source_target_pairs={{0,2},{1,3},{2,0},{3,1},{4,6},{5,7},{6,4},{7,5},{8,10},{9,11},{10,... | collective-permute-start | bytes 786440 | tf_op jit(solution)/shard_map/ppermute | solution.py:759
  155.6 13.4 %collective-permute-start.39 = (bf16[128,1024]{1,0:T(8,128)(2,1)S(1)}, bf16[128,1024]{1,0:T(8,128)(2,1)S(1)}, u32[]{:S(2)}, u32[]{:S(2)}) collective-permute-start(bf16[128,1024]{1,0:T(8,128)(2,1)S(1)} %get-tuple-element.232.refs_2_), channel_id=1, source_target_pairs={{0,1},{1,0},{2,3},{3,2},{4,5},{5,4},{6,7},{7,6},{8,9},{9,8},{10,11... | collective-permute-start | bytes 786440 | tf_op jit(solution)/shard_map/ppermute | solution.py:759
  167.0 2.0 collective-permute-start.42
  167.0 2.0 collective-permute-start.44
  167.5 1.8 collective-permute-start.46
  167.5 19.5 %collective-permute-start.50 = (bf16[512,512]{1,0:T(8,128)(2,1)S(1)}, bf16[512,512]{1,0:T(8,128)(2,1)S(1)}, u32[]{:S(2)}, u32[]{:S(2)}) collective-permute-start(bf16[512,512]{1,0:T(8,128)(2,1)S(1)} %get-tuple-element.257), channel_id=1, source_target_pairs={{0,16},{1,17},{2,18},{3,19},{4,20},{5,21},{6,22},{7,23},{8,24},{9,... | collective-permute-start | bytes 1572872 | tf_op jit(solution)/shard_map/ppermute | solution.py:793
  169.3 26.2 %collective-permute-start.51 = (bf16[512,512]{1,0:T(8,128)(2,1)S(1)}, bf16[512,512]{1,0:T(8,128)(2,1)S(1)}, u32[]{:S(2)}, u32[]{:S(2)}) collective-permute-start(bf16[512,512]{1,0:T(8,128)(2,1)S(1)} %fold.3), channel_id=1, source_target_pairs={{0,8},{1,9},{2,10},{3,11},{4,12},{5,13},{6,14},{7,15},{8,0},{9,1},... | collective-permute-start | bytes 1572872 | tf_op jit(solution)/shard_map/ppermute | solution.py:793
  169.9 17.1 %collective-permute-start.47 = (bf16[128,1024]{1,0:T(8,128)(2,1)S(1)}, bf16[128,1024]{1,0:T(8,128)(2,1)S(1)}, u32[]{:S(2)}, u32[]{:S(2)}) collective-permute-start(bf16[128,1024]{1,0:T(8,128)(2,1)S(1)} %get-tuple-element.254), channel_id=1, source_target_pairs={{0,2},{1,3},{2,0},{3,1},{4,6},{5,7},{6,4},{7,5},{8,10},{9,11},{10,... | collective-permute-start | bytes 786440 | tf_op jit(solution)/shard_map/ppermute | solution.py:759
  171.3 16.5 %collective-permute-start.48 = (bf16[128,1024]{1,0:T(8,128)(2,1)S(1)}, bf16[128,1024]{1,0:T(8,128)(2,1)S(1)}, u32[]{:S(2)}, u32[]{:S(2)}) collective-permute-start(bf16[128,1024]{1,0:T(8,128)(2,1)S(1)} %get-tuple-element.255), channel_id=1, source_target_pairs={{0,4},{1,5},{2,6},{3,7},{4,0},{5,1},{6,2},{7,3},{8,12},{9,13},{10,... | collective-permute-start | bytes 786440 | tf_op jit(solution)/shard_map/ppermute | solution.py:759
  172.2 20.5 %collective-permute-start.49 = (bf16[128,1024]{1,0:T(8,128)(2,1)S(1)}, bf16[128,1024]{1,0:T(8,128)(2,1)S(1)}, u32[]{:S(2)}, u32[]{:S(2)}) collective-permute-start(bf16[128,1024]{1,0:T(8,128)(2,1)S(1)} %get-tuple-element.256), channel_id=1, source_target_pairs={{0,6},{1,7},{2,4},{3,5},{4,2},{5,3},{6,0},{7,1},{8,14},{9,15},{10,... | collective-permute-start | bytes 786440 | tf_op jit(solution)/shard_map/ppermute | solution.py:759
  195.5 7.7 %collective-permute-start.52 = (bf16[512,1024]{1,0:T(8,128)(2,1)S(1)}, bf16[512,1024]{1,0:T(8,128)(2,1)S(1)}, u32[]{:S(2)}, u32[]{:S(2)}) collective-permute-start(bf16[512,1024]{1,0:T(8,128)(2,1)S(1)} %get-tuple-element.259), channel_id=1, source_target_pairs={{0,1},{1,0},{2,3},{3,2},{4,5},{5,4},{6,7},{7,6},{8,9},{9,8},{10,11... | collective-permute-start | bytes 3145736 | tf_op jit(solution)/shard_map/ppermute | solution.py:759
  201.7 15.3 %collective-permute-start.53 = (bf16[16,40,384]{2,1,0:T(8,128)(2,1)S(1)}, bf16[16,40,384]{2,1,0:T(8,128)(2,1)S(1)}, u32[]{:S(2)}, u32[]{:S(2)}) collective-permute-start(bf16[16,40,384]{2,1,0:T(8,128)(2,1)S(1)} %get-tuple-element.264), channel_id=1, source_target_pairs={{0,16},{16,0},{1,17},{17,1},{2,18},{18,2},{3,19},{19,3},{4,20},{20... | collective-permute-start | bytes 1474568 | tf_op jit(solution)/shard_map/ppermute | solution.py:820
  206.9 10.2 %all-to-all-start.2 = ((bf16[8,32,512]{2,1,0:T(8,128)(2,1)}), bf16[8,32,512]{2,1,0:T(8,128)(2,1)S(1)}, u32[]{:S(2)}, u32[]{:S(2)}) async-start(bf16[8,32,512]{2,1,0:T(8,128)(2,1)} %get-tuple-element.262), calls=%async_computation.2 | async-start | bytes 524288 | tf_op jit(solution)/shard_map/all_to_all | solution.py:797
  212.9 11.6 %collective-permute-start.54 = (bf16[2,32,1024]{2,1,0:T(8,128)(2,1)S(1)}, bf16[2,32,1024]{2,1,0:T(8,128)(2,1)S(1)}, u32[]{:S(2)}, u32[]{:S(2)}) collective-permute-start(bf16[2,32,1024]{2,1,0:T(8,128)(2,1)S(1)} %get-tuple-element.270), channel_id=1, source_target_pairs={{0,16},{16,0},{1,17},{17,1},{2,18},{18,2},{3,19},{19,3},{4,20},{20... | collective-permute-start | bytes 393224 | tf_op jit(solution)/shard_map/ppermute | solution.py:820
  213.6 11.0 %collective-permute-start.55 = (bf16[128,1024]{1,0:T(8,128)(2,1)S(1)}, bf16[128,1024]{1,0:T(8,128)(2,1)}, u32[]{:S(2)}, u32[]{:S(2)}) collective-permute-start(bf16[128,1024]{1,0:T(8,128)(2,1)S(1)} %get-tuple-element.271), channel_id=1, source_target_pairs={{0,2},{1,3},{2,0},{3,1},{4,6},{5,7},{6,4},{7,5},{8,10},{9,11},{10,... | collective-permute-start | bytes 786440 | tf_op jit(solution)/shard_map/ppermute | solution.py:759
  215.5 9.3 %collective-permute-start.56 = (bf16[128,1024]{1,0:T(8,128)(2,1)S(1)}, bf16[128,1024]{1,0:T(8,128)(2,1)}, u32[]{:S(2)}, u32[]{:S(2)}) collective-permute-start(bf16[128,1024]{1,0:T(8,128)(2,1)S(1)} %get-tuple-element.272), channel_id=1, source_target_pairs={{0,4},{1,5},{2,6},{3,7},{4,0},{5,1},{6,2},{7,3},{8,12},{9,13},{10,... | collective-permute-start | bytes 786440 | tf_op jit(solution)/shard_map/ppermute | solution.py:759
  217.0 12.4 %collective-permute-start.57 = (bf16[128,1024]{1,0:T(8,128)(2,1)S(1)}, bf16[128,1024]{1,0:T(8,128)(2,1)}, u32[]{:S(2)}, u32[]{:S(2)}) collective-permute-start(bf16[128,1024]{1,0:T(8,128)(2,1)S(1)} %get-tuple-element.273), channel_id=1, source_target_pairs={{0,6},{1,7},{2,4},{3,5},{4,2},{5,3},{6,0},{7,1},{8,14},{9,15},{10,... | collective-permute-start | bytes 786440 | tf_op jit(solution)/shard_map/ppermute | solution.py:759
  219.0 34.6 %all-to-all-start.3 = ((bf16[16,40,384]{2,1,0:T(8,128)(2,1)}), bf16[16,40,384]{2,1,0:T(8,128)(2,1)S(1)}, u32[]{:S(2)}, u32[]{:S(2)}) async-start(bf16[16,40,384]{2,1,0:T(8,128)(2,1)} %fold.4), calls=%async_computation.3 | async-start | bytes 983040 | tf_op jit(solution)/shard_map/all_to_all | solution.py:1099
  231.6 19.1 %collective-permute-start.58 = (bf16[96,1024]{1,0:T(8,128)(2,1)S(1)}, bf16[96,1024]{1,0:T(8,128)(2,1)S(1)}, u32[]{:S(2)}, u32[]{:S(2)}) collective-permute-start(bf16[96,1024]{1,0:T(8,128)(2,1)S(1)} %get-tuple-element.276), channel_id=1, source_target_pairs={{0,8},{1,9},{2,10},{3,11},{4,12},{5,13},{6,14},{7,15},{8,0},{9,1},... | collective-permute-start | bytes 589832 | tf_op jit(solution)/shard_map/ppermute | solution.py:759
  237.0 16.6 %collective-permute-start.60 = (bf16[64,1024]{1,0:T(8,128)(2,1)S(1)}, bf16[64,1024]{1,0:T(8,128)(2,1)S(1)}, u32[]{:S(2)}, u32[]{:S(2)}) collective-permute-start(bf16[64,1024]{1,0:T(8,128)(2,1)S(1)} %get-tuple-element.280), channel_id=1, source_target_pairs={{0,8},{1,9},{2,10},{3,11},{4,12},{5,13},{6,14},{7,15},{8,0},{9,1},... | collective-permute-start | bytes 393224 | tf_op jit(solution)/shard_map/ppermute | solution.py:759
  250.8 2.8 %collective-permute-start.59 = (bf16[32,1024]{1,0:T(8,128)(2,1)S(1)}, bf16[32,1024]{1,0:T(8,128)(2,1)S(1)}, u32[]{:S(2)}, u32[]{:S(2)}) collective-permute-start(bf16[32,1024]{1,0:T(8,128)(2,1)S(1)} %fusion), channel_id=1, source_target_pairs={{0,0},{8,1},{16,2},{24,3},{1,4},{9,5},{17,6},{25,7},{2,8},{10,9},{... | collective-permute-start | bytes 196616 | tf_op jit(solution)/shard_map/ppermute | solution.py:1128
  (13 other events, 87.1 us)

commit v3 on v2

--- a/solution.py
+++ b/solution.py
@@ -622,24 +622,21 @@
 
 
 def last_kernel(count, place, *refs):
-    ins, rider = refs[: count + 3], refs[count + 3]
-    kept, sent = refs[count + 4 : count + 6]
-    held = refs[count + 6 : 2 * count + 9]
-    out_s, sems = refs[2 * count + 9 :]
-    move = Mover(sems)
+    ins, (x, dy1_in, vec_in, rider) = refs[:count], refs[count : count + 4]
+    kept, sent, dy1, vec, sems = refs[count + 4 :]
+    move = Mover(sems)
+    loads = [move.start(dy1_in, dy1), move.start(vec_in, vec)]
     half = kept.shape[0]
-    move.put(rider.at[1], sent.at[half:, :])
-    for copy in [move.start(a, b) for a, b in zip(ins, held)]:
-        copy.wait()
-    x, dy1, vec = held[count:]
-    dh = held[0][...]
+    sent[half:, :] = rider[1]
+    dh = ins[0][...]
     for i in range(1, count):
-        dh = dh + held[i][...].astype(f32)
+        dh = dh + ins[i][...].astype(f32)
     scaled, inv_std = normalize(x[...].astype(f32))
-    out_s[...] = (dy1[...] + norm_back(dh, scaled, inv_std, vec[0:1, :])).astype(bf16)
-    move.put(out_s.at[half:, :], sent.at[:half, :])
-    move.put(out_s.at[:half, :], kept)
-    move.drain()
+    for copy in loads:
+        copy.wait()
+    out = (dy1[...] + norm_back(dh, scaled, inv_std, vec[0:1, :])).astype(bf16)
+    sent[:half, :] = out[half:]
+    kept[...] = out[:half]
 
 
 def ffn_sum_kernel(count, place, *refs):
@@ -1116,12 +1113,12 @@
     kept, sent = call(
         grid,
         functools.partial(last_kernel, count),
-        near(ins[: count + 1]) + ins[count + 1 :] + near([out_w_sum]),
-        near([half_sds, sds((half + rs, width), bf16)]),
+        held_in(ins[: count + 1]) + ins[count + 1 :] + held_in([out_w_sum]),
+        held_in([half_sds, sds((half + rs, width), bf16)]),
         "last",
         cost(2),
-        scratch=[vmem(a) for a in ins + [row_sds]],
-        sems=len(ins) + 3,
+        scratch=[vmem(dy1), vmem(vec)],
+        sems=2,
     )
     other = xor(sent, n)
     out_w = (out_w_sum[0].astype(f32) + other[half:].astype(f32)).astype(bf16)

time: 261 us -> 261 us (level)
  no operation moved by 1% of the time
where the time goes in v3:
time: 261 us; the launch traced here: 256 us
  waiting for transfers between devices  99 us (38%)
  Pallas kernels  79.6 us (30%)
  starting transfers between devices  73 us (28%)
    pallas_call x25, Pallas kernels, call(): pl.pallas_call(body, out_shape=tuple((o.array if isinstance(o, Near) else...  79.6 us
    ppermute x49, waiting for transfers between devices, xor(): return lax.ppermute(value, 'seq', [(i, i ^ bit) for i in range(seq_size)])  73.5 us
    ppermute x49, starting transfers between devices, xor(): return lax.ppermute(value, 'seq', [(i, i ^ bit) for i in range(seq_size)])  42 us
    ppermute x6, waiting for transfers between devices, to_group(): return lax.ppermute(value, both, pairs)  16.2 us
    all_to_all x1, waiting for transfers between devices, on_device(): attn_w = lax.all_to_all(packed, 'seq', 0, 0, tiled=True)  9.27 us
    all_to_all x1, starting transfers between devices, on_device(): attn_w = lax.all_to_all(packed, 'seq', 0, 0, tiled=True)  7.4 us
    all_to_all x2, starting transfers between devices, members(): lax.all_to_all(value, 'seq', 0, 0, tiled=True, axis_index_groups=index)  6.85 us
    all_to_all x1, starting transfers between devices, on_device(): back = lax.all_to_all(attn_sum, 'seq', 0, 0, tiled=True)  5.47 us
  transfers between devices with their start and end apart: 65, of which 28 were waited for; matrix products, arithmetic and copies ran while one was open for 0% of the time, Pallas kernels for 24%

profile of v3, /device:TPU:0, one launch (start us, length us, event | category | flops | bytes accessed | tf_op | source)
XLA Modules:
  0.0 255.6 jit_solution(5859461517792878550)
XLA Ops:
  1.8 1.9 pack.1
  3.8 7.4 %all-to-all-start = ((bf16[16,40,384]{2,1,0:T(8,128)(2,1)}), bf16[16,40,384]{2,1,0:T(8,128)(2,1)S(1)}, u32[]{:S(2)}, u32[]{:S(2)}) async-start(bf16[16,40,384]{2,1,0:T(8,128)(2,1)} %pack.1), calls=%async_computation | async-start | bytes 983040 | tf_op jit(solution)/shard_map/all_to_all | solution.py:858
  11.2 2.8 %collective-permute-start.1 = (bf16[64,1024]{1,0:T(8,128)(2,1)S(1)}, bf16[64,1024]{1,0:T(8,128)(2,1)S(1)}, u32[]{:S(2)}, u32[]{:S(2)}) collective-permute-start(bf16[64,1024]{1,0:T(8,128)(2,1)S(1)} %get-tuple-element.158), channel_id=1, source_target_pairs={{0,8},{1,9},{2,10},{3,11},{4,12},{5,13},{6,14},{7,15},{8,0},{9,1},... | collective-permute-start | bytes 393224 | tf_op jit(solution)/shard_map/ppermute | solution.py:756
  14.0 1.5 collective-permute-start.4
  16.1 9.3 %all-to-all-done.refs_10_ = bf16[16,40,384]{2,1,0:T(8,128)(2,1)S(1)} async-done(((bf16[16,40,384]{2,1,0:T(8,128)(2,1)}), bf16[16,40,384]{2,1,0:T(8,128)(2,1)S(1)}, u32[]{:S(2)}, u32[]{:S(2)}) %all-to-all-start) | async-done | bytes 491552 | tf_op jit(solution)/shard_map/all_to_all | solution.py:858
  25.4 1.5 collective-permute-start.2
  26.9 5.8 %collective-permute-done.1 = bf16[64,1024]{1,0:T(8,128)(2,1)S(1)} collective-permute-done((bf16[64,1024]{1,0:T(8,128)(2,1)S(1)}, bf16[64,1024]{1,0:T(8,128)(2,1)S(1)}, u32[]{:S(2)}, u32[]{:S(2)}) %collective-permute-start.1) | collective-permute-done | bytes 131104 | tf_op jit(solution)/shard_map/ppermute | solution.py:756
  32.9 2.9 %collective-permute-start.9 = (bf16[128,1024]{1,0:T(8,128)(2,1)S(1)}, bf16[128,1024]{1,0:T(8,128)(2,1)S(1)}, u32[]{:S(2)}, u32[]{:S(2)}) collective-permute-start(bf16[128,1024]{1,0:T(8,128)(2,1)S(1)} %constant_dynamic-update-slice_fusion.2.refs_2_.refs_4_), channel_id=1, source_target_pairs={{0,4},{1,5},{2,6},{3,7},{4,0},{5,1},{6,2},{7,3},{8,12},{9,13},{10,... | collective-permute-start | bytes 786440 | tf_op jit(solution)/shard_map/ppermute | solution.py:756
  36.3 1.7 pack_up.1
  38.1 3.4 %all-to-all-start.1 = ((bf16[8,32,512]{2,1,0:T(8,128)(2,1)}), bf16[8,32,512]{2,1,0:T(8,128)(2,1)S(1)}, u32[]{:S(2)}, u32[]{:S(2)}) async-start(bf16[8,32,512]{2,1,0:T(8,128)(2,1)} %pack_up.1), calls=%async_computation.1 | async-start | bytes 524288 | tf_op jit(solution)/shard_map/all_to_all | solution.py:794
  41.5 1.2 collective-permute-start.5
  42.7 7.4 %collective-permute-done.5.refs_13_ = bf16[2,32,1024]{2,1,0:T(8,128)(2,1)S(1)} collective-permute-done((bf16[2,32,1024]{2,1,0:T(8,128)(2,1)S(1)}, bf16[2,32,1024]{2,1,0:T(8,128)(2,1)S(1)}, u32[]{:S(2)}, u32[]{:S(2)}) %collective-permute-start.5) | collective-permute-done | bytes 131104 | tf_op jit(solution)/shard_map/ppermute | solution.py:756
  50.8 3.4 %collective-permute-start = (bf16[64,1024]{1,0:T(8,128)(2,1)S(1)}, bf16[64,1024]{1,0:T(8,128)(2,1)S(1)}, u32[]{:S(2)}, u32[]{:S(2)}) collective-permute-start(bf16[64,1024]{1,0:T(8,128)(2,1)S(1)} %get-tuple-element.163), channel_id=1, source_target_pairs={{0,8},{1,9},{2,10},{3,11},{4,12},{5,13},{6,14},{7,15},{8,0},{9,1},... | collective-permute-start | bytes 393224 | tf_op jit(solution)/shard_map/ppermute | solution.py:756
  55.3 4.7 %collective-permute-done = bf16[64,1024]{1,0:T(8,128)(2,1)S(1)} collective-permute-done((bf16[64,1024]{1,0:T(8,128)(2,1)S(1)}, bf16[64,1024]{1,0:T(8,128)(2,1)S(1)}, u32[]{:S(2)}, u32[]{:S(2)}) %collective-permute-start) | collective-permute-done | bytes 131104 | tf_op jit(solution)/shard_map/ppermute | solution.py:756
  60.3 3.1 %collective-permute-start.17 = (bf16[128,1024]{1,0:T(8,128)(2,1)S(1)}, bf16[128,1024]{1,0:T(8,128)(2,1)S(1)}, u32[]{:S(2)}, u32[]{:S(2)}) collective-permute-start(bf16[128,1024]{1,0:T(8,128)(2,1)S(1)} %constant_dynamic-update-slice_fusion.refs_0_.refs_6_), channel_id=1, source_target_pairs={{0,6},{1,7},{2,4},{3,5},{4,2},{5,3},{6,0},{7,1},{8,14},{9,15},{10,... | collective-permute-start | bytes 786440 | tf_op jit(solution)/shard_map/ppermute | solution.py:756
  64.1 1.5 collective-permute-start.14
  65.6 12.8 %first.1 = (bf16[1024,1024]{1,0:T(8,128)(2,1)}, bf16[1024,1024]{1,0:T(8,128)(2,1)}, bf16[1024,384]{1,0:T(8,128)(2,1)}, bf16[1024,128]{1,0:T(8,128)(2,1)}, f32[2,...) custom-call(s32[2]{0:T(128)S(1)} %copy-done, ...), custom_call_target="tpu_custom_call" | custom-call | flops 19549999104 | bytes 10531584 | tf_op jit(solution)/shard_map/first/pallas_call | solution.py:95
  78.4 4.5 %collective-permute-done.13.refs_9_ = bf16[512,512]{1,0:T(8,128)(2,1)S(1)} collective-permute-done((bf16[512,512]{1,0:T(8,128)(2,1)S(1)}, bf16[512,512]{1,0:T(8,128)(2,1)S(1)}, u32[]{:S(2)}, u32[]{:S(2)}) %collective-permute-start.13) | collective-permute-done | bytes 524320 | tf_op jit(solution)/shard_map/ppermute | solution.py:790
  83.7 2.7 %collective-permute-done.18.refs_1_ = bf16[512,1024]{1,0:T(8,128)(2,1)S(1)} collective-permute-done((bf16[512,1024]{1,0:T(8,128)(2,1)S(1)}, bf16[512,1024]{1,0:T(8,128)(2,1)S(1)}, u32[]{:S(2)}, u32[]{:S(2)}) %collective-permute-start.18) | collective-permute-done | bytes 1048608 | tf_op jit(solution)/shard_map/ppermute | solution.py:756
  86.4 1.3 pair.4
  87.7 1.5 collective-permute-start.19
  89.2 2.0 collective-permute-start.21
  91.8 4.3 %collective-permute-done.19.refs_1_ = bf16[128,1024]{1,0:T(8,128)(2,1)S(1)} collective-permute-done((bf16[128,1024]{1,0:T(8,128)(2,1)S(1)}, bf16[128,1024]{1,0:T(8,128)(2,1)S(1)}, u32[]{:S(2)}, u32[]{:S(2)}) %collective-permute-start.19) | collective-permute-done | bytes 262176 | tf_op jit(solution)/shard_map/ppermute | solution.py:756
  96.1 2.3 collective-permute-done.20.refs_2_
  98.4 4.5 %collective-permute-done.21.refs_3_ = bf16[128,1024]{1,0:T(8,128)(2,1)S(1)} collective-permute-done((bf16[128,1024]{1,0:T(8,128)(2,1)S(1)}, bf16[128,1024]{1,0:T(8,128)(2,1)S(1)}, u32[]{:S(2)}, u32[]{:S(2)}) %collective-permute-start.21) | collective-permute-done | bytes 262176 | tf_op jit(solution)/shard_map/ppermute | solution.py:756
  102.9 1.6 mid.1
  104.5 1.3 collective-permute-start.32
  105.8 1.7 collective-permute-start.30
  108.1 4.0 %down_back.1 = (bf16[1024,1024]{1,0:T(8,128)(2,1)}, f32[1024,512]{1,0:T(8,128)}, bf16[1024,512]{1,0:T(8,128)(2,1)}, bf16[512,1024]{1,0:T(8,128)(2,1)}) custom-call(bf16[128,1024]{1,0:T(8,128)(2,1)S(1)} %constant_dynamic-update-slice_fusion.refs_0_.refs_6_, bf16[128,1024]{1,0:T(8,128)(2,1)S(1)} %collective-permute-done.24.refs_1_, ...), custom_call_target="tpu_custom_call" | custom-call | flops 5750000128 | bytes 10485760 | tf_op jit(solution)/shard_map/down_back/pallas_call | solution.py:95
  112.1 2.6 %collective-permute-done.32.refs_6_ = bf16[128,1024]{1,0:T(8,128)(2,1)S(1)} collective-permute-done((bf16[128,1024]{1,0:T(8,128)(2,1)S(1)}, bf16[128,1024]{1,0:T(8,128)(2,1)S(1)}, u32[]{:S(2)}, u32[]{:S(2)}) %collective-permute-start.32) | collective-permute-done | bytes 262176 | tf_op jit(solution)/shard_map/ppermute | solution.py:756
  114.6 5.2 %collective-permute-done.30.refs_4_ = bf16[128,1024]{1,0:T(8,128)(2,1)S(1)} collective-permute-done((bf16[128,1024]{1,0:T(8,128)(2,1)S(1)}, bf16[128,1024]{1,0:T(8,128)(2,1)S(1)}, u32[]{:S(2)}, u32[]{:S(2)}) %collective-permute-start.30) | collective-permute-done | bytes 262176 | tf_op jit(solution)/shard_map/ppermute | solution.py:756
  122.2 7.7 %ffn.1 = (bf16[1024,1024]{1,0:T(8,128)(2,1)}, bf16[1024,512]{1,0:T(8,128)(2,1)}, bf16[1024,512]{1,0:T(8,128)(2,1)}, bf16[512,1024]{1,0:T(8,128)(2,1)}, bf16[512,1024]{1,0:T(8,128)(2,1)S(1)}, /*index=5*/f32[1,512]{1,0:T(1,128)}) custom-call(bf16[128,1024]{1,0:T(8,128)(2,1)S(1)} %get-tuple-element.192.refs_0_, ...), custom_call_target="tpu_custom_call" | custom-call | flops 10350000128 | bytes 11538432 | tf_op jit(solution)/shard_map/ffn/pallas_call | solution.py:95
  130.0 2.5 collective-permute-done.34.refs_1_
  132.6 1.3 pair.5
  133.9 1.5 collective-permute-start.35
  135.6 1.8 collective-permute-start.37
  137.4 5.8 %ffn_grads.1 = (f32[512,512]{1,0:T(8,128)}, bf16[512,512]{1,0:T(8,128)(2,1)S(1)}, bf16[512,512]{1,0:T(8,128)(2,1)S(1)}, bf16[512,512]{1,0:T(8,128)(2,1)S(1)}) custom-call(bf16[1024,1024]{1,0:T(8,128)(2,1)} %get-tuple-element.215.refs_0_, bf16[1024,512]{1,0:T(8,128)(2,1)} %get-tuple-element.216.refs_1_, bf16[1024,1024]{1,0:T(8,128)(2,1)} %get-tuple-element.217.refs_2_, ...), custom_call_target="tpu_custom_call" | custom-call | bytes 8912896 | tf_op jit(solution)/shard_map/ffn_grads/pallas_call | solution.py:95
  143.3 4.1 %down.1 = (bf16[512,1024]{1,0:T(8,128)(2,1)}, bf16[512,1024]{1,0:T(8,128)(2,1)S(1)}) custom-call(bf16[1024,512]{1,0:T(8,128)(2,1)} %get-tuple-element.207.refs_0_.refs_3_, bf16[512,1024]{1,0:T(8,128)(2,1)} %get-tuple-element.208.refs_1_), custom_call_target="tpu_custom_call" | custom-call | flops 4600000000 | bytes 4194304 | tf_op jit(solution)/shard_map/down/pallas_call | solution.py:95
  147.4 1.7 collective-permute-done.37.refs_3_
  149.1 2.3 mid_back.1
  153.2 1.3 collective-permute-start.43
  155.6 1.3 pair.6
  156.9 8.9 %collective-permute-done.41.refs_1_ = bf16[512,512]{1,0:T(8,128)(2,1)S(1)} collective-permute-done((bf16[512,512]{1,0:T(8,128)(2,1)S(1)}, bf16[512,512]{1,0:T(8,128)(2,1)S(1)}, u32[]{:S(2)}, u32[]{:S(2)}) %collective-permute-start.41) | collective-permute-done | bytes 524320 | tf_op jit(solution)/shard_map/ppermute | solution.py:790
  167.5 1.5 collective-permute-start.50
  169.9 1.4 collective-permute-start.47
  173.4 13.6 %attend_back.1 = (bf16[1024,384]{1,0:T(8,128)(2,1)}, bf16[512,1024]{1,0:T(8,128)(2,1)}, bf16[512,1024]{1,0:T(8,128)(2,1)S(1)}, f32[1,384]{1,0:T(1,128)}, bf16[1024,1024]{1,0:T(8,128)(2,1)}) custom-call(s32[2]{0:T(128)S(1)} %copy-done, s32[4]{0:T(128)S(1)} %copy-done.1, bf16[128,1024]{1,0:T(8,128)(2,1)S(1)} %get-tuple-element.232.refs_2_, ...), custom_call_target="tpu_custom_call" | custom-call | bytes 8922624 | tf_op jit(solution)/shard_map/attend_back/pallas_call | solution.py:95
  187.9 4.8 %collective-permute-done.49.refs_3_ = bf16[128,1024]{1,0:T(8,128)(2,1)S(1)} collective-permute-done((bf16[128,1024]{1,0:T(8,128)(2,1)S(1)}, bf16[128,1024]{1,0:T(8,128)(2,1)S(1)}, u32[]{:S(2)}, u32[]{:S(2)}) %collective-permute-start.49) | collective-permute-done | bytes 262176 | tf_op jit(solution)/shard_map/ppermute | solution.py:756
  192.7 2.8 %collective-permute-done.51.refs_2_ = bf16[512,512]{1,0:T(8,128)(2,1)S(1)} collective-permute-done((bf16[512,512]{1,0:T(8,128)(2,1)S(1)}, bf16[512,512]{1,0:T(8,128)(2,1)S(1)}, u32[]{:S(2)}, u32[]{:S(2)}) %collective-permute-start.51) | collective-permute-done | bytes 524320 | tf_op jit(solution)/shard_map/ppermute | solution.py:790
  195.5 5.5 %attn_grads.1 = (bf16[16,40,384]{2,1,0:T(8,128)(2,1)S(1)}, bf16[16,40,384]{2,1,0:T(8,128)(2,1)S(1)}) custom-call(bf16[1024,384]{1,0:T(8,128)(2,1)} %get-tuple-element.244.refs_0_, bf16[1024,1024]{1,0:T(8,128)(2,1)} %get-tuple-element.245.refs_1_, bf16[1024,384]{1,0:T(8,128)(2,1)} %get-tuple-element.243.refs_13_.refs_2_, ...), custom_call_target="tpu_custom_call" | custom-call | flops 6899999744 | bytes 5789696 | tf_op jit(solution)/shard_map/attn_grads/pallas_call | solution.py:95
  201.7 1.4 collective-permute-start.53
  203.1 1.3 pair.7
  204.4 2.4 ffn_sum.1
  206.9 3.4 %all-to-all-start.2 = ((bf16[8,32,512]{2,1,0:T(8,128)(2,1)}), bf16[8,32,512]{2,1,0:T(8,128)(2,1)S(1)}, u32[]{:S(2)}, u32[]{:S(2)}) async-start(bf16[8,32,512]{2,1,0:T(8,128)(2,1)} %get-tuple-element.262), calls=%async_computation.2 | async-start | bytes 524288 | tf_op jit(solution)/shard_map/all_to_all | solution.py:794
  210.3 2.6 %out_grads.1 = (bf16[2,32,1024]{2,1,0:T(8,128)(2,1)S(1)}, bf16[2,32,1024]{2,1,0:T(8,128)(2,1)S(1)}) custom-call(bf16[1024,1024]{1,0:T(8,128)(2,1)} %get-tuple-element.265.refs_0_, bf16[1024,128]{1,0:T(8,128)(2,1)} %get-tuple-element.267.refs_1_), custom_call_target="tpu_custom_call" | custom-call | flops 2300000000 | bytes 2359552 | tf_op jit(solution)/shard_map/out_grads/pallas_call | solution.py:95
  213.6 1.9 collective-permute-start.55
  215.5 1.5 collective-permute-start.56
  219.0 5.5 %all-to-all-start.3 = ((bf16[16,40,384]{2,1,0:T(8,128)(2,1)}), bf16[16,40,384]{2,1,0:T(8,128)(2,1)S(1)}, u32[]{:S(2)}, u32[]{:S(2)}) async-start(bf16[16,40,384]{2,1,0:T(8,128)(2,1)} %fold.4), calls=%async_computation.3 | async-start | bytes 983040 | tf_op jit(solution)/shard_map/all_to_all | solution.py:1096
  224.8 4.5 %collective-permute-done.57.refs_3_ = bf16[128,1024]{1,0:T(8,128)(2,1)} collective-permute-done((bf16[128,1024]{1,0:T(8,128)(2,1)S(1)}, bf16[128,1024]{1,0:T(8,128)(2,1)}, u32[]{:S(2)}, u32[]{:S(2)}) %collective-permute-start.57) | collective-permute-done | bytes 262176 | tf_op jit(solution)/shard_map/ppermute | solution.py:756
  229.4 2.6 %last.1 = (bf16[64,1024]{1,0:T(8,128)(2,1)S(1)}, bf16[96,1024]{1,0:T(8,128)(2,1)S(1)}) custom-call(f32[128,1024]{1,0:T(8,128)S(1)} %copy-done.8, bf16[128,1024]{1,0:T(8,128)(2,1)} %collective-permute-done.55.refs_1_, bf16[128,1024]{1,0:T(8,128)(2,1)} %collective-permute-done.56.refs_2_, bf16[128,1024]{1,0:T(8,128)(2,1)} %collective-permute-done.57.refs_3_, ...), custom_call_target="tpu_custom_call" | custom-call | flops 2300000000 | bytes 2457728 | tf_op jit(solution)/shard_map/last/pallas_call | solution.py:95
  231.9 3.6 %collective-permute-start.58 = (bf16[96,1024]{1,0:T(8,128)(2,1)S(1)}, bf16[96,1024]{1,0:T(8,128)(2,1)S(1)}, u32[]{:S(2)}, u32[]{:S(2)}) collective-permute-start(bf16[96,1024]{1,0:T(8,128)(2,1)S(1)} %get-tuple-element.276), channel_id=1, source_target_pairs={{0,8},{1,9},{2,10},{3,11},{4,12},{5,13},{6,14},{7,15},{8,0},{9,1},... | collective-permute-start | bytes 589832 | tf_op jit(solution)/shard_map/ppermute | solution.py:756
  235.6 1.7 out.1
  237.4 13.4 %collective-permute-done.58.refs_6_ = bf16[96,1024]{1,0:T(8,128)(2,1)S(1)} collective-permute-done((bf16[96,1024]{1,0:T(8,128)(2,1)S(1)}, bf16[96,1024]{1,0:T(8,128)(2,1)S(1)}, u32[]{:S(2)}, u32[]{:S(2)}) %collective-permute-start.58) | collective-permute-done | bytes 196640 | tf_op jit(solution)/shard_map/ppermute | solution.py:756
  251.5 2.1 collective-permute-done.60.refs_4_
  253.6 1.8 unpack.1
  (121 shorter events, 22.8 us)
Async XLA Ops:
  3.8 21.7 %all-to-all-start = ((bf16[16,40,384]{2,1,0:T(8,128)(2,1)}), bf16[16,40,384]{2,1,0:T(8,128)(2,1)S(1)}, u32[]{:S(2)}, u32[]{:S(2)}) async-start(bf16[16,40,384]{2,1,0:T(8,128)(2,1)} %pack.1), calls=%async_computation | async-start | bytes 983040 | tf_op jit(solution)/shard_map/all_to_all | solution.py:858
  11.2 21.6 %collective-permute-start.1 = (bf16[64,1024]{1,0:T(8,128)(2,1)S(1)}, bf16[64,1024]{1,0:T(8,128)(2,1)S(1)}, u32[]{:S(2)}, u32[]{:S(2)}) collective-permute-start(bf16[64,1024]{1,0:T(8,128)(2,1)S(1)} %get-tuple-element.158), channel_id=1, source_target_pairs={{0,8},{1,9},{2,10},{3,11},{4,12},{5,13},{6,14},{7,15},{8,0},{9,1},... | collective-permute-start | bytes 393224 | tf_op jit(solution)/shard_map/ppermute | solution.py:756
  14.0 21.8 %collective-permute-start.4 = (bf16[32,1024]{1,0:T(8,128)(2,1)S(1)}, bf16[32,1024]{1,0:T(8,128)(2,1)S(1)}, u32[]{:S(2)}, u32[]{:S(2)}) collective-permute-start(bf16[32,1024]{1,0:T(8,128)(2,1)S(1)} %copy-done.11), channel_id=1, source_target_pairs={{0,16},{1,24},{2,0},{3,8},{4,17},{5,25},{6,1},{7,9},{8,18},{9,26},... | collective-permute-start | bytes 196616 | tf_op jit(solution)/shard_map/ppermute | solution.py:827
  15.5 26.0 %collective-permute-start.3 = (bf16[32,1024]{1,0:T(8,128)(2,1)S(1)}, bf16[32,1024]{1,0:T(8,128)(2,1)S(1)}, u32[]{:S(2)}, u32[]{:S(2)}) collective-permute-start(bf16[32,1024]{1,0:T(8,128)(2,1)S(1)} %copy-done.11), channel_id=1, source_target_pairs={{0,0},{1,8},{2,16},{3,24},{4,1},{5,9},{6,17},{7,25},{8,2},{9,10},{... | collective-permute-start | bytes 196616 | tf_op jit(solution)/shard_map/ppermute | solution.py:827
  25.4 28.8 %collective-permute-start.2 = (bf16[16,40,384]{2,1,0:T(8,128)(2,1)S(1)}, bf16[16,40,384]{2,1,0:T(8,128)(2,1)S(1)}, u32[]{:S(2)}, u32[]{:S(2)}) collective-permute-start(bf16[16,40,384]{2,1,0:T(8,128)(2,1)S(1)} %all-to-all-done.refs_10_), channel_id=1, source_target_pairs={{0,16},{16,0},{1,17},{17,1},{2,18},{18,2},{3,19},{19,3},{4,20},{20... | collective-permute-start | bytes 1474568 | tf_op jit(solution)/shard_map/ppermute | solution.py:817
  32.8 21.4 %collective-permute-start.11 = (bf16[128,1024]{1,0:T(8,128)(2,1)S(1)}, bf16[128,1024]{1,0:T(8,128)(2,1)S(1)}, u32[]{:S(2)}, u32[]{:S(2)}) collective-permute-start(bf16[128,1024]{1,0:T(8,128)(2,1)S(1)} %constant_dynamic-update-slice_fusion.2.refs_2_.refs_4_), channel_id=1, source_target_pairs={{0,6},{1,7},{2,4},{3,5},{4,2},{5,3},{6,0},{7,1},{8,14},{9,15},{10,... | collective-permute-start | bytes 786440 | tf_op jit(solution)/shard_map/ppermute | solution.py:756
  32.9 21.4 %collective-permute-start.9 = (bf16[128,1024]{1,0:T(8,128)(2,1)S(1)}, bf16[128,1024]{1,0:T(8,128)(2,1)S(1)}, u32[]{:S(2)}, u32[]{:S(2)}) collective-permute-start(bf16[128,1024]{1,0:T(8,128)(2,1)S(1)} %constant_dynamic-update-slice_fusion.2.refs_2_.refs_4_), channel_id=1, source_target_pairs={{0,4},{1,5},{2,6},{3,7},{4,0},{5,1},{6,2},{7,3},{8,12},{9,13},{10,... | collective-permute-start | bytes 786440 | tf_op jit(solution)/shard_map/ppermute | solution.py:756
  35.8 18.4 %collective-permute-start.7 = (bf16[128,1024]{1,0:T(8,128)(2,1)S(1)}, bf16[128,1024]{1,0:T(8,128)(2,1)S(1)}, u32[]{:S(2)}, u32[]{:S(2)}) collective-permute-start(bf16[128,1024]{1,0:T(8,128)(2,1)S(1)} %constant_dynamic-update-slice_fusion.2.refs_2_.refs_4_), channel_id=1, source_target_pairs={{0,2},{1,3},{2,0},{3,1},{4,6},{5,7},{6,4},{7,5},{8,10},{9,11},{10,... | collective-permute-start | bytes 786440 | tf_op jit(solution)/shard_map/ppermute | solution.py:756
  38.1 22.0 %all-to-all-start.1 = ((bf16[8,32,512]{2,1,0:T(8,128)(2,1)}), bf16[8,32,512]{2,1,0:T(8,128)(2,1)S(1)}, u32[]{:S(2)}, u32[]{:S(2)}) async-start(bf16[8,32,512]{2,1,0:T(8,128)(2,1)} %pack_up.1), calls=%async_computation.1 | async-start | bytes 524288 | tf_op jit(solution)/shard_map/all_to_all | solution.py:794
  41.5 8.6 %collective-permute-start.5 = (bf16[2,32,1024]{2,1,0:T(8,128)(2,1)S(1)}, bf16[2,32,1024]{2,1,0:T(8,128)(2,1)S(1)}, u32[]{:S(2)}, u32[]{:S(2)}) collective-permute-start(bf16[2,32,1024]{2,1,0:T(8,128)(2,1)S(1)} %pad_maximum_fusion.refs_12_), channel_id=1, source_target_pairs={{0,8},{1,9},{2,10},{3,11},{4,12},{5,13},{6,14},{7,15},{8,0},{9,1},... | collective-permute-start | bytes 393224 | tf_op jit(solution)/shard_map/ppermute | solution.py:756
  50.8 9.2 %collective-permute-start = (bf16[64,1024]{1,0:T(8,128)(2,1)S(1)}, bf16[64,1024]{1,0:T(8,128)(2,1)S(1)}, u32[]{:S(2)}, u32[]{:S(2)}) collective-permute-start(bf16[64,1024]{1,0:T(8,128)(2,1)S(1)} %get-tuple-element.163), channel_id=1, source_target_pairs={{0,8},{1,9},{2,10},{3,11},{4,12},{5,13},{6,14},{7,15},{8,0},{9,1},... | collective-permute-start | bytes 393224 | tf_op jit(solution)/shard_map/ppermute | solution.py:756
  54.2 6.1 %collective-permute-start.6 = (bf16[128,1024]{1,0:T(8,128)(2,1)S(1)}, bf16[128,1024]{1,0:T(8,128)(2,1)S(1)}, u32[]{:S(2)}, u32[]{:S(2)}) collective-permute-start(bf16[128,1024]{1,0:T(8,128)(2,1)S(1)} %constant_dynamic-update-slice_fusion.2.refs_2_.refs_4_), channel_id=1, source_target_pairs={{0,1},{1,0},{2,3},{3,2},{4,5},{5,4},{6,7},{7,6},{8,9},{9,8},{10,11... | collective-permute-start | bytes 786440 | tf_op jit(solution)/shard_map/ppermute | solution.py:756
  54.3 6.0 %collective-permute-start.8 = (bf16[128,1024]{1,0:T(8,128)(2,1)S(1)}, bf16[128,1024]{1,0:T(8,128)(2,1)}, u32[]{:S(2)}, u32[]{:S(2)}) collective-permute-start(bf16[128,1024]{1,0:T(8,128)(2,1)S(1)} %collective-permute-done.7.refs_4_), channel_id=1, source_target_pairs={{0,1},{1,0},{2,3},{3,2},{4,5},{5,4},{6,7},{7,6},{8,9},{9,8},{10,11... | collective-permute-start | bytes 786440 | tf_op jit(solution)/shard_map/ppermute | solution.py:756
  54.8 5.5 %collective-permute-start.10 = (bf16[128,1024]{1,0:T(8,128)(2,1)S(1)}, bf16[128,1024]{1,0:T(8,128)(2,1)}, u32[]{:S(2)}, u32[]{:S(2)}) collective-permute-start(bf16[128,1024]{1,0:T(8,128)(2,1)S(1)} %collective-permute-done.9.refs_6_), channel_id=1, source_target_pairs={{0,1},{1,0},{2,3},{3,2},{4,5},{5,4},{6,7},{7,6},{8,9},{9,8},{10,11... | collective-permute-start | bytes 786440 | tf_op jit(solution)/shard_map/ppermute | solution.py:756
  54.9 5.4 %collective-permute-start.12 = (bf16[128,1024]{1,0:T(8,128)(2,1)S(1)}, bf16[128,1024]{1,0:T(8,128)(2,1)}, u32[]{:S(2)}, u32[]{:S(2)}) collective-permute-start(bf16[128,1024]{1,0:T(8,128)(2,1)S(1)} %collective-permute-done.11.refs_8_), channel_id=1, source_target_pairs={{0,1},{1,0},{2,3},{3,2},{4,5},{5,4},{6,7},{7,6},{8,9},{9,8},{10,11... | collective-permute-start | bytes 786440 | tf_op jit(solution)/shard_map/ppermute | solution.py:756
  60.2 22.7 %collective-permute-start.13 = (bf16[512,512]{1,0:T(8,128)(2,1)S(1)}, bf16[512,512]{1,0:T(8,128)(2,1)S(1)}, u32[]{:S(2)}, u32[]{:S(2)}) collective-permute-start(bf16[512,512]{1,0:T(8,128)(2,1)S(1)} %join.1.refs_8_), channel_id=1, source_target_pairs={{0,8},{1,9},{2,10},{3,11},{4,12},{5,13},{6,14},{7,15},{8,0},{9,1},... | collective-permute-start | bytes 1572872 | tf_op jit(solution)/shard_map/ppermute | solution.py:790
  60.3 22.5 %collective-permute-start.17 = (bf16[128,1024]{1,0:T(8,128)(2,1)S(1)}, bf16[128,1024]{1,0:T(8,128)(2,1)S(1)}, u32[]{:S(2)}, u32[]{:S(2)}) collective-permute-start(bf16[128,1024]{1,0:T(8,128)(2,1)S(1)} %constant_dynamic-update-slice_fusion.refs_0_.refs_6_), channel_id=1, source_target_pairs={{0,6},{1,7},{2,4},{3,5},{4,2},{5,3},{6,0},{7,1},{8,14},{9,15},{10,... | collective-permute-start | bytes 786440 | tf_op jit(solution)/shard_map/ppermute | solution.py:756
  63.4 20.3 %collective-permute-start.16 = (bf16[128,1024]{1,0:T(8,128)(2,1)S(1)}, bf16[128,1024]{1,0:T(8,128)(2,1)S(1)}, u32[]{:S(2)}, u32[]{:S(2)}) collective-permute-start(bf16[128,1024]{1,0:T(8,128)(2,1)S(1)} %constant_dynamic-update-slice_fusion.refs_0_.refs_6_), channel_id=1, source_target_pairs={{0,4},{1,5},{2,6},{3,7},{4,0},{5,1},{6,2},{7,3},{8,12},{9,13},{10,... | collective-permute-start | bytes 786440 | tf_op jit(solution)/shard_map/ppermute | solution.py:756
  63.4 20.3 %collective-permute-start.15 = (bf16[128,1024]{1,0:T(8,128)(2,1)S(1)}, bf16[128,1024]{1,0:T(8,128)(2,1)S(1)}, u32[]{:S(2)}, u32[]{:S(2)}) collective-permute-start(bf16[128,1024]{1,0:T(8,128)(2,1)S(1)} %constant_dynamic-update-slice_fusion.refs_0_.refs_6_), channel_id=1, source_target_pairs={{0,2},{1,3},{2,0},{3,1},{4,6},{5,7},{6,4},{7,5},{8,10},{9,11},{10,... | collective-permute-start | bytes 786440 | tf_op jit(solution)/shard_map/ppermute | solution.py:756
  64.1 19.6 %collective-permute-start.14 = (bf16[512,512]{1,0:T(8,128)(2,1)S(1)}, bf16[512,512]{1,0:T(8,128)(2,1)S(1)}, u32[]{:S(2)}, u32[]{:S(2)}) collective-permute-start(bf16[512,512]{1,0:T(8,128)(2,1)S(1)} %join.1.refs_8_), channel_id=1, source_target_pairs={{0,16},{1,17},{2,18},{3,19},{4,20},{5,21},{6,22},{7,23},{8,24},{9,... | collective-permute-start | bytes 1572872 | tf_op jit(solution)/shard_map/ppermute | solution.py:790
  83.7 2.7 %collective-permute-start.18 = (bf16[512,1024]{1,0:T(8,128)(2,1)S(1)}, bf16[512,1024]{1,0:T(8,128)(2,1)S(1)}, u32[]{:S(2)}, u32[]{:S(2)}) collective-permute-start(bf16[512,1024]{1,0:T(8,128)(2,1)S(1)} %get-tuple-element.186), channel_id=1, source_target_pairs={{0,1},{1,0},{2,3},{3,2},{4,5},{5,4},{6,7},{7,6},{8,9},{9,8},{10,11... | collective-permute-start | bytes 3145736 | tf_op jit(solution)/shard_map/ppermute | solution.py:756
  87.7 8.4 %collective-permute-start.19 = (bf16[128,1024]{1,0:T(8,128)(2,1)S(1)}, bf16[128,1024]{1,0:T(8,128)(2,1)S(1)}, u32[]{:S(2)}, u32[]{:S(2)}) collective-permute-start(bf16[128,1024]{1,0:T(8,128)(2,1)S(1)} %get-tuple-element.188), channel_id=1, source_target_pairs={{0,2},{1,3},{2,0},{3,1},{4,6},{5,7},{6,4},{7,5},{8,10},{9,11},{10,... | collective-permute-start | bytes 786440 | tf_op jit(solution)/shard_map/ppermute | solution.py:756
  89.2 9.2 %collective-permute-start.20 = (bf16[128,1024]{1,0:T(8,128)(2,1)S(1)}, bf16[128,1024]{1,0:T(8,128)(2,1)S(1)}, u32[]{:S(2)}, u32[]{:S(2)}) collective-permute-start(bf16[128,1024]{1,0:T(8,128)(2,1)S(1)} %get-tuple-element.189), channel_id=1, source_target_pairs={{0,4},{1,5},{2,6},{3,7},{4,0},{5,1},{6,2},{7,3},{8,12},{9,13},{10,... | collective-permute-start | bytes 786440 | tf_op jit(solution)/shard_map/ppermute | solution.py:756
  89.2 13.7 %collective-permute-start.21 = (bf16[128,1024]{1,0:T(8,128)(2,1)S(1)}, bf16[128,1024]{1,0:T(8,128)(2,1)S(1)}, u32[]{:S(2)}, u32[]{:S(2)}) collective-permute-start(bf16[128,1024]{1,0:T(8,128)(2,1)S(1)} %get-tuple-element.190), channel_id=1, source_target_pairs={{0,6},{1,7},{2,4},{3,5},{4,2},{5,3},{6,0},{7,1},{8,14},{9,15},{10,... | collective-permute-start | bytes 786440 | tf_op jit(solution)/shard_map/ppermute | solution.py:756
  91.2 16.9 %collective-permute-start.28 = (bf16[512,512]{1,0:T(8,128)(2,1)S(1)}, bf16[512,512]{1,0:T(8,128)(2,1)S(1)}, u32[]{:S(2)}, u32[]{:S(2)}) collective-permute-start(bf16[512,512]{1,0:T(8,128)(2,1)S(1)} %collective-permute-done.13.refs_9_), channel_id=1, source_target_pairs={{0,16},{1,17},{2,18},{3,19},{4,20},{5,21},{6,22},{7,23},{8,24},{9,... | collective-permute-start | bytes 1572872 | tf_op jit(solution)/shard_map/ppermute | solution.py:790
  91.8 12.7 %collective-permute-start.24 = (bf16[128,1024]{1,0:T(8,128)(2,1)S(1)}, bf16[128,1024]{1,0:T(8,128)(2,1)S(1)}, u32[]{:S(2)}, u32[]{:S(2)}) collective-permute-start(bf16[128,1024]{1,0:T(8,128)(2,1)S(1)} %constant_dynamic-update-slice_fusion.refs_0_.refs_6_), channel_id=1, source_target_pairs={{0,1},{1,0},{2,3},{3,2},{4,5},{5,4},{6,7},{7,6},{8,9},{9,8},{10,11... | collective-permute-start | bytes 786440 | tf_op jit(solution)/shard_map/ppermute | solution.py:756
  96.1 9.7 %collective-permute-start.25 = (bf16[128,1024]{1,0:T(8,128)(2,1)S(1)}, bf16[128,1024]{1,0:T(8,128)(2,1)S(1)}, u32[]{:S(2)}, u32[]{:S(2)}) collective-permute-start(bf16[128,1024]{1,0:T(8,128)(2,1)S(1)} %collective-permute-done.15.refs_2_), channel_id=1, source_target_pairs={{0,1},{1,0},{2,3},{3,2},{4,5},{5,4},{6,7},{7,6},{8,9},{9,8},{10,11... | collective-permute-start | bytes 786440 | tf_op jit(solution)/shard_map/ppermute | solution.py:756
  98.4 9.1 %collective-permute-start.26 = (bf16[128,1024]{1,0:T(8,128)(2,1)S(1)}, bf16[128,1024]{1,0:T(8,128)(2,1)S(1)}, u32[]{:S(2)}, u32[]{:S(2)}) collective-permute-start(bf16[128,1024]{1,0:T(8,128)(2,1)S(1)} %collective-permute-done.16.refs_4_), channel_id=1, source_target_pairs={{0,1},{1,0},{2,3},{3,2},{4,5},{5,4},{6,7},{7,6},{8,9},{9,8},{10,11... | collective-permute-start | bytes 786440 | tf_op jit(solution)/shard_map/ppermute | solution.py:756
  102.9 5.2 %collective-permute-start.27 = (bf16[128,1024]{1,0:T(8,128)(2,1)S(1)}, bf16[128,1024]{1,0:T(8,128)(2,1)S(1)}, u32[]{:S(2)}, u32[]{:S(2)}) collective-permute-start(bf16[128,1024]{1,0:T(8,128)(2,1)S(1)} %collective-permute-done.17.refs_6_), channel_id=1, source_target_pairs={{0,1},{1,0},{2,3},{3,2},{4,5},{5,4},{6,7},{7,6},{8,9},{9,8},{10,11... | collective-permute-start | bytes 786440 | tf_op jit(solution)/shard_map/ppermute | solution.py:756
  104.5 10.1 %collective-permute-start.32 = (bf16[128,1024]{1,0:T(8,128)(2,1)S(1)}, bf16[128,1024]{1,0:T(8,128)(2,1)S(1)}, u32[]{:S(2)}, u32[]{:S(2)}) collective-permute-start(bf16[128,1024]{1,0:T(8,128)(2,1)S(1)} %get-tuple-element.192.refs_0_), channel_id=1, source_target_pairs={{0,6},{1,7},{2,4},{3,5},{4,2},{5,3},{6,0},{7,1},{8,14},{9,15},{10,... | collective-permute-start | bytes 786440 | tf_op jit(solution)/shard_map/ppermute | solution.py:756
  105.8 14.1 %collective-permute-start.30 = (bf16[128,1024]{1,0:T(8,128)(2,1)S(1)}, bf16[128,1024]{1,0:T(8,128)(2,1)S(1)}, u32[]{:S(2)}, u32[]{:S(2)}) collective-permute-start(bf16[128,1024]{1,0:T(8,128)(2,1)S(1)} %get-tuple-element.192.refs_0_), channel_id=1, source_target_pairs={{0,4},{1,5},{2,6},{3,7},{4,0},{5,1},{6,2},{7,3},{8,12},{9,13},{10,... | collective-permute-start | bytes 786440 | tf_op jit(solution)/shard_map/ppermute | solution.py:756
  107.5 12.3 %collective-permute-start.23 = (bf16[128,1024]{1,0:T(8,128)(2,1)S(1)}, bf16[128,1024]{1,0:T(8,128)(2,1)S(1)}, u32[]{:S(2)}, u32[]{:S(2)}) collective-permute-start(bf16[128,1024]{1,0:T(8,128)(2,1)S(1)} %get-tuple-element.192.refs_0_), channel_id=1, source_target_pairs={{0,2},{1,3},{2,0},{3,1},{4,6},{5,7},{6,4},{7,5},{8,10},{9,11},{10,... | collective-permute-start | bytes 786440 | tf_op jit(solution)/shard_map/ppermute | solution.py:756
  108.1 12.3 %collective-permute-start.22 = (bf16[128,1024]{1,0:T(8,128)(2,1)S(1)}, bf16[128,1024]{1,0:T(8,128)(2,1)S(1)}, u32[]{:S(2)}, u32[]{:S(2)}) collective-permute-start(bf16[128,1024]{1,0:T(8,128)(2,1)S(1)} %get-tuple-element.192.refs_0_), channel_id=1, source_target_pairs={{0,1},{1,0},{2,3},{3,2},{4,5},{5,4},{6,7},{7,6},{8,9},{9,8},{10,11... | collective-permute-start | bytes 786440 | tf_op jit(solution)/shard_map/ppermute | solution.py:756
  119.9 1.9 collective-permute-start.31
  120.4 1.8 collective-permute-start.33
  129.8 2.7 %collective-permute-start.34 = (bf16[512,1024]{1,0:T(8,128)(2,1)S(1)}, bf16[512,1024]{1,0:T(8,128)(2,1)S(1)}, u32[]{:S(2)}, u32[]{:S(2)}) collective-permute-start(bf16[512,1024]{1,0:T(8,128)(2,1)S(1)} %get-tuple-element.205), channel_id=1, source_target_pairs={{0,1},{1,0},{2,3},{3,2},{4,5},{5,4},{6,7},{7,6},{8,9},{9,8},{10,11... | collective-permute-start | bytes 3145736 | tf_op jit(solution)/shard_map/ppermute | solution.py:756
  133.9 13.5 %collective-permute-start.35 = (bf16[128,1024]{1,0:T(8,128)(2,1)S(1)}, bf16[128,1024]{1,0:T(8,128)(2,1)S(1)}, u32[]{:S(2)}, u32[]{:S(2)}) collective-permute-start(bf16[128,1024]{1,0:T(8,128)(2,1)S(1)} %get-tuple-element.211), channel_id=1, source_target_pairs={{0,2},{1,3},{2,0},{3,1},{4,6},{5,7},{6,4},{7,5},{8,10},{9,11},{10,... | collective-permute-start | bytes 786440 | tf_op jit(solution)/shard_map/ppermute | solution.py:756
  135.4 12.0 %collective-permute-start.36 = (bf16[128,1024]{1,0:T(8,128)(2,1)S(1)}, bf16[128,1024]{1,0:T(8,128)(2,1)S(1)}, u32[]{:S(2)}, u32[]{:S(2)}) collective-permute-start(bf16[128,1024]{1,0:T(8,128)(2,1)S(1)} %get-tuple-element.212), channel_id=1, source_target_pairs={{0,4},{1,5},{2,6},{3,7},{4,0},{5,1},{6,2},{7,3},{8,12},{9,13},{10,... | collective-permute-start | bytes 786440 | tf_op jit(solution)/shard_map/ppermute | solution.py:756
  135.6 13.5 %collective-permute-start.37 = (bf16[128,1024]{1,0:T(8,128)(2,1)S(1)}, bf16[128,1024]{1,0:T(8,128)(2,1)S(1)}, u32[]{:S(2)}, u32[]{:S(2)}) collective-permute-start(bf16[128,1024]{1,0:T(8,128)(2,1)S(1)} %get-tuple-element.213), channel_id=1, source_target_pairs={{0,6},{1,7},{2,4},{3,5},{4,2},{5,3},{6,0},{7,1},{8,14},{9,15},{10,... | collective-permute-start | bytes 786440 | tf_op jit(solution)/shard_map/ppermute | solution.py:756
  151.4 4.2 %collective-permute-start.38 = (bf16[512,1024]{1,0:T(8,128)(2,1)S(1)}, bf16[512,1024]{1,0:T(8,128)(2,1)S(1)}, u32[]{:S(2)}, u32[]{:S(2)}) collective-permute-start(bf16[512,1024]{1,0:T(8,128)(2,1)S(1)} %get-tuple-element.221), channel_id=1, source_target_pairs={{0,1},{1,0},{2,3},{3,2},{4,5},{5,4},{6,7},{7,6},{8,9},{9,8},{10,11... | collective-permute-start | bytes 3145736 | tf_op jit(solution)/shard_map/ppermute | solution.py:756
  151.5 14.3 %collective-permute-start.41 = (bf16[512,512]{1,0:T(8,128)(2,1)S(1)}, bf16[512,512]{1,0:T(8,128)(2,1)S(1)}, u32[]{:S(2)}, u32[]{:S(2)}) collective-permute-start(bf16[512,512]{1,0:T(8,128)(2,1)S(1)} %get-tuple-element.228), channel_id=1, source_target_pairs={{0,16},{1,17},{2,18},{3,19},{4,20},{5,21},{6,22},{7,23},{8,24},{9,... | collective-permute-start | bytes 1572872 | tf_op jit(solution)/shard_map/ppermute | solution.py:790
  152.1 13.9 %collective-permute-start.45 = (bf16[128,1024]{1,0:T(8,128)(2,1)S(1)}, bf16[128,1024]{1,0:T(8,128)(2,1)S(1)}, u32[]{:S(2)}, u32[]{:S(2)}) collective-permute-start(bf16[128,1024]{1,0:T(8,128)(2,1)S(1)} %get-tuple-element.232.refs_2_), channel_id=1, source_target_pairs={{0,6},{1,7},{2,4},{3,5},{4,2},{5,3},{6,0},{7,1},{8,14},{9,15},{10,... | collective-permute-start | bytes 786440 | tf_op jit(solution)/shard_map/ppermute | solution.py:756
  153.2 13.5 %collective-permute-start.43 = (bf16[128,1024]{1,0:T(8,128)(2,1)S(1)}, bf16[128,1024]{1,0:T(8,128)(2,1)S(1)}, u32[]{:S(2)}, u32[]{:S(2)}) collective-permute-start(bf16[128,1024]{1,0:T(8,128)(2,1)S(1)} %get-tuple-element.232.refs_2_), channel_id=1, source_target_pairs={{0,4},{1,5},{2,6},{3,7},{4,0},{5,1},{6,2},{7,3},{8,12},{9,13},{10,... | collective-permute-start | bytes 786440 | tf_op jit(solution)/shard_map/ppermute | solution.py:756
  154.5 12.5 %collective-permute-start.40 = (bf16[128,1024]{1,0:T(8,128)(2,1)S(1)}, bf16[128,1024]{1,0:T(8,128)(2,1)S(1)}, u32[]{:S(2)}, u32[]{:S(2)}) collective-permute-start(bf16[128,1024]{1,0:T(8,128)(2,1)S(1)} %get-tuple-element.232.refs_2_), channel_id=1, source_target_pairs={{0,2},{1,3},{2,0},{3,1},{4,6},{5,7},{6,4},{7,5},{8,10},{9,11},{10,... | collective-permute-start | bytes 786440 | tf_op jit(solution)/shard_map/ppermute | solution.py:756
  155.6 13.4 %collective-permute-start.39 = (bf16[128,1024]{1,0:T(8,128)(2,1)S(1)}, bf16[128,1024]{1,0:T(8,128)(2,1)S(1)}, u32[]{:S(2)}, u32[]{:S(2)}) collective-permute-start(bf16[128,1024]{1,0:T(8,128)(2,1)S(1)} %get-tuple-element.232.refs_2_), channel_id=1, source_target_pairs={{0,1},{1,0},{2,3},{3,2},{4,5},{5,4},{6,7},{7,6},{8,9},{9,8},{10,11... | collective-permute-start | bytes 786440 | tf_op jit(solution)/shard_map/ppermute | solution.py:756
  167.0 2.0 collective-permute-start.42
  167.0 2.0 collective-permute-start.44
  167.5 1.8 collective-permute-start.46
  167.5 19.5 %collective-permute-start.50 = (bf16[512,512]{1,0:T(8,128)(2,1)S(1)}, bf16[512,512]{1,0:T(8,128)(2,1)S(1)}, u32[]{:S(2)}, u32[]{:S(2)}) collective-permute-start(bf16[512,512]{1,0:T(8,128)(2,1)S(1)} %get-tuple-element.257), channel_id=1, source_target_pairs={{0,16},{1,17},{2,18},{3,19},{4,20},{5,21},{6,22},{7,23},{8,24},{9,... | collective-permute-start | bytes 1572872 | tf_op jit(solution)/shard_map/ppermute | solution.py:790
  169.3 26.2 %collective-permute-start.51 = (bf16[512,512]{1,0:T(8,128)(2,1)S(1)}, bf16[512,512]{1,0:T(8,128)(2,1)S(1)}, u32[]{:S(2)}, u32[]{:S(2)}) collective-permute-start(bf16[512,512]{1,0:T(8,128)(2,1)S(1)} %fold.3), channel_id=1, source_target_pairs={{0,8},{1,9},{2,10},{3,11},{4,12},{5,13},{6,14},{7,15},{8,0},{9,1},... | collective-permute-start | bytes 1572872 | tf_op jit(solution)/shard_map/ppermute | solution.py:790
  169.9 17.1 %collective-permute-start.47 = (bf16[128,1024]{1,0:T(8,128)(2,1)S(1)}, bf16[128,1024]{1,0:T(8,128)(2,1)S(1)}, u32[]{:S(2)}, u32[]{:S(2)}) collective-permute-start(bf16[128,1024]{1,0:T(8,128)(2,1)S(1)} %get-tuple-element.254), channel_id=1, source_target_pairs={{0,2},{1,3},{2,0},{3,1},{4,6},{5,7},{6,4},{7,5},{8,10},{9,11},{10,... | collective-permute-start | bytes 786440 | tf_op jit(solution)/shard_map/ppermute | solution.py:756
  171.3 16.5 %collective-permute-start.48 = (bf16[128,1024]{1,0:T(8,128)(2,1)S(1)}, bf16[128,1024]{1,0:T(8,128)(2,1)S(1)}, u32[]{:S(2)}, u32[]{:S(2)}) collective-permute-start(bf16[128,1024]{1,0:T(8,128)(2,1)S(1)} %get-tuple-element.255), channel_id=1, source_target_pairs={{0,4},{1,5},{2,6},{3,7},{4,0},{5,1},{6,2},{7,3},{8,12},{9,13},{10,... | collective-permute-start | bytes 786440 | tf_op jit(solution)/shard_map/ppermute | solution.py:756
  172.2 20.5 %collective-permute-start.49 = (bf16[128,1024]{1,0:T(8,128)(2,1)S(1)}, bf16[128,1024]{1,0:T(8,128)(2,1)S(1)}, u32[]{:S(2)}, u32[]{:S(2)}) collective-permute-start(bf16[128,1024]{1,0:T(8,128)(2,1)S(1)} %get-tuple-element.256), channel_id=1, source_target_pairs={{0,6},{1,7},{2,4},{3,5},{4,2},{5,3},{6,0},{7,1},{8,14},{9,15},{10,... | collective-permute-start | bytes 786440 | tf_op jit(solution)/shard_map/ppermute | solution.py:756
  195.5 7.7 %collective-permute-start.52 = (bf16[512,1024]{1,0:T(8,128)(2,1)S(1)}, bf16[512,1024]{1,0:T(8,128)(2,1)S(1)}, u32[]{:S(2)}, u32[]{:S(2)}) collective-permute-start(bf16[512,1024]{1,0:T(8,128)(2,1)S(1)} %get-tuple-element.259), channel_id=1, source_target_pairs={{0,1},{1,0},{2,3},{3,2},{4,5},{5,4},{6,7},{7,6},{8,9},{9,8},{10,11... | collective-permute-start | bytes 3145736 | tf_op jit(solution)/shard_map/ppermute | solution.py:756
  201.7 15.3 %collective-permute-start.53 = (bf16[16,40,384]{2,1,0:T(8,128)(2,1)S(1)}, bf16[16,40,384]{2,1,0:T(8,128)(2,1)S(1)}, u32[]{:S(2)}, u32[]{:S(2)}) collective-permute-start(bf16[16,40,384]{2,1,0:T(8,128)(2,1)S(1)} %get-tuple-element.264), channel_id=1, source_target_pairs={{0,16},{16,0},{1,17},{17,1},{2,18},{18,2},{3,19},{19,3},{4,20},{20... | collective-permute-start | bytes 1474568 | tf_op jit(solution)/shard_map/ppermute | solution.py:817
  206.9 10.2 %all-to-all-start.2 = ((bf16[8,32,512]{2,1,0:T(8,128)(2,1)}), bf16[8,32,512]{2,1,0:T(8,128)(2,1)S(1)}, u32[]{:S(2)}, u32[]{:S(2)}) async-start(bf16[8,32,512]{2,1,0:T(8,128)(2,1)} %get-tuple-element.262), calls=%async_computation.2 | async-start | bytes 524288 | tf_op jit(solution)/shard_map/all_to_all | solution.py:794
  212.9 11.6 %collective-permute-start.54 = (bf16[2,32,1024]{2,1,0:T(8,128)(2,1)S(1)}, bf16[2,32,1024]{2,1,0:T(8,128)(2,1)S(1)}, u32[]{:S(2)}, u32[]{:S(2)}) collective-permute-start(bf16[2,32,1024]{2,1,0:T(8,128)(2,1)S(1)} %get-tuple-element.270), channel_id=1, source_target_pairs={{0,16},{16,0},{1,17},{17,1},{2,18},{18,2},{3,19},{19,3},{4,20},{20... | collective-permute-start | bytes 393224 | tf_op jit(solution)/shard_map/ppermute | solution.py:817
  213.6 11.0 %collective-permute-start.55 = (bf16[128,1024]{1,0:T(8,128)(2,1)S(1)}, bf16[128,1024]{1,0:T(8,128)(2,1)}, u32[]{:S(2)}, u32[]{:S(2)}) collective-permute-start(bf16[128,1024]{1,0:T(8,128)(2,1)S(1)} %get-tuple-element.271), channel_id=1, source_target_pairs={{0,2},{1,3},{2,0},{3,1},{4,6},{5,7},{6,4},{7,5},{8,10},{9,11},{10,... | collective-permute-start | bytes 786440 | tf_op jit(solution)/shard_map/ppermute | solution.py:756
  215.5 9.3 %collective-permute-start.56 = (bf16[128,1024]{1,0:T(8,128)(2,1)S(1)}, bf16[128,1024]{1,0:T(8,128)(2,1)}, u32[]{:S(2)}, u32[]{:S(2)}) collective-permute-start(bf16[128,1024]{1,0:T(8,128)(2,1)S(1)} %get-tuple-element.272), channel_id=1, source_target_pairs={{0,4},{1,5},{2,6},{3,7},{4,0},{5,1},{6,2},{7,3},{8,12},{9,13},{10,... | collective-permute-start | bytes 786440 | tf_op jit(solution)/shard_map/ppermute | solution.py:756
  217.0 12.4 %collective-permute-start.57 = (bf16[128,1024]{1,0:T(8,128)(2,1)S(1)}, bf16[128,1024]{1,0:T(8,128)(2,1)}, u32[]{:S(2)}, u32[]{:S(2)}) collective-permute-start(bf16[128,1024]{1,0:T(8,128)(2,1)S(1)} %get-tuple-element.273), channel_id=1, source_target_pairs={{0,6},{1,7},{2,4},{3,5},{4,2},{5,3},{6,0},{7,1},{8,14},{9,15},{10,... | collective-permute-start | bytes 786440 | tf_op jit(solution)/shard_map/ppermute | solution.py:756
  219.0 34.6 %all-to-all-start.3 = ((bf16[16,40,384]{2,1,0:T(8,128)(2,1)}), bf16[16,40,384]{2,1,0:T(8,128)(2,1)S(1)}, u32[]{:S(2)}, u32[]{:S(2)}) async-start(bf16[16,40,384]{2,1,0:T(8,128)(2,1)} %fold.4), calls=%async_computation.3 | async-start | bytes 983040 | tf_op jit(solution)/shard_map/all_to_all | solution.py:1096
  231.9 18.8 %collective-permute-start.58 = (bf16[96,1024]{1,0:T(8,128)(2,1)S(1)}, bf16[96,1024]{1,0:T(8,128)(2,1)S(1)}, u32[]{:S(2)}, u32[]{:S(2)}) collective-permute-start(bf16[96,1024]{1,0:T(8,128)(2,1)S(1)} %get-tuple-element.276), channel_id=1, source_target_pairs={{0,8},{1,9},{2,10},{3,11},{4,12},{5,13},{6,14},{7,15},{8,0},{9,1},... | collective-permute-start | bytes 589832 | tf_op jit(solution)/shard_map/ppermute | solution.py:756
  237.3 16.3 %collective-permute-start.60 = (bf16[64,1024]{1,0:T(8,128)(2,1)S(1)}, bf16[64,1024]{1,0:T(8,128)(2,1)S(1)}, u32[]{:S(2)}, u32[]{:S(2)}) collective-permute-start(bf16[64,1024]{1,0:T(8,128)(2,1)S(1)} %get-tuple-element.280), channel_id=1, source_target_pairs={{0,8},{1,9},{2,10},{3,11},{4,12},{5,13},{6,14},{7,15},{8,0},{9,1},... | collective-permute-start | bytes 393224 | tf_op jit(solution)/shard_map/ppermute | solution.py:756
  250.8 2.8 %collective-permute-start.59 = (bf16[32,1024]{1,0:T(8,128)(2,1)S(1)}, bf16[32,1024]{1,0:T(8,128)(2,1)S(1)}, u32[]{:S(2)}, u32[]{:S(2)}) collective-permute-start(bf16[32,1024]{1,0:T(8,128)(2,1)S(1)} %fusion), channel_id=1, source_target_pairs={{0,0},{8,1},{16,2},{24,3},{1,4},{9,5},{17,6},{25,7},{2,8},{10,9},{... | collective-permute-start | bytes 196616 | tf_op jit(solution)/shard_map/ppermute | solution.py:1125
  (13 other events, 87.4 us)
